TPU v7x, 512 devices: a whole 4x4x16 slice. The times are simulated.
512 devices in a mesh: dp: 32 (over z, core), tensor: 16 (over y, x).
Axes of the slice: x: 4, y: 4, z: 16, core: 2. Of those that a mesh axis runs over, the one named last changes fastest.
Arguments:
- features: bfloat16 [40960, 2048], P(('dp', 'tensor')), may hold values from -6 to 6
- w_hidden: bfloat16 [2048, 2048], P(None, 'tensor'), may hold values from -0.125 to 0.125
- w_embed: bfloat16 [2048, 768], P('tensor'), may hold values from -0.125 to 0.125
- members: bfloat16 [32, 2048, 768], P('dp', 'tensor'), may hold values from -6 to 6
- doc_owner: int32 [40960, 1], P('dp'), may hold values from 0 to 31; in each aligned block of 80 rows (0 to 79, 80 to 159, ...) at most 5 rows name the same one
- doc_local: int32 [40960], P('dp'), may hold values from 0 to 15
- member_cluster: int32 [32, 2048], P('dp', 'tensor'), may hold values from 0 to 15, never falling along the last dimension, each value on 1 to 192 neighbouring positions
- member_valid: int32 [32, 2048], P('dp', 'tensor'), may hold values 0 or 1
Outputs:
- best: float32 [40960], P(('dp', 'tensor'))
Inputs may be any that keep to these rules, and one draw needn't show every extreme that they name: Among the 80 documents of one device (aligned blocks of doc_owner's rows, in the order of dp then tensor) no owner is named more than 5 times; some owner is named exactly 5 times. `member_cluster`: along each owner's row the clusters never fall; every cluster has 1 to 192 slots.
All inputs are finite; a program needn't handle non-finite values. No bound on the sum of `member_valid` on one device may be relied on, other than what follows from the above.
Results may differ from a plain program's by a relative error of at most 0.013.
Values may be sent and summed in bfloat16 or wider, within the bound.
No kernel may reach another device: no remote copies, remote signals or barrier semaphores. Data moves between devices by JAX's collectives and lax.ppermute only.
A program may use at most 64 MiB of HBM per device.

v0:
```python
import jax
import jax.numpy as jnp
from jax import lax
from jax.sharding import PartitionSpec as P

epsilon = 1e-06


def unit_rows(vectors):
    values = vectors.astype(jnp.float32)
    return (values / jnp.sqrt(jnp.sum(values * values, axis=-1, keepdims=True) + epsilon)).astype(
        jnp.bfloat16
    )


def slot_of(owner, owners_count, slot_cap):
    onehot = (owner[:, None] == jnp.arange(owners_count, dtype=jnp.int32)[None, :]).astype(
        jnp.int32
    )
    ranking = jnp.sum((jnp.cumsum(onehot, axis=0) - 1) * onehot, axis=1)
    return owner * slot_cap + ranking


def pack_rows(query, local, slot_index, slot_total):
    placing = slot_index[None, :] == jnp.arange(slot_total, dtype=jnp.int32)[:, None]
    outgoing = jnp.dot(
        placing.astype(jnp.bfloat16), query, preferred_element_type=jnp.float32
    ).astype(jnp.bfloat16)
    slot_tag = jnp.sum(jnp.where(placing, local[None, :] + 1, 0), axis=1)
    return (outgoing, slot_tag)


def best_scores(arrived, arrived_tag, unit, cluster_here, valid_here):
    scores = lax.dot_general(
        arrived, unit, (((1,), (1,)), ((), ())), preferred_element_type=jnp.float32
    )
    allowed = (valid_here[None, :] == 1) & (cluster_here[None, :] == arrived_tag[:, None] - 1)
    return jnp.max(jnp.where(allowed, scores, -1.0), axis=1)


def body(features, w_hidden, w_embed, members, doc_owner, doc_local, member_cluster, member_valid):
    owners_count = lax.axis_size("dp")
    tensor_index = lax.axis_index("tensor")
    row_total = features.shape[0]
    slot_cap = min(row_total, max(2, 2 * row_total // owners_count))
    hidden = jax.nn.gelu(
        jnp.dot(
            lax.all_gather(features, "tensor", axis=0, tiled=True),
            w_hidden,
            preferred_element_type=jnp.float32,
        )
    ).astype(jnp.bfloat16)
    unit = unit_rows(members.reshape(members.shape[1], members.shape[2]))
    cluster_here = member_cluster.reshape(-1)
    valid_here = member_valid.reshape(-1)
    owner_all = doc_owner[:, 0]
    summed = lax.psum_scatter(
        jnp.dot(hidden, w_embed, preferred_element_type=jnp.float32).astype(jnp.bfloat16),
        "tensor",
        scatter_dimension=0,
        tiled=True,
    ).astype(jnp.float32)
    query = unit_rows(summed)
    owner = lax.dynamic_slice_in_dim(owner_all, tensor_index * row_total, row_total, 0)
    local = lax.dynamic_slice_in_dim(doc_local, tensor_index * row_total, row_total, 0)
    slot_total = owners_count * slot_cap
    slot_index = slot_of(owner, owners_count, slot_cap)
    outgoing, slot_tag = pack_rows(query, local, slot_index, slot_total)
    arrived, arrived_tag = (
        lax.all_to_all(outgoing, "dp", split_axis=0, concat_axis=0, tiled=True),
        lax.all_to_all(slot_tag, "dp", split_axis=0, concat_axis=0, tiled=True),
    )
    shared, shared_tag = (
        lax.all_gather(arrived, "tensor", axis=0, tiled=True),
        lax.all_gather(arrived_tag, "tensor", axis=0, tiled=True),
    )
    partial_value = best_scores(shared, shared_tag, unit, cluster_here, valid_here)
    merged = lax.pmax(partial_value, "tensor")
    own_best = lax.dynamic_slice_in_dim(merged, tensor_index * slot_total, slot_total, 0)
    answers = lax.all_to_all(own_best, "dp", split_axis=0, concat_axis=0, tiled=True)
    return jnp.take(answers, slot_index, axis=0)


def solution(mesh):
    return jax.shard_map(
        body,
        mesh=mesh,
        in_specs=(
            P(("dp", "tensor"), None),
            P(None, "tensor"),
            P("tensor", None),
            P("dp", "tensor", None),
            P("dp", None),
            P("dp"),
            P("dp", "tensor"),
            P("dp", "tensor"),
        ),
        out_specs=P(("dp", "tensor")),
        check_vma=False,
    )
```

profile of v0, /device:TPU:1, one launch (start us, length us, event | category | flops | bytes accessed | tf_op | source)
XLA Modules:
  0.0 418.8 jit_solution(9117724124348048883)
XLA Ops:
  6.5 0.0 copy-start
  6.5 0.0 all-gather.3.cloned.1.call-start
  6.5 0.7 all-gather.3.cloned.1.call-update
  7.3 0.0 reduce-scatter.2.cloned.1.call-start
  7.3 80.1 %all-gather.3.cloned.1.call-done = bf16[1280,2048]{1,0:T(8,128)(2,1)} async-done(((bf16[80,2048]{1,0:T(8,128)(2,1)}), bf16[1280,2048]{1,0:T(8,128)(2,1)}) %all-gather.3.cloned.1.call-update) | async-done | bytes 5242896 | tf_op jit(solution)/shard_map/all_gather | solution.py:48
  87.4 0.0 copy-done
  87.4 6.7 %convolution_convert_fusion = bf16[1280,768]{1,0:T(8,128)(2,1)} fusion(bf16[128,768]{1,0:T(8,128)(2,1)} %param.10, bf16[1280,2048]{1,0:T(8,128)(2,1)} %all-gather.3.cloned.1.call-done, bf16[2048,128]{1,0:T(8,128)(2,1)S(1)} %copy-done), kind=kOutput, calls=%fused_computation.2 | convolution fusion | flops 925204480 | bytes 7929856 | tf_op jit(solution)/shard_map/dot_general | solution.py:58
  94.1 0.0 reduce-scatter.2.cloned.1.call-update
  94.1 0.0 all-gather.5.cloned.1.call-start
  94.2 0.8 fusion.25
  94.9 0.1 fusion.24
  95.0 0.1 reduce_window_sum.11
  95.1 0.2 select_reduce_fusion.1
  95.3 0.8 multiply_add_fusion
  96.1 85.9 %reduce-scatter.2.cloned.1.call-done = bf16[80,768]{1,0:T(8,128)(2,1)} async-done(((bf16[1280,768]{1,0:T(8,128)(2,1)}), bf16[80,768]{1,0:T(8,128)(2,1)}) %reduce-scatter.2.cloned.1.call-update) | async-done | bytes 122896 | tf_op jit(solution)/shard_map/reduce_scatter | solution.py:57
  182.0 1.0 fusion.16
  183.0 1.2 convolution_convert_fusion.1
  184.2 0.1 all_to_all.27
  184.3 42.5 %all_to_all.36 = bf16[32,5,768]{2,1,0:T(8,128)(2,1)S(1)} all-to-all(bf16[32,5,768]{2,1,0:T(8,128)(2,1)S(1)} %all_to_all.27), channel_id=1, replica_groups=mesh['dp'=32,'tensor'=16] {'dp'}, dimensions={0} | all-to-all | bytes 491520 | tf_op jit(solution)/shard_map/all_to_all | solution.py:70
  226.8 0.8 all_to_all.29
  227.6 0.0 all-gather.5.cloned.1.call-update
  227.6 0.8 dynamic-slice_add_fusion
  228.4 0.1 select_reduce_fusion
  228.5 0.7 all_to_all.24
  229.3 3.9 all-to-all-start
  233.2 0.0 copy-done.1
  233.2 0.1 fusion.9
  233.3 0.8 compare_select_fusion
  234.1 0.0 copy-done.2
  234.1 1.3 dynamic-slice.1
  236.0 9.0 %all-to-all-done = s32[32,5,1]{1,2,0:T(1,128)S(1)} async-done(((s32[32,5,1]{1,2,0:T(1,128)}), s32[32,5,1]{1,2,0:T(1,128)S(1)}, u32[]{:S(2)}, u32[]{:S(2)}) %all-to-all-start) | async-done | bytes 672 | tf_op jit(solution)/shard_map/all_to_all | solution.py:71
  245.0 0.5 broadcast.54
  245.5 0.7 reduce.6
  246.2 0.1 reshape.50
  246.3 0.3 dynamic-update-slice
  246.6 58.3 %all-reduce = s32[2560]{0:T(1024)S(1)} all-reduce(s32[2560]{0:T(1024)S(1)} %dynamic-update-slice), channel_id=1, replica_groups=mesh['dp'=32,'tensor'=16] {'tensor'}, use_global_device_ids=true, to_apply=%add | all-reduce | flops 2560 | bytes 20480
  304.9 0.0 copy-done.3
  304.9 3.5 fusion
  308.5 55.9 %pmax.7 = f32[2560]{0:T(1024)S(1)} all-reduce(f32[2560]{0:T(1024)S(1)} %fusion), channel_id=1, replica_groups=mesh['dp'=32,'tensor'=16] {'tensor'}, use_global_device_ids=true, to_apply=%region_7.8 | all-reduce | flops 2560 | bytes 20480 | tf_op jit(solution)/shard_map/pmax | solution.py:78
  364.4 0.1 dynamic_slice.11
  364.5 0.7 all_to_all.30
  365.2 32.1 %all-to-all-start.2 = ((f32[32,5,1]{1,2,0:T(1,128)}), f32[32,5,1]{1,2,0:T(1,128)S(1)}, u32[]{:S(2)}, u32[]{:S(2)}) async-start(f32[32,5,1]{1,2,0:T(1,128)} %bitcast.9), calls=%async_computation.3 | async-start | bytes 32768 | tf_op jit(solution)/shard_map/all_to_all | solution.py:80
  397.3 11.9 %all-to-all-done.2 = f32[32,5,1]{1,2,0:T(1,128)S(1)} async-done(((f32[32,5,1]{1,2,0:T(1,128)}), f32[32,5,1]{1,2,0:T(1,128)S(1)}, u32[]{:S(2)}, u32[]{:S(2)}) %all-to-all-start.2) | async-done | bytes 672 | tf_op jit(solution)/shard_map/all_to_all | solution.py:80
  409.2 0.5 broadcast.55
  409.7 0.7 reduce.7
  410.4 0.1 all_to_all.32
  410.5 1.3 gather_fusion
  411.7 0.5 bitcast_select_fusion
  (10 shorter events, 0.0 us)
Async XLA Ops:
  6.5 80.9 %copy-start = (bf16[2048,128]{1,0:T(8,128)(2,1)S(1)}, bf16[2048,128]{1,0:T(8,128)(2,1)}, u32[]{:S(2)}) copy-start(bf16[2048,128]{1,0:T(8,128)(2,1)} %param.9) | copy-start | bytes 1572868
  6.5 80.9 %all-gather.3.cloned.1.call-start = ((), (), s32[]{:S(2)}) async-start(), calls=%async_computation.4 | async-start | bytes 5570560 | tf_op jit(solution)/shard_map/all_gather | solution.py:48
  7.3 174.7 %reduce-scatter.2.cloned.1.call-start = ((), (), s32[]{:S(2)}) async-start(), calls=%async_computation.5 | async-start | bytes 2088960 | tf_op jit(solution)/shard_map/reduce_scatter | solution.py:57
  94.1 139.1 %copy-start.1 = (bf16[1,128,768]{2,1,0:T(8,128)(2,1)S(1)}, bf16[1,128,768]{2,1,0:T(8,128)(2,1)}, u32[]{:S(2)}) copy-start(bf16[1,128,768]{2,1,0:T(8,128)(2,1)} %param.11) | copy-start | bytes 589828
  94.1 140.0 %copy-start.2 = (s32[1,128]{1,0:T(1,128)S(1)}, s32[1,128]{1,0:T(1,128)}, u32[]{:S(2)}) copy-start(s32[1,128]{1,0:T(1,128)} %param.15) | copy-start | bytes 1540
  94.1 210.9 %copy-start.3 = (s32[1,128]{1,0:T(1,128)S(1)}, s32[1,128]{1,0:T(1,128)}, u32[]{:S(2)}) copy-start(s32[1,128]{1,0:T(1,128)} %param.14) | copy-start | bytes 1540
  94.1 210.8 %all-gather.5.cloned.1.call-start = ((), (), s32[]{:S(2)}) async-start(), calls=%async_computation.6 | async-start | bytes 4177920 | tf_op jit(solution)/shard_map/all_gather | solution.py:74
  229.3 15.8 %all-to-all-start = ((s32[32,5,1]{1,2,0:T(1,128)}), s32[32,5,1]{1,2,0:T(1,128)S(1)}, u32[]{:S(2)}, u32[]{:S(2)}) async-start(s32[32,5,1]{1,2,0:T(1,128)} %bitcast.5), calls=%async_computation | async-start | bytes 32768 | tf_op jit(solution)/shard_map/all_to_all | solution.py:71
  365.2 44.0 %all-to-all-start.2 = ((f32[32,5,1]{1,2,0:T(1,128)}), f32[32,5,1]{1,2,0:T(1,128)S(1)}, u32[]{:S(2)}, u32[]{:S(2)}) async-start(f32[32,5,1]{1,2,0:T(1,128)} %bitcast.9), calls=%async_computation.3 | async-start | bytes 32768 | tf_op jit(solution)/shard_map/all_to_all | solution.py:80
Sparse Core Ops, SparseCore 0:
  10.4 76.9 all-gather.2
  94.2 87.7 reduce-scatter.1
  227.8 55.1 all-gather.4
where the time goes:
time: 419 us
  waiting for transfers between devices  188 us (45%)
  blocking collectives  157 us (37%)
  starting transfers between devices  36.1 us (9%)
  between operations  13.9 us (3%)
  matrix products  11.4 us (3%)
  local copies, waits for them, and re-layouts  7.26 us (2%)
  other arithmetic  5.84 us (1%)
    reduce_scatter x1, waiting for transfers between devices, body(): lax.psum_scatter(jnp.dot(hidden, w_embed, preferred_element_type=jnp.floa...  85.9 us
    all_gather x1, waiting for transfers between devices, body(): lax.all_gather(features, 'tensor', axis=0, tiled=True)  80.1 us
    unnamed x1, blocking collectives  58.3 us
    pmax x1, blocking collectives, body(): merged = lax.pmax(partial_value, 'tensor')  55.9 us
    all_to_all x1, blocking collectives, body(): lax.all_to_all(outgoing, 'dp', split_axis=0, concat_axis=0, tiled=True)  42.5 us
    all_to_all x1, starting transfers between devices, body(): lax.all_to_all(own_best, 'dp', split_axis=0, concat_axis=0, tiled=True)  32.1 us
    all_to_all x1, waiting for transfers between devices, body(): lax.all_to_all(own_best, 'dp', split_axis=0, concat_axis=0, tiled=True)  11.9 us
    all_to_all x1, waiting for transfers between devices, body(): lax.all_to_all(slot_tag, 'dp', split_axis=0, concat_axis=0, tiled=True)  8.98 us
  transfers between devices with their start and end apart: 5, of which 4 were waited for; matrix products, arithmetic and copies ran while one was open for 2% of the time, Pallas kernels for 0%

commit v1 on v0

v1 whole, which is shorter than its diff:
```python
import jax
import jax.numpy as jnp
import numpy as np
from jax import lax
from jax.experimental import pallas as pl
from jax.experimental.pallas import tpu as pltpu
from jax.sharding import Mesh, PartitionSpec as P

EPS = 1e-06
HID, EMB, ROWS, SLOTS, BLOCK, OWNERS, CAP = 2048, 768, 80, 128, 128, 32, 5
HALF = HID // 2
PACK = HALF + 3 * BLOCK
UNIT = SLOTS + 8
CHUNK = 256
LINES = 16
F32, BF16, I32 = jnp.float32, jnp.bfloat16, jnp.int32
PARAMS = pltpu.CompilerParams(vmem_limit_bytes=48 << 20)


def sds(shape, dtype):
    return jax.ShapeDtypeStruct(shape, dtype)


def iota(shape, dim):
    return lax.broadcasted_iota(I32, shape, dim)


def call(body, out, name, scalars=0):
    vm = pl.BlockSpec(memory_space=pltpu.VMEM)
    sm = pl.BlockSpec(memory_space=pltpu.SMEM)

    def run(*args):
        specs = [sm] * scalars + [vm] * (len(args) - scalars)
        outs = jax.tree.map(lambda _: vm, out)
        return pl.pallas_call(
            body, out_shape=out, in_specs=specs, out_specs=outs, name=name, compiler_params=PARAMS
        )(*args)

    return run


def unit_kernel(members, cluster, valid, out):
    values = members[0].astype(F32)
    norm = jnp.sum(values * values, axis=1, keepdims=True)
    out[0:SLOTS, :] = (values * (1.0 / jnp.sqrt(norm + EPS))).astype(BF16)
    tag = jnp.where(valid[...] == 1, cluster[...] + 1, 0).astype(F32)
    tag = jnp.concatenate([tag] * (EMB // SLOTS), axis=1)
    out[SLOTS:UNIT, :] = jnp.broadcast_to(tag, (8, EMB)).astype(BF16)


def weights_kernel(core, w_hidden, w_embed, out):
    c = core[0]
    upper = w_hidden[pl.ds(pl.multiple_of(c * HALF, HALF), HALF), :]
    for j in range(4):
        out[j, 0:HALF, :] = upper
    for i in range(3):
        piece = w_embed[:, pl.ds(pl.multiple_of(c * 3 * BLOCK + i * BLOCK, BLOCK), BLOCK)]
        for j in range(4):
            out[j, HALF + i * BLOCK : HALF + (i + 1) * BLOCK, :] = piece


def slots_kernel(owner_row, owner_col, local_col, place, tags, rank_row):
    row, col = owner_row[...], owner_col[...]
    same = row == col
    up, across = iota((ROWS, ROWS), 0), iota((ROWS, ROWS), 1)
    ranks = jnp.sum(jnp.where(same & (up < across), 1, 0), axis=0, keepdims=True)
    ranks_col = jnp.sum(jnp.where(same & (across < up), 1, 0), axis=1, keepdims=True)
    rank_row[...] = ranks
    line = iota((OWNERS * LINES, ROWS), 0)
    mine = row == line // LINES
    inner = line % LINES
    parts = [mine & (inner == k * CAP + ranks) for k in range(3)] + [mine & (inner == LINES - 1)]
    for k in range(4):
        place[k] = jnp.where(parts[k], 1.0, 0.0).astype(BF16)
    lane = iota((ROWS, CHUNK), 1)
    tags[...] = jnp.where(lane == ranks_col, local_col[...] + 1, 0).astype(F32).astype(BF16)


def head_kernel(features, weights, out):
    docs = features[...].reshape(4 * ROWS, HID)
    total = None
    for pair in range(2):
        a, b = 2 * pair, 2 * pair + 1
        pre = None
        for c in range(2):
            w = jnp.concatenate([weights[c, a, 0:HALF, :], weights[c, b, 0:HALF, :]], axis=1)
            part = jnp.dot(docs[:, c * HALF : (c + 1) * HALF], w, preferred_element_type=F32)
            pre = part if pre is None else pre + part
        hidden = jax.nn.gelu(pre).astype(BF16)
        rows = []
        for j in (a, b):
            rows.append(
                jnp.concatenate(
                    [
                        weights[c, j, HALF + i * BLOCK : HALF + (i + 1) * BLOCK, :]
                        for c in range(2)
                        for i in range(3)
                    ],
                    axis=1,
                )
            )
        part = jnp.dot(hidden, jnp.concatenate(rows, axis=0), preferred_element_type=F32)
        total = part if total is None else total + part
    out[...] = total.astype(BF16).reshape(4, ROWS, EMB)


def query_kernel(partial, place, tags, out):
    proj = partial[0].astype(F32)
    for j in range(1, 4):
        proj = proj + partial[j].astype(F32)
    norm = jnp.sum(proj * proj, axis=1, keepdims=True)
    query = (proj * (1.0 / jnp.sqrt(norm + EPS))).astype(BF16)
    total = jnp.dot(place[3], tags[...], preferred_element_type=F32)
    for k in range(3):
        total = total + jnp.dot(
            place[k], query[:, k * CHUNK : (k + 1) * CHUNK], preferred_element_type=F32
        )
    out[...] = total.astype(BF16).reshape(OWNERS, LINES, CHUNK)


def score_kernel(arrived, pick, unit, out):
    flat = arrived[...].reshape(OWNERS * LINES, CHUNK)
    moved = jnp.dot(pick[...], flat, preferred_element_type=F32)
    count = OWNERS * CAP
    query = jnp.concatenate(
        [moved[k * count : (k + 1) * count].astype(BF16) for k in range(3)], axis=1
    )
    slot = iota((count, CHUNK), 0) // OWNERS
    tag = jnp.sum(
        jnp.where(iota((count, CHUNK), 1) == slot, moved[3 * count :], 0.0), axis=1, keepdims=True
    )
    best = jnp.full((count, 2 * SLOTS), -1.0, F32)
    for j in range(0, 16, 2):
        blocks, marks = [], []
        for i in (j, j + 1):
            blocks.append(unit[i * UNIT : i * UNIT + SLOTS, :])
            marks.append(unit[i * UNIT + SLOTS : (i + 1) * UNIT, 0:SLOTS].astype(F32)[0:1])
        scores = lax.dot_general(
            query,
            jnp.concatenate(blocks, axis=0),
            (((1,), (1,)), ((), ())),
            preferred_element_type=F32,
        )
        allowed = jnp.concatenate(marks, axis=1) == tag
        best = jnp.maximum(best, jnp.where(allowed, scores, -1.0))
    best = jnp.max(best, axis=1, keepdims=True)
    lane = iota((OWNERS, SLOTS), 1)
    result = jnp.zeros((OWNERS, SLOTS), F32)
    for s in range(CAP):
        result = jnp.where(lane == s, best[s * OWNERS : (s + 1) * OWNERS], result)
    out[...] = result


def answer_kernel(answers, owner_row, rank_row, out):
    mine = owner_row[...] == iota((OWNERS, ROWS), 0)
    total = jnp.zeros((1, ROWS), F32)
    for s in range(CAP):
        value = jnp.sum(jnp.where(mine, answers[:, s : s + 1], 0.0), axis=0, keepdims=True)
        total = jnp.where(rank_row[...] == s, value, total)
    out[...] = total


def picking():
    count = OWNERS * CAP
    pick = np.zeros((4 * count, OWNERS * LINES), np.float32)
    for s in range(CAP):
        for o in range(OWNERS):
            for k in range(3):
                pick[k * count + s * OWNERS + o, o * LINES + k * CAP + s] = 1
            pick[3 * count + s * OWNERS + o, o * LINES + LINES - 1] = 1
    return jnp.asarray(pick, BF16)


def body(features, w_hidden, w_embed, members, doc_owner, doc_local, member_cluster, member_valid):
    dp = ("z", "core")
    unit = call(unit_kernel, sds((UNIT, EMB), BF16), "unit")(members, member_cluster, member_valid)
    units = lax.all_gather(unit, ("y", "x"), axis=0, tiled=True)

    core = lax.axis_index("core").astype(I32).reshape(1)
    half = call(weights_kernel, sds((4, PACK, BLOCK), BF16), "weights", 1)(core, w_hidden, w_embed)
    docs = lax.all_to_all(
        jnp.broadcast_to(features[None], (4, ROWS, HID)), "x", 0, 0, tiled=True
    )
    halves = lax.all_to_all(half, "y", 0, 0, tiled=True)
    weights = lax.all_to_all(
        jnp.broadcast_to(halves[None], (2, 4, PACK, BLOCK)), "core", 0, 0, tiled=True
    )

    first = lax.axis_index(("y", "x")) * ROWS
    owner = lax.dynamic_slice_in_dim(doc_owner[:, 0], first, ROWS, 0)
    local = lax.dynamic_slice_in_dim(doc_local, first, ROWS, 0)
    owner_row = owner.reshape(1, ROWS)
    place, tags, rank_row = call(
        slots_kernel,
        (
            sds((4, OWNERS * LINES, ROWS), BF16),
            sds((ROWS, CHUNK), BF16),
            sds((1, ROWS), I32),
        ),
        "slots",
    )(owner_row, owner.reshape(ROWS, 1), local.reshape(ROWS, 1))

    partial = call(head_kernel, sds((4, ROWS, EMB), BF16), "head")(docs, weights)
    partial = lax.all_to_all(partial, "x", 0, 0, tiled=True)
    outgoing = call(query_kernel, sds((OWNERS, LINES, CHUNK), BF16), "query")(partial, place, tags)
    arrived = lax.all_to_all(outgoing, dp, 0, 0, tiled=True)
    best = call(score_kernel, sds((OWNERS, SLOTS), F32), "score")(arrived, picking(), units)
    answers = lax.all_to_all(best, dp, 0, 0, tiled=True)
    result = call(answer_kernel, sds((1, ROWS), F32), "answer")(answers, owner_row, rank_row)
    return result.reshape(ROWS)


def solution(mesh):
    grid = Mesh(mesh.devices.reshape(16, 2, 4, 4), ("z", "core", "y", "x"))
    dp, tensor = ("z", "core"), ("y", "x")
    every = dp + tensor
    return jax.shard_map(
        body,
        mesh=grid,
        in_specs=(
            P(every, None),
            P(None, tensor),
            P(tensor, None),
            P(dp, tensor, None),
            P(dp, None),
            P(dp),
            P(dp, tensor),
            P(dp, tensor),
        ),
        out_specs=P(every),
        check_vma=False,
    )
```

time: 419 us -> 149 us (0.36)
  waiting for transfers between devices: 188 us -> 23.8 us
  blocking collectives: 157 us -> 87.5 us
  starting transfers between devices: 36.1 us -> 8.57 us
  matrix products: 11.4 us -> 0 us
  Pallas kernels: 0 us -> 6.3 us
  other arithmetic: 5.84 us -> 0 us
    reduce_scatter x1 -> x0, waiting for transfers between devices: 85.9 us -> none  [body(): lax.psum_scatter(jnp.dot(hidden, w_embed, preferred_element_type=jnp.floa...]
    all_gather x2 -> x1, waiting for transfers between devices: 80.1 us -> 0.01 us  [body(): units = lax.all_gather(unit, ('y', 'x'), axis=0, tiled=True)]
    unnamed x1 -> x0, blocking collectives: 58.3 us -> none
    pmax x1 -> x0, blocking collectives: 55.9 us -> none  [body(): merged = lax.pmax(partial_value, 'tensor')]
    all_to_all x1 -> x4, blocking collectives: 42.5 us -> 87.5 us  [the longest x1 35.3 us: body(): arrived = lax.all_to_all(outgoing, dp, 0, 0, tiled=True)]
    all_to_all x2, starting transfers between devices: 36 us -> 8.57 us  [the longest x1 4.97 us: body(): lax.all_to_all(jnp.broadcast_to(features[None], (4, ROWS, HID)), 'x', 0,...]
    dot_general x3 -> x0, matrix products: 11.4 us -> none  [the longest x1 6.66 us: body(): jnp.dot(hidden, w_embed, preferred_element_type=jnp.float32)]
    pallas_call x0 -> x7, Pallas kernels: none -> 6.3 us  [run(): pl.pallas_call(body, out_shape=out, in_specs=specs, out_specs=outs, name=...]
  transfers between devices with their start and end apart: 5 -> 3, of which waited for: 4 -> 2; matrix products, arithmetic and copies ran while one was open for 2% -> 3% of each run, Pallas kernels for 0% -> 2%
where the time goes in v1:
time: 149 us; the launch traced here: 148 us
  blocking collectives  87.5 us (59%)
  waiting for transfers between devices  23.8 us (16%)
  between operations  13.5 us (9%)
  local copies, waits for them, and re-layouts  8.58 us (6%)
  starting transfers between devices  8.57 us (6%)
  Pallas kernels  6.3 us (4%)
    all_to_all x1, blocking collectives, body(): arrived = lax.all_to_all(outgoing, dp, 0, 0, tiled=True)  35.3 us
    all_to_all x1, blocking collectives, body(): halves = lax.all_to_all(half, 'y', 0, 0, tiled=True)  29.3 us
    all_to_all x1, blocking collectives, body(): answers = lax.all_to_all(best, dp, 0, 0, tiled=True)  15.5 us
    all_to_all x1, waiting for transfers between devices, body(): partial = lax.all_to_all(partial, 'x', 0, 0, tiled=True)  11.9 us
    all_to_all x1, waiting for transfers between devices, body(): lax.all_to_all(jnp.broadcast_to(features[None], (4, ROWS, HID)), 'x', 0,...  11.9 us
    all_to_all x1, blocking collectives, body(): lax.all_to_all(jnp.broadcast_to(halves[None], (2, 4, PACK, BLOCK)), 'core...  7.49 us
    pallas_call x7, Pallas kernels, run(): pl.pallas_call(body, out_shape=out, in_specs=specs, out_specs=outs, name=...  6.3 us
    all_to_all x1, starting transfers between devices, body(): lax.all_to_all(jnp.broadcast_to(features[None], (4, ROWS, HID)), 'x', 0,...  4.97 us
  transfers between devices with their start and end apart: 3, of which 2 were waited for; matrix products, arithmetic and copies ran while one was open for 3% of the time, Pallas kernels for 2%

profile of v1, /device:TPU:1, one launch (start us, length us, event | category | flops | bytes accessed | tf_op | source)
XLA Modules:
  0.0 148.2 jit_solution(11599672463492646657)
XLA Ops:
  6.5 0.0 copy-start
  6.5 0.0 all-gather.2.cloned.1.call-start
  6.5 0.0 copy-start.5
  6.5 0.9 copy-done.5
  7.5 0.0 copy-start.6
  7.5 0.7 copy-done.6
  8.1 0.0 copy-start.7
  8.1 0.7 copy-done.7
  8.8 0.8 unit.1
  9.6 0.0 all-gather.2.cloned.1.call-update
  9.6 2.2 %broadcast_in_dim.4 = bf16[4,80,2048]{2,1,0:T(8,128)(2,1)} broadcast(bf16[80,2048]{1,0:T(8,128)(2,1)} %param.9), dimensions={1,2} | broadcast | bytes 1638400 | tf_op jit(solution)/shard_map/broadcast_in_dim | solution.py:182
  11.8 0.0 copy-start.3
  11.8 0.0 copy-start.4
  11.8 5.0 %all-to-all-start = ((bf16[4,80,2048]{2,1,0:T(8,128)(2,1)}), bf16[4,80,2048]{2,1,0:T(8,128)(2,1)S(1)}, u32[]{:S(2)}, u32[]{:S(2)}) async-start(bf16[4,80,2048]{2,1,0:T(8,128)(2,1)} %broadcast_in_dim.4), calls=%async_computation | async-start | bytes 2621440 | tf_op jit(solution)/shard_map/all_to_all | solution.py:181
  16.8 0.0 copy-done.3
  16.8 0.0 copy-done.4
  16.8 0.2 weights.1
  17.0 11.9 %all-to-all-done.features = bf16[4,80,2048]{2,1,0:T(8,128)(2,1)S(1)} async-done(((bf16[4,80,2048]{2,1,0:T(8,128)(2,1)}), bf16[4,80,2048]{2,1,0:T(8,128)(2,1)S(1)}, u32[]{:S(2)}, u32[]{:S(2)}) %all-to-all-start) | async-done | bytes 1310752 | tf_op jit(solution)/shard_map/all_to_all | solution.py:181
  28.9 29.3 %all_to_all.36 = bf16[4,1408,128]{2,1,0:T(8,128)(2,1)S(1)} all-to-all(bf16[4,1408,128]{2,1,0:T(8,128)(2,1)S(1)} %weights.1), channel_id=1, replica_groups=mesh['z'=16,'core'=2,'y'=4,'x'=4] {'y'}, dimensions={0} | all-to-all | bytes 2883584 | tf_op jit(solution)/shard_map/all_to_all | solution.py:184
  58.2 0.4 broadcast_in_dim.5
  58.6 7.5 %all_to_all.37.weights = bf16[2,4,1408,128]{3,2,1,0:T(8,128)(2,1)S(1)} all-to-all(bf16[2,4,1408,128]{3,2,1,0:T(8,128)(2,1)S(1)} %broadcast_in_dim.5), channel_id=1, replica_groups=mesh['z'=16,'core'=2,'y'=4,'x'=4] {'core'}, dimensions={0} | all-to-all | bytes 5767168 | tf_op jit(solution)/shard_map/all_to_all | solution.py:185
  66.1 2.1 %head.1 = bf16[4,80,768]{2,1,0:T(8,128)(2,1)} custom-call(bf16[4,80,2048]{2,1,0:T(8,128)(2,1)S(1)} %all-to-all-done.features, bf16[2,4,1408,128]{3,2,1,0:T(8,128)(2,1)S(1)} %all_to_all.37.weights), custom_call_target="tpu_custom_call" | custom-call | tf_op jit(solution)/shard_map/head/pallas_call | solution.py:35
  68.2 0.0 copy-start.2
  68.2 3.6 %all-to-all-start.3 = ((bf16[4,80,768]{2,1,0:T(8,128)(2,1)}), bf16[4,80,768]{2,1,0:T(8,128)(2,1)S(1)}, u32[]{:S(2)}, u32[]{:S(2)}) async-start(bf16[4,80,768]{2,1,0:T(8,128)(2,1)} %head.1), calls=%async_computation.3 | async-start | bytes 983040 | tf_op jit(solution)/shard_map/all_to_all | solution.py:204
  71.8 0.0 copy-done
  71.8 0.1 dynamic-slice_bitcast_fusion
  71.9 0.1 copy.15.local_col
  72.0 0.8 constant_dynamic-slice_fusion
  72.8 0.1 copy.17.owner_col
  72.9 0.8 fusion.owner_row
  73.6 0.4 slots.1
  74.1 11.9 %all-to-all-done.3.partial = bf16[4,80,768]{2,1,0:T(8,128)(2,1)S(1)} async-done(((bf16[4,80,768]{2,1,0:T(8,128)(2,1)}), bf16[4,80,768]{2,1,0:T(8,128)(2,1)S(1)}, u32[]{:S(2)}, u32[]{:S(2)}) %all-to-all-start.3) | async-done | bytes 491552 | tf_op jit(solution)/shard_map/all_to_all | solution.py:204
  86.0 0.6 query.1
  86.5 35.3 %all_to_all.38.arrived = bf16[32,16,256]{2,1,0:T(8,128)(2,1)S(1)} all-to-all(bf16[32,16,256]{2,1,0:T(8,128)(2,1)S(1)} %query.1), channel_id=1, replica_groups=mesh['z'=16,'core'=2,'y'=4,'x'=4] {'z','core'}, dimensions={0} | all-to-all | bytes 524288 | tf_op jit(solution)/shard_map/all_to_all | solution.py:206
  121.8 0.0 all-gather.2.cloned.1.call-done.unit
  121.8 0.0 copy-done.2
  121.8 0.0 copy-start.1
  121.8 1.9 %copy-done.1 = bf16[2176,768]{1,0:T(8,128)(2,1)S(1)} copy-done((bf16[2176,768]{1,0:T(8,128)(2,1)S(1)}, bf16[2176,768]{1,0:T(8,128)(2,1)}, u32[]{:S(2)}) %copy-start.1) | copy-done | bytes 3342360
  123.8 1.5 %score.1 = f32[32,128]{1,0:T(8,128)S(1)} custom-call(bf16[32,16,256]{2,1,0:T(8,128)(2,1)S(1)} %all_to_all.38.arrived, bf16[640,512]{1,0:T(8,128)(2,1)S(1)} %copy-done.2, bf16[2176,768]{1,0:T(8,128)(2,1)S(1)} %copy-done.1), custom_call_target="tpu_custom_call" | custom-call | tf_op jit(solution)/shard_map/score/pallas_call | solution.py:35
  125.3 15.5 %all_to_all.39 = f32[32,1,128]{2,1,0:T(1,128)S(1)} all-to-all(f32[32,1,128]{2,1,0:T(1,128)S(1)} %bitcast.11), channel_id=1, replica_groups=mesh['z'=16,'core'=2,'y'=4,'x'=4] {'z','core'}, dimensions={0} | all-to-all | bytes 32768 | tf_op jit(solution)/shard_map/all_to_all | solution.py:208
  140.8 0.6 answer.1
Async XLA Ops:
  6.5 65.3 %copy-start = (s32[1280]{0:T(1024)S(1)}, s32[1280]{0:T(1024)}, u32[]{:S(2)}) copy-start(s32[1280]{0:T(1024)} %param.14) | copy-start | bytes 15364
  6.5 115.3 %all-gather.2.cloned.1.call-start = ((), (), s32[]{:S(2)}) async-start(), calls=%async_computation.6 | async-start | bytes 3551232 | tf_op jit(solution)/shard_map/all_gather | solution.py:177
  6.5 0.9 copy-start.5
  7.5 0.7 copy-start.6
  8.1 0.7 copy-start.7
  11.8 5.0 %copy-start.3 = (bf16[2048,128]{1,0:T(8,128)(2,1)S(1)}, bf16[2048,128]{1,0:T(8,128)(2,1)}, u32[]{:S(2)}) copy-start(bf16[2048,128]{1,0:T(8,128)(2,1)} %w_hidden.1) | copy-start | bytes 1572868
  11.8 5.0 %copy-start.4 = (bf16[128,768]{1,0:T(8,128)(2,1)S(1)}, bf16[128,768]{1,0:T(8,128)(2,1)}, u32[]{:S(2)}) copy-start(bf16[128,768]{1,0:T(8,128)(2,1)} %w_embed.1) | copy-start | bytes 589828
  11.8 17.1 %all-to-all-start = ((bf16[4,80,2048]{2,1,0:T(8,128)(2,1)}), bf16[4,80,2048]{2,1,0:T(8,128)(2,1)S(1)}, u32[]{:S(2)}, u32[]{:S(2)}) async-start(bf16[4,80,2048]{2,1,0:T(8,128)(2,1)} %broadcast_in_dim.4), calls=%async_computation | async-start | bytes 2621440 | tf_op jit(solution)/shard_map/all_to_all | solution.py:181
  68.2 53.6 %copy-start.2 = (bf16[640,512]{1,0:T(8,128)(2,1)S(1)}, bf16[640,512]{1,0:T(8,128)(2,1)}, u32[]{:S(2)}) copy-start(bf16[640,512]{1,0:T(8,128)(2,1)} %constant.24.clone.pick) | copy-start | bytes 1966084
  68.2 17.8 %all-to-all-start.3 = ((bf16[4,80,768]{2,1,0:T(8,128)(2,1)}), bf16[4,80,768]{2,1,0:T(8,128)(2,1)S(1)}, u32[]{:S(2)}, u32[]{:S(2)}) async-start(bf16[4,80,768]{2,1,0:T(8,128)(2,1)} %head.1), calls=%async_computation.3 | async-start | bytes 983040 | tf_op jit(solution)/shard_map/all_to_all | solution.py:204
  121.8 1.9 %copy-start.1 = (bf16[2176,768]{1,0:T(8,128)(2,1)S(1)}, bf16[2176,768]{1,0:T(8,128)(2,1)}, u32[]{:S(2)}) copy-start(bf16[2176,768]{1,0:T(8,128)(2,1)} %all-gather.2.cloned.1.call-done.unit) | copy-start | bytes 10027012
Sparse Core Ops, SparseCore 0:
  10.4 75.0 all-gather.1

commit v2 on v1

v2 whole, which is shorter than its diff:
```python
import jax
import jax.numpy as jnp
import numpy as np
from jax import lax
from jax.experimental import pallas as pl
from jax.experimental.pallas import tpu as pltpu
from jax.sharding import Mesh, PartitionSpec as P

EPS = 1e-06
HID, EMB, ROWS, SLOTS, BLOCK, OWNERS, CAP = 2048, 768, 80, 128, 128, 32, 5
HALF = HID // 2
PACK = HALF + 3 * BLOCK
CHUNK = 256
LINES = 16
UNIT = SLOTS + 8
PARTS = 4
F32, BF16, I32 = jnp.float32, jnp.bfloat16, jnp.int32
PARAMS = pltpu.CompilerParams(vmem_limit_bytes=16 << 20)


def sds(shape, dtype):
    return jax.ShapeDtypeStruct(shape, dtype)


def iota(shape, dim):
    return lax.broadcasted_iota(I32, shape, dim)


def call(body, out, name):
    vm = pl.BlockSpec(memory_space=pltpu.VMEM)

    def run(*args):
        specs = [vm] * len(args)
        outs = jax.tree.map(lambda _: vm, out)
        return pl.pallas_call(
            body, out_shape=out, in_specs=specs, out_specs=outs, name=name, compiler_params=PARAMS
        )(*args)

    return run


def prepare_kernel(
    w_hidden, w_embed, members, cluster, valid, half, unit, held, slots, live, sem, sems
):
    c = lax.axis_index("core")
    first = [
        pltpu.make_async_copy(members.at[0], held, sem.at[0]),
        pltpu.make_async_copy(cluster, slots, sem.at[1]),
        pltpu.make_async_copy(valid, live, sem.at[2]),
    ]
    rest = []
    for j in range(4):
        rest.append(
            pltpu.make_async_copy(
                w_hidden.at[pl.ds(pl.multiple_of(c * HALF, HALF), HALF), :],
                half.at[j, 0:HALF, :],
                sems.at[j, 3],
            )
        )
        for i in range(3):
            rest.append(
                pltpu.make_async_copy(
                    w_embed.at[:, pl.ds(pl.multiple_of((3 * c + i) * BLOCK, BLOCK), BLOCK)],
                    half.at[j, HALF + i * BLOCK : HALF + (i + 1) * BLOCK, :],
                    sems.at[j, i],
                )
            )
    for copy in first + rest:
        copy.start()
    for copy in first:
        copy.wait()
    values = held[...].astype(F32)
    norm = jnp.sum(values * values, axis=1, keepdims=True)
    unit[0:SLOTS, :] = (values * (1.0 / jnp.sqrt(norm + EPS))).astype(BF16)
    tag = jnp.where(live[...] == 1, slots[...] + 1, 0).astype(F32)
    tag = jnp.concatenate([tag] * (EMB // SLOTS), axis=1)
    unit[SLOTS:UNIT, :] = jnp.broadcast_to(tag, (8, EMB)).astype(BF16)
    for copy in rest:
        copy.wait()


def slots_kernel(owner_row, owner_col, local_col, mark, place, tags, rank_row):
    row, col = owner_row[...], owner_col[...]
    same = row == col
    up, across = iota((ROWS, ROWS), 0), iota((ROWS, ROWS), 1)
    ranks = jnp.sum(jnp.where(same & (up < across), 1, 0), axis=0, keepdims=True)
    ranks_col = jnp.sum(jnp.where(same & (across < up), 1, 0), axis=1, keepdims=True)
    rank_row[...] = ranks
    line = iota((OWNERS * LINES, ROWS), 0)
    mine = row == line // LINES
    inner = line % LINES
    parts = [mine & (inner == k * CAP + ranks) for k in range(3)] + [mine & (inner == LINES - 1)]
    for k in range(4):
        place[k] = jnp.where(parts[k], 1.0, 0.0).astype(BF16)
    lane = iota((ROWS, CHUNK), 1)
    tags[...] = jnp.where(lane == ranks_col, local_col[...] + 1, 0).astype(F32).astype(BF16)


def head_kernel(
    own, left, right, far, mine, other, own_out, left_out, right_out, far_out, docs, kept, sem
):
    c = lax.axis_index("core")
    copies = [
        pltpu.make_async_copy(part, docs.at[i * ROWS : (i + 1) * ROWS, :], sem.at[i + 1])
        for i, part in enumerate((own, left, right, far))
    ]
    for copy in copies:
        copy.start()
    for copy in copies:
        copy.wait()
    pre, embeds = None, []
    for half, weights in ((c, mine), (1 - c, other)):
        lines = docs[:, pl.ds(pl.multiple_of(half * HALF, HALF), HALF)]
        w = jnp.concatenate([weights[j, 0:HALF, :] for j in range(4)], axis=1)
        part = jnp.dot(lines, w, preferred_element_type=F32)
        pre = part if pre is None else pre + part
        rows = []
        for j in range(4):
            cut = [HALF + i * BLOCK for i in range(3)]
            rows.append(jnp.concatenate([weights[j, r : r + BLOCK, :] for r in cut], axis=1))
        embeds.append(jnp.concatenate(rows, axis=0))
    hidden = jax.nn.gelu(pre).astype(BF16)
    for k, embed in enumerate(embeds):
        total = jnp.dot(hidden, embed, preferred_element_type=F32)
        cut = slice(k * 3 * BLOCK, (k + 1) * 3 * BLOCK)
        kept[:, cut] = total[0:ROWS]
        for j, out in enumerate((left_out, right_out, far_out)):
            out[:, cut] = total[(j + 1) * ROWS : (j + 2) * ROWS].astype(BF16)
    copy = pltpu.make_async_copy(kept, own_out, sem.at[0])
    copy.start()
    copy.wait()


def query_kernel(own, left, right, far, place, tags, out, kept, sem):
    copy = pltpu.make_async_copy(own, kept, sem.at[0])
    copy.start()
    proj = left[...].astype(F32) + right[...].astype(F32) + far[...].astype(F32)
    copy.wait()
    proj = proj + kept[...]
    norm = jnp.sum(proj * proj, axis=1, keepdims=True)
    query = proj * (1.0 / jnp.sqrt(norm + EPS))
    low, high = query[:, 0 : EMB // 2], query[:, EMB // 2 :]
    straight = lax.axis_index("core") == 0
    query = jnp.concatenate(
        [jnp.where(straight, low, high), jnp.where(straight, high, low)], axis=1
    ).astype(BF16)
    total = jnp.dot(place[3], tags[...], preferred_element_type=F32)
    for k in range(3):
        total = total + jnp.dot(
            place[k], query[:, k * CHUNK : (k + 1) * CHUNK], preferred_element_type=F32
        )
    out[...] = total.astype(BF16).reshape(OWNERS, LINES, CHUNK)


def score_kernel(arrived, pick, units, out, held, sem):
    rows = 16 * UNIT // PARTS
    copies = [
        pltpu.make_async_copy(
            units.at[i * rows : (i + 1) * rows, :], held.at[i * rows : (i + 1) * rows, :], sem.at[i]
        )
        for i in range(PARTS)
    ]
    for copy in copies:
        copy.start()
    flat = arrived[...].reshape(OWNERS * LINES, CHUNK)
    moved = jnp.dot(pick[...], flat, preferred_element_type=F32)
    count = OWNERS * CAP
    query = jnp.concatenate(
        [moved[k * count : (k + 1) * count].astype(BF16) for k in range(3)], axis=1
    )
    slot = iota((count, CHUNK), 0) // OWNERS
    tag = jnp.sum(
        jnp.where(iota((count, CHUNK), 1) == slot, moved[3 * count :], 0.0), axis=1, keepdims=True
    )
    best = jnp.full((count, 2 * SLOTS), -1.0, F32)
    for j in range(0, 16, 2):
        if j % (16 // PARTS) == 0:
            copies[j // (16 // PARTS)].wait()
        blocks, marks = [], []
        for i in (j, j + 1):
            blocks.append(held[i * UNIT : i * UNIT + SLOTS, :])
            marks.append(held[i * UNIT + SLOTS : (i + 1) * UNIT, 0:SLOTS].astype(F32)[0:1])
        scores = lax.dot_general(
            query,
            jnp.concatenate(blocks, axis=0),
            (((1,), (1,)), ((), ())),
            preferred_element_type=F32,
        )
        allowed = jnp.concatenate(marks, axis=1) == tag
        best = jnp.maximum(best, jnp.where(allowed, scores, -1.0))
    best = jnp.max(best, axis=1, keepdims=True)
    lane = iota((OWNERS, SLOTS), 1)
    result = jnp.zeros((OWNERS, SLOTS), F32)
    for s in range(CAP):
        result = jnp.where(lane == s, best[s * OWNERS : (s + 1) * OWNERS], result)
    out[...] = result


def answer_kernel(answers, owner_row, rank_row, out):
    mine = owner_row[...] == iota((OWNERS, ROWS), 0)
    total = jnp.zeros((1, ROWS), F32)
    for s in range(CAP):
        value = jnp.sum(jnp.where(mine, answers[:, s : s + 1], 0.0), axis=0, keepdims=True)
        total = jnp.where(rank_row[...] == s, value, total)
    out[...] = total


def picking():
    count = OWNERS * CAP
    pick = np.zeros((4 * count, OWNERS * LINES), np.float32)
    for s in range(CAP):
        for o in range(OWNERS):
            for k in range(3):
                pick[k * count + s * OWNERS + o, o * LINES + k * CAP + s] = 1
            pick[3 * count + s * OWNERS + o, o * LINES + LINES - 1] = 1
    return jnp.asarray(pick, BF16)


def shift(value, axis, step):
    return lax.ppermute(value, axis, [(i, (i + step) % 4) for i in range(4)])


HBM = pl.BlockSpec(memory_space=pltpu.HBM)
VMEM = pl.BlockSpec(memory_space=pltpu.VMEM)


def prepared(*arrays):
    return pl.pallas_call(
        prepare_kernel,
        out_shape=(sds((4, PACK, BLOCK), BF16), sds((UNIT, EMB), BF16)),
        in_specs=[HBM] * 5,
        out_specs=(VMEM, VMEM),
        scratch_shapes=[
            pltpu.VMEM((SLOTS, EMB), BF16),
            pltpu.VMEM((1, SLOTS), I32),
            pltpu.VMEM((1, SLOTS), I32),
            pltpu.SemaphoreType.DMA((3,)),
            pltpu.SemaphoreType.DMA((4, 4)),
        ],
        name="prepare",
        compiler_params=PARAMS,
    )(*arrays)


KEPT = [pltpu.VMEM((ROWS, EMB), F32), pltpu.SemaphoreType.DMA((1,))]


def head(*arrays):
    piece = sds((ROWS, EMB), BF16)
    return pl.pallas_call(
        head_kernel,
        out_shape=(pltpu.HBM((ROWS, EMB), F32), piece, piece, piece),
        in_specs=[HBM] * 4 + [VMEM] * 2,
        out_specs=(HBM, VMEM, VMEM, VMEM),
        scratch_shapes=[
            pltpu.VMEM((4 * ROWS, HID), BF16),
            pltpu.VMEM((ROWS, EMB), F32),
            pltpu.SemaphoreType.DMA((5,)),
        ],
        name="head",
        compiler_params=PARAMS,
    )(*arrays)


def query(*arrays):
    return pl.pallas_call(
        query_kernel,
        out_shape=sds((OWNERS, LINES, CHUNK), BF16),
        in_specs=[HBM] + [VMEM] * 5,
        out_specs=VMEM,
        scratch_shapes=KEPT,
        name="query",
        compiler_params=PARAMS,
    )(*arrays)


def score(arrived, pick, units):
    return pl.pallas_call(
        score_kernel,
        out_shape=sds((OWNERS, SLOTS), F32),
        in_specs=[VMEM, VMEM, HBM],
        out_specs=VMEM,
        scratch_shapes=[pltpu.VMEM((16 * UNIT, EMB), BF16), pltpu.SemaphoreType.DMA((PARTS,))],
        name="score",
        compiler_params=PARAMS,
    )(arrived, pick, units)


def stay(value):
    return pltpu.with_memory_space_constraint(value, pltpu.HBM)


def swap(value):
    return lax.ppermute(value, "core", [(0, 1), (1, 0)])


def body(features, w_hidden, w_embed, members, doc_owner, doc_local, member_cluster, member_valid):
    dp = ("z", "core")
    steps = (1, -1, 2)
    half, unit = prepared(*map(stay, (w_hidden, w_embed, members, member_cluster, member_valid)))
    units = lax.all_gather(unit, ("y", "x"), axis=0, tiled=True)
    mine = lax.all_to_all(half, "y", 0, 0, tiled=True)
    docs = [shift(features, "x", k) for k in steps]
    mine, *docs = lax.optimization_barrier((mine, *docs))
    other = swap(mine)
    mark = swap(member_cluster)

    first = lax.axis_index(("y", "x")) * ROWS
    owner = lax.dynamic_slice_in_dim(doc_owner[:, 0], first, ROWS, 0)
    local = lax.dynamic_slice_in_dim(doc_local, first, ROWS, 0)
    owner_row = owner.reshape(1, ROWS)
    place, tags, rank_row = call(
        slots_kernel,
        (
            sds((4, OWNERS * LINES, ROWS), BF16),
            sds((ROWS, CHUNK), BF16),
            sds((1, ROWS), I32),
        ),
        "slots",
    )(owner_row, owner.reshape(ROWS, 1), local.reshape(ROWS, 1), mark)

    own, *parts = head(*map(stay, (features, *docs)), mine, other)
    parts = [shift(p, "x", -k) for p, k in zip(parts, steps)]
    outgoing = query(stay(own), *parts, place, tags)
    arrived = lax.all_to_all(outgoing, dp, 0, 0, tiled=True)
    best = score(arrived, picking(), stay(units))
    answers = lax.all_to_all(best, dp, 0, 0, tiled=True)
    result = call(answer_kernel, sds((1, ROWS), F32), "answer")(answers, owner_row, rank_row)
    return result.reshape(ROWS)


def solution(mesh):
    grid = Mesh(mesh.devices.reshape(16, 2, 4, 4), ("z", "core", "y", "x"))
    dp, tensor = ("z", "core"), ("y", "x")
    every = dp + tensor
    return jax.shard_map(
        body,
        mesh=grid,
        in_specs=(
            P(every, None),
            P(None, tensor),
            P(tensor, None),
            P(dp, tensor, None),
            P(dp, None),
            P(dp),
            P(dp, tensor),
            P(dp, tensor),
        ),
        out_specs=P(every),
        check_vma=False,
    )
```

time: 149 us -> 128 us (0.86)
  blocking collectives: 87.5 us -> 52.9 us
  starting transfers between devices: 8.57 us -> 36.1 us
  waiting for transfers between devices: 23.8 us -> 9.89 us
  Pallas kernels: 6.3 us -> 12.4 us
  local copies, waits for them, and re-layouts: 8.58 us -> 2.57 us
    all_to_all x2 -> x0, blocking collectives: 36.8 us -> none  [the longest x1 29.3 us: body(): halves = lax.all_to_all(half, 'y', 0, 0, tiled=True)]
    ppermute x0 -> x8, starting transfers between devices: none -> 31 us  [the longest x6 20.4 us: shift(): return lax.ppermute(value, axis, [(i, (i + step) % 4) for i in range(4)])]
    all_to_all x2 -> x1, waiting for transfers between devices: 23.8 us -> 0.01 us  [body(): mine = lax.all_to_all(half, 'y', 0, 0, tiled=True)]
    pallas_call x0 -> x4, Pallas kernels: none -> 11.3 us  [the longest x1 3.46 us: score(): pl.pallas_call(score_kernel, out_shape=sds((OWNERS, SLOTS), F32), in_spec...]
    ppermute x0 -> x8, waiting for transfers between devices: none -> 9.87 us  [the longest x6 9.75 us: shift(): return lax.ppermute(value, axis, [(i, (i + step) % 4) for i in range(4)])]
    pallas_call x7 -> x2, Pallas kernels: 6.3 us -> 1.05 us  [run(): pl.pallas_call(body, out_shape=out, in_specs=specs, out_specs=outs, name=...]
    unnamed x17 -> x13, local copies, waits for them, and re-layouts: 4.31 us -> 0.88 us
    all_to_all x2 -> x1, starting transfers between devices: 8.57 us -> 5.16 us  [body(): mine = lax.all_to_all(half, 'y', 0, 0, tiled=True)]
  transfers between devices with their start and end apart: 3 -> 10, of which waited for: 2 -> 5; matrix products, arithmetic and copies ran while one was open for 3% -> 1% of each run, Pallas kernels for 2% -> 4%
where the time goes in v2:
time: 128 us; the launch traced here: 127 us
  blocking collectives  52.9 us (41%)
  starting transfers between devices  36.1 us (28%)
  between operations  13.6 us (11%)
  Pallas kernels  12.4 us (10%)
  waiting for transfers between devices  9.89 us (8%)
  local copies, waits for them, and re-layouts  2.57 us (2%)
    all_to_all x1, blocking collectives, body(): arrived = lax.all_to_all(outgoing, dp, 0, 0, tiled=True)  37.4 us
    ppermute x6, starting transfers between devices, shift(): return lax.ppermute(value, axis, [(i, (i + step) % 4) for i in range(4)])  20.4 us
    all_to_all x1, blocking collectives, body(): answers = lax.all_to_all(best, dp, 0, 0, tiled=True)  15.5 us
    ppermute x2, starting transfers between devices, swap(): return lax.ppermute(value, 'core', [(0, 1), (1, 0)])  10.6 us
    ppermute x6, waiting for transfers between devices, shift(): return lax.ppermute(value, axis, [(i, (i + step) % 4) for i in range(4)])  9.75 us
    all_to_all x1, starting transfers between devices, body(): mine = lax.all_to_all(half, 'y', 0, 0, tiled=True)  5.16 us
    pallas_call x1, Pallas kernels, score(): pl.pallas_call(score_kernel, out_shape=sds((OWNERS, SLOTS), F32), in_spec...  3.46 us
    pallas_call x1, Pallas kernels, head(): pl.pallas_call(head_kernel, out_shape=(pltpu.HBM((ROWS, EMB), F32), piece...  3.3 us
  transfers between devices with their start and end apart: 10, of which 5 were waited for; matrix products, arithmetic and copies ran while one was open for 1% of the time, Pallas kernels for 4%

profile of v2, /device:TPU:1, one launch (start us, length us, event | category | flops | bytes accessed | tf_op | source)
XLA Modules:
  0.0 127.5 jit_solution(2672078243155207701)
XLA Ops:
  6.5 0.0 copy-start
  6.5 0.0 all-gather.2.cloned.1.call-start
  6.5 3.1 %prepare.1 = (bf16[4,1408,128]{2,1,0:T(8,128)(2,1)}, bf16[136,768]{1,0:T(8,128)(2,1)}) custom-call(bf16[2048,128]{1,0:T(8,128)(2,1)} %w_hidden.1, bf16[128,768]{1,0:T(8,128)(2,1)} %w_embed.1, bf16[1,128,768]{2,1,0:T(8,128)(2,1)} %members.1, s32[1,128]{1,0:T(1,128)} %cluster.1, s32[1,128]{1,0:T(1,128)} %valid.1), custom_call_target="tpu_custom_call" | custom-call | tf_op jit(solution)/shard_map/prepare/pallas_call | solution.py:228
  9.6 0.0 all-gather.2.cloned.1.call-update
  9.7 0.0 copy-start.2
  9.7 0.0 copy-start.5
  9.7 5.2 %all-to-all-start = ((bf16[4,1408,128]{2,1,0:T(8,128)(2,1)}), bf16[4,1408,128]{2,1,0:T(8,128)(2,1)S(1)}, u32[]{:S(2)}, u32[]{:S(2)}) async-start(bf16[4,1408,128]{2,1,0:T(8,128)(2,1)} %get-tuple-element.18), calls=%async_computation | async-start | bytes 2883584 | tf_op jit(solution)/shard_map/all_to_all | solution.py:302
  14.9 0.0 copy-done.2
  14.9 3.1 %collective-permute-start = (bf16[80,2048]{1,0:T(8,128)(2,1)S(1)}, bf16[80,2048]{1,0:T(8,128)(2,1)S(1)}, u32[]{:S(2)}, u32[]{:S(2)}) collective-permute-start(bf16[80,2048]{1,0:T(8,128)(2,1)S(1)} %copy-done.2), channel_id=1, source_target_pairs={{0,1},{1,2},{2,3},{3,0},{4,5},{5,6},{6,7},{7,4},{8,9},{9,10},{10,1... | collective-permute-start | bytes 983048 | tf_op jit(solution)/shard_map/ppermute | solution.py:220
  18.0 3.4 %collective-permute-start.1 = (bf16[80,2048]{1,0:T(8,128)(2,1)S(1)}, bf16[80,2048]{1,0:T(8,128)(2,1)S(1)}, u32[]{:S(2)}, u32[]{:S(2)}) collective-permute-start(bf16[80,2048]{1,0:T(8,128)(2,1)S(1)} %copy-done.2), channel_id=1, source_target_pairs={{0,3},{1,0},{2,1},{3,2},{4,7},{5,4},{6,5},{7,6},{8,11},{9,8},{10,9... | collective-permute-start | bytes 983048 | tf_op jit(solution)/shard_map/ppermute | solution.py:220
  21.4 3.4 %collective-permute-start.2 = (bf16[80,2048]{1,0:T(8,128)(2,1)S(1)}, bf16[80,2048]{1,0:T(8,128)(2,1)}, u32[]{:S(2)}, u32[]{:S(2)}) collective-permute-start(bf16[80,2048]{1,0:T(8,128)(2,1)S(1)} %copy-done.2), channel_id=1, source_target_pairs={{0,2},{1,3},{2,0},{3,1},{4,6},{5,7},{6,4},{7,5},{8,10},{9,11},{10,... | collective-permute-start | bytes 983048 | tf_op jit(solution)/shard_map/ppermute | solution.py:220
  24.8 0.0 collective-permute-done.left
  24.8 0.0 copy-start.3
  24.8 1.3 collective-permute-done.1.right
  26.1 0.0 copy-done.3
  26.1 0.0 copy-start.4
  26.1 0.7 copy-done.4
  26.8 5.4 %collective-permute-done.2.far = bf16[80,2048]{1,0:T(8,128)(2,1)} collective-permute-done((bf16[80,2048]{1,0:T(8,128)(2,1)S(1)}, bf16[80,2048]{1,0:T(8,128)(2,1)}, u32[]{:S(2)}, u32[]{:S(2)}) %collective-permute-start.2) | collective-permute-done | bytes 327712 | tf_op jit(solution)/shard_map/ppermute | solution.py:220
  32.2 0.0 all-to-all-done.mine
  32.2 8.7 %collective-permute-start.3 = (bf16[4,1408,128]{2,1,0:T(8,128)(2,1)S(1)}, bf16[4,1408,128]{2,1,0:T(8,128)(2,1)S(1)}, u32[]{:S(2)}, u32[]{:S(2)}) collective-permute-start(bf16[4,1408,128]{2,1,0:T(8,128)(2,1)S(1)} %all-to-all-done.mine), channel_id=1, source_target_pairs={{0,16},{16,0},{1,17},{17,1},{2,18},{18,2},{3,19},{19,3},{4,20},{20... | collective-permute-start | bytes 4325384 | tf_op jit(solution)/shard_map/ppermute | solution.py:294
  40.9 0.0 copy-done.5
  40.9 1.9 %collective-permute-start.7 = (s32[1,128]{1,0:T(1,128)S(1)}, s32[1,128]{1,0:T(1,128)S(1)}, u32[]{:S(2)}, u32[]{:S(2)}) collective-permute-start(s32[1,128]{1,0:T(1,128)S(1)} %copy-done.5), channel_id=1, source_target_pairs={{0,16},{16,0},{1,17},{17,1},{2,18},{18,2},{3,19},{19,3},{4,20},{20... | collective-permute-start | bytes 1544 | tf_op jit(solution)/shard_map/ppermute | solution.py:294
  42.9 0.8 fusion.owner_row
  43.6 0.1 collective-permute-done.3.other
  43.8 3.3 %head.1 = (f32[80,768]{1,0:T(8,128)}, bf16[80,768]{1,0:T(8,128)(2,1)S(1)}, bf16[80,768]{1,0:T(8,128)(2,1)S(1)}, bf16[80,768]{1,0:T(8,128)(2,1)S(1)}) custom-call(bf16[80,2048]{1,0:T(8,128)(2,1)} %own.1, bf16[80,2048]{1,0:T(8,128)(2,1)} %copy-done.3, bf16[80,2048]{1,0:T(8,128)(2,1)} %copy-done.4, bf16[80,2048]{1,0:T(8,128)(2,1)} %collective-permute-done.2.far, ...), custom_call_target="tpu_custom_call" | custom-call | tf_op jit(solution)/shard_map/head/pallas_call | solution.py:250
  47.1 0.0 copy-start.1
  47.1 5.4 %collective-permute-start.4 = (bf16[80,768]{1,0:T(8,128)(2,1)S(1)}, bf16[80,768]{1,0:T(8,128)(2,1)S(1)}, u32[]{:S(2)}, u32[]{:S(2)}) collective-permute-start(bf16[80,768]{1,0:T(8,128)(2,1)S(1)} %get-tuple-element.24), channel_id=1, source_target_pairs={{0,3},{1,0},{2,1},{3,2},{4,7},{5,4},{6,5},{7,6},{8,11},{9,8},{10,9... | collective-permute-start | bytes 368648 | tf_op jit(solution)/shard_map/ppermute | solution.py:220
  52.5 1.9 %collective-permute-start.5 = (bf16[80,768]{1,0:T(8,128)(2,1)S(1)}, bf16[80,768]{1,0:T(8,128)(2,1)S(1)}, u32[]{:S(2)}, u32[]{:S(2)}) collective-permute-start(bf16[80,768]{1,0:T(8,128)(2,1)S(1)} %get-tuple-element.25), channel_id=1, source_target_pairs={{0,1},{1,2},{2,3},{3,0},{4,5},{5,6},{6,7},{7,4},{8,9},{9,10},{10,1... | collective-permute-start | bytes 368648 | tf_op jit(solution)/shard_map/ppermute | solution.py:220
  54.4 3.1 %collective-permute-start.6 = (bf16[80,768]{1,0:T(8,128)(2,1)S(1)}, bf16[80,768]{1,0:T(8,128)(2,1)S(1)}, u32[]{:S(2)}, u32[]{:S(2)}) collective-permute-start(bf16[80,768]{1,0:T(8,128)(2,1)S(1)} %get-tuple-element.26), channel_id=1, source_target_pairs={{0,2},{1,3},{2,0},{3,1},{4,6},{5,7},{6,4},{7,5},{8,10},{9,11},{10,... | collective-permute-start | bytes 368648 | tf_op jit(solution)/shard_map/ppermute | solution.py:220
  57.5 0.8 constant_dynamic-slice_fusion
  58.3 0.0 copy-done
  58.3 0.1 dynamic-slice_bitcast_fusion
  58.4 0.1 copy.17.owner_col
  58.5 0.1 copy.15.local_col
  58.6 0.0 collective-permute-done.7.mark
  58.6 0.4 slots.1
  59.0 0.0 collective-permute-done.4.left
  59.0 0.8 collective-permute-done.5.right
  59.8 2.3 %collective-permute-done.6.far = bf16[80,768]{1,0:T(8,128)(2,1)S(1)} collective-permute-done((bf16[80,768]{1,0:T(8,128)(2,1)S(1)}, bf16[80,768]{1,0:T(8,128)(2,1)S(1)}, u32[]{:S(2)}, u32[]{:S(2)}) %collective-permute-start.6) | collective-permute-done | bytes 122912 | tf_op jit(solution)/shard_map/ppermute | solution.py:220
  62.1 1.5 %query.1 = bf16[32,16,256]{2,1,0:T(8,128)(2,1)S(1)} custom-call(f32[80,768]{1,0:T(8,128)} %get-tuple-element.23.own, bf16[80,768]{1,0:T(8,128)(2,1)S(1)} %collective-permute-done.4.left, bf16[80,768]{1,0:T(8,128)(2,1)S(1)} %collective-permute-done.5.right, bf16[80,768]{1,0:T(8,128)(2,1)S(1)} %collective-permute-done.6.far, ...), custom_call_target="tpu_custom_call" | custom-call | tf_op jit(solution)/shard_map/query/pallas_call | solution.py:266
  63.6 37.4 %all_to_all.21.arrived = bf16[32,16,256]{2,1,0:T(8,128)(2,1)S(1)} all-to-all(bf16[32,16,256]{2,1,0:T(8,128)(2,1)S(1)} %query.1), channel_id=1, replica_groups=mesh['z'=16,'core'=2,'y'=4,'x'=4] {'z','core'}, dimensions={0} | all-to-all | bytes 524288 | tf_op jit(solution)/shard_map/all_to_all | solution.py:325
  101.0 0.0 all-gather.2.cloned.1.call-done.units
  101.0 0.0 copy-done.1
  101.0 3.5 %score.1 = f32[32,128]{1,0:T(8,128)S(1)} custom-call(bf16[32,16,256]{2,1,0:T(8,128)(2,1)S(1)} %all_to_all.21.arrived, bf16[640,512]{1,0:T(8,128)(2,1)S(1)} %copy-done.1, bf16[2176,768]{1,0:T(8,128)(2,1)} %all-gather.2.cloned.1.call-done.units), custom_call_target="tpu_custom_call" | custom-call | tf_op jit(solution)/shard_map/score/pallas_call | solution.py:278
  104.5 15.5 %all_to_all.22 = f32[32,1,128]{2,1,0:T(1,128)S(1)} all-to-all(f32[32,1,128]{2,1,0:T(1,128)S(1)} %bitcast.10), channel_id=1, replica_groups=mesh['z'=16,'core'=2,'y'=4,'x'=4] {'z','core'}, dimensions={0} | all-to-all | bytes 32768 | tf_op jit(solution)/shard_map/all_to_all | solution.py:327
  120.0 0.6 answer.1
Async XLA Ops:
  6.5 51.8 %copy-start = (s32[1280]{0:T(1024)S(1)}, s32[1280]{0:T(1024)}, u32[]{:S(2)}) copy-start(s32[1280]{0:T(1024)} %param.14) | copy-start | bytes 15364
  6.5 94.5 %all-gather.2.cloned.1.call-start = ((), (), s32[]{:S(2)}) async-start(), calls=%async_computation.3 | async-start | bytes 3551232 | tf_op jit(solution)/shard_map/all_gather | solution.py:301
  9.7 5.2 %copy-start.2 = (bf16[80,2048]{1,0:T(8,128)(2,1)S(1)}, bf16[80,2048]{1,0:T(8,128)(2,1)}, u32[]{:S(2)}) copy-start(bf16[80,2048]{1,0:T(8,128)(2,1)} %own.1) | copy-start | bytes 983044
  9.7 31.3 %copy-start.5 = (s32[1,128]{1,0:T(1,128)S(1)}, s32[1,128]{1,0:T(1,128)}, u32[]{:S(2)}) copy-start(s32[1,128]{1,0:T(1,128)} %cluster.1) | copy-start | bytes 1540
  9.7 22.5 %all-to-all-start = ((bf16[4,1408,128]{2,1,0:T(8,128)(2,1)}), bf16[4,1408,128]{2,1,0:T(8,128)(2,1)S(1)}, u32[]{:S(2)}, u32[]{:S(2)}) async-start(bf16[4,1408,128]{2,1,0:T(8,128)(2,1)} %get-tuple-element.18), calls=%async_computation | async-start | bytes 2883584 | tf_op jit(solution)/shard_map/all_to_all | solution.py:302
  14.9 10.0 %collective-permute-start = (bf16[80,2048]{1,0:T(8,128)(2,1)S(1)}, bf16[80,2048]{1,0:T(8,128)(2,1)S(1)}, u32[]{:S(2)}, u32[]{:S(2)}) collective-permute-start(bf16[80,2048]{1,0:T(8,128)(2,1)S(1)} %copy-done.2), channel_id=1, source_target_pairs={{0,1},{1,2},{2,3},{3,0},{4,5},{5,6},{6,7},{7,4},{8,9},{9,10},{10,1... | collective-permute-start | bytes 983048 | tf_op jit(solution)/shard_map/ppermute | solution.py:220
  18.0 8.1 %collective-permute-start.1 = (bf16[80,2048]{1,0:T(8,128)(2,1)S(1)}, bf16[80,2048]{1,0:T(8,128)(2,1)S(1)}, u32[]{:S(2)}, u32[]{:S(2)}) collective-permute-start(bf16[80,2048]{1,0:T(8,128)(2,1)S(1)} %copy-done.2), channel_id=1, source_target_pairs={{0,3},{1,0},{2,1},{3,2},{4,7},{5,4},{6,5},{7,6},{8,11},{9,8},{10,9... | collective-permute-start | bytes 983048 | tf_op jit(solution)/shard_map/ppermute | solution.py:220
  21.4 10.9 %collective-permute-start.2 = (bf16[80,2048]{1,0:T(8,128)(2,1)S(1)}, bf16[80,2048]{1,0:T(8,128)(2,1)}, u32[]{:S(2)}, u32[]{:S(2)}) collective-permute-start(bf16[80,2048]{1,0:T(8,128)(2,1)S(1)} %copy-done.2), channel_id=1, source_target_pairs={{0,2},{1,3},{2,0},{3,1},{4,6},{5,7},{6,4},{7,5},{8,10},{9,11},{10,... | collective-permute-start | bytes 983048 | tf_op jit(solution)/shard_map/ppermute | solution.py:220
  24.8 1.3 copy-start.3
  26.1 0.8 copy-start.4
  32.2 11.5 %collective-permute-start.3 = (bf16[4,1408,128]{2,1,0:T(8,128)(2,1)S(1)}, bf16[4,1408,128]{2,1,0:T(8,128)(2,1)S(1)}, u32[]{:S(2)}, u32[]{:S(2)}) collective-permute-start(bf16[4,1408,128]{2,1,0:T(8,128)(2,1)S(1)} %all-to-all-done.mine), channel_id=1, source_target_pairs={{0,16},{16,0},{1,17},{17,1},{2,18},{18,2},{3,19},{19,3},{4,20},{20... | collective-permute-start | bytes 4325384 | tf_op jit(solution)/shard_map/ppermute | solution.py:294
  40.9 17.6 %collective-permute-start.7 = (s32[1,128]{1,0:T(1,128)S(1)}, s32[1,128]{1,0:T(1,128)S(1)}, u32[]{:S(2)}, u32[]{:S(2)}) collective-permute-start(s32[1,128]{1,0:T(1,128)S(1)} %copy-done.5), channel_id=1, source_target_pairs={{0,16},{16,0},{1,17},{17,1},{2,18},{18,2},{3,19},{19,3},{4,20},{20... | collective-permute-start | bytes 1544 | tf_op jit(solution)/shard_map/ppermute | solution.py:294
  47.1 54.0 %copy-start.1 = (bf16[640,512]{1,0:T(8,128)(2,1)S(1)}, bf16[640,512]{1,0:T(8,128)(2,1)}, u32[]{:S(2)}) copy-start(bf16[640,512]{1,0:T(8,128)(2,1)} %constant.18.clone.pick) | copy-start | bytes 1966084
  47.1 12.0 %collective-permute-start.4 = (bf16[80,768]{1,0:T(8,128)(2,1)S(1)}, bf16[80,768]{1,0:T(8,128)(2,1)S(1)}, u32[]{:S(2)}, u32[]{:S(2)}) collective-permute-start(bf16[80,768]{1,0:T(8,128)(2,1)S(1)} %get-tuple-element.24), channel_id=1, source_target_pairs={{0,3},{1,0},{2,1},{3,2},{4,7},{5,4},{6,5},{7,6},{8,11},{9,8},{10,9... | collective-permute-start | bytes 368648 | tf_op jit(solution)/shard_map/ppermute | solution.py:220
  52.5 7.3 %collective-permute-start.5 = (bf16[80,768]{1,0:T(8,128)(2,1)S(1)}, bf16[80,768]{1,0:T(8,128)(2,1)S(1)}, u32[]{:S(2)}, u32[]{:S(2)}) collective-permute-start(bf16[80,768]{1,0:T(8,128)(2,1)S(1)} %get-tuple-element.25), channel_id=1, source_target_pairs={{0,1},{1,2},{2,3},{3,0},{4,5},{5,6},{6,7},{7,4},{8,9},{9,10},{10,1... | collective-permute-start | bytes 368648 | tf_op jit(solution)/shard_map/ppermute | solution.py:220
  54.4 7.7 %collective-permute-start.6 = (bf16[80,768]{1,0:T(8,128)(2,1)S(1)}, bf16[80,768]{1,0:T(8,128)(2,1)S(1)}, u32[]{:S(2)}, u32[]{:S(2)}) collective-permute-start(bf16[80,768]{1,0:T(8,128)(2,1)S(1)} %get-tuple-element.26), channel_id=1, source_target_pairs={{0,2},{1,3},{2,0},{3,1},{4,6},{5,7},{6,4},{7,5},{8,10},{9,11},{10,... | collective-permute-start | bytes 368648 | tf_op jit(solution)/shard_map/ppermute | solution.py:220
Sparse Core Ops, SparseCore 0:
  10.4 72.3 all-gather.1

commit v3 on v2

--- a/solution.py
+++ b/solution.py
@@ -79,7 +79,7 @@
         copy.wait()
 
 
-def slots_kernel(owner_row, owner_col, local_col, mark, place, tags, rank_row):
+def slots_kernel(owner_row, owner_col, local_col, place, tags, rank_row):
     row, col = owner_row[...], owner_col[...]
     same = row == col
     up, across = iota((ROWS, ROWS), 0), iota((ROWS, ROWS), 1)
@@ -96,47 +96,43 @@
     tags[...] = jnp.where(lane == ranks_col, local_col[...] + 1, 0).astype(F32).astype(BF16)
 
 
-def head_kernel(
-    own, left, right, far, mine, other, own_out, left_out, right_out, far_out, docs, kept, sem
-):
+def first_kernel(own, left, right, far_a, far_b, mine, pre, rest, docs, sem):
     c = lax.axis_index("core")
-    copies = [
-        pltpu.make_async_copy(part, docs.at[i * ROWS : (i + 1) * ROWS, :], sem.at[i + 1])
-        for i, part in enumerate((own, left, right, far))
-    ]
+    copies, row = [], 0
+    for i, part in enumerate((own, left, right, far_a, far_b)):
+        rows = part.shape[0]
+        copies.append(pltpu.make_async_copy(part, docs.at[row : row + rows, :], sem.at[i]))
+        row += rows
     for copy in copies:
         copy.start()
+    w = jnp.concatenate([mine[j, 0:HALF, :] for j in range(4)], axis=1)
     for copy in copies:
         copy.wait()
-    pre, embeds = None, []
-    for half, weights in ((c, mine), (1 - c, other)):
-        lines = docs[:, pl.ds(pl.multiple_of(half * HALF, HALF), HALF)]
-        w = jnp.concatenate([weights[j, 0:HALF, :] for j in range(4)], axis=1)
-        part = jnp.dot(lines, w, preferred_element_type=F32)
-        pre = part if pre is None else pre + part
+    lines = docs[:, pl.ds(pl.multiple_of(c * HALF, HALF), HALF)]
+    pre[...] = jnp.dot(lines, w, preferred_element_type=F32)
+    rest[...] = docs[:, pl.ds(pl.multiple_of((1 - c) * HALF, HALF), HALF)]
+
+
+def head_kernel(pre, rest, mine, other, out):
+    x = lax.axis_index("x")
+    w = jnp.concatenate([other[j, 0:HALF, :] for j in range(4)], axis=1)
+    total = pre[...] + jnp.dot(rest[...], w, preferred_element_type=F32)
+    hidden = jax.nn.gelu(total).astype(BF16)
+    for k, weights in enumerate((mine, other)):
         rows = []
         for j in range(4):
             cut = [HALF + i * BLOCK for i in range(3)]
             rows.append(jnp.concatenate([weights[j, r : r + BLOCK, :] for r in cut], axis=1))
-        embeds.append(jnp.concatenate(rows, axis=0))
-    hidden = jax.nn.gelu(pre).astype(BF16)
-    for k, embed in enumerate(embeds):
-        total = jnp.dot(hidden, embed, preferred_element_type=F32)
+        total = jnp.dot(hidden, jnp.concatenate(rows, axis=0), preferred_element_type=F32)
         cut = slice(k * 3 * BLOCK, (k + 1) * 3 * BLOCK)
-        kept[:, cut] = total[0:ROWS]
-        for j, out in enumerate((left_out, right_out, far_out)):
-            out[:, cut] = total[(j + 1) * ROWS : (j + 2) * ROWS].astype(BF16)
-    copy = pltpu.make_async_copy(kept, own_out, sem.at[0])
-    copy.start()
-    copy.wait()
-
-
-def query_kernel(own, left, right, far, place, tags, out, kept, sem):
-    copy = pltpu.make_async_copy(own, kept, sem.at[0])
-    copy.start()
-    proj = left[...].astype(F32) + right[...].astype(F32) + far[...].astype(F32)
-    copy.wait()
-    proj = proj + kept[...]
+        for j, step in enumerate((0, 3, 1, 2)):
+            out[lax.rem(x + step, 4), :, cut] = total[j * ROWS : (j + 1) * ROWS].astype(BF16)
+
+
+def query_kernel(partial, place, tags, out):
+    proj = partial[0].astype(F32)
+    for j in range(1, 4):
+        proj = proj + partial[j].astype(F32)
     norm = jnp.sum(proj * proj, axis=1, keepdims=True)
     query = proj * (1.0 / jnp.sqrt(norm + EPS))
     low, high = query[:, 0 : EMB // 2], query[:, EMB // 2 :]
@@ -196,15 +192,6 @@
     out[...] = result
 
 
-def answer_kernel(answers, owner_row, rank_row, out):
-    mine = owner_row[...] == iota((OWNERS, ROWS), 0)
-    total = jnp.zeros((1, ROWS), F32)
-    for s in range(CAP):
-        value = jnp.sum(jnp.where(mine, answers[:, s : s + 1], 0.0), axis=0, keepdims=True)
-        total = jnp.where(rank_row[...] == s, value, total)
-    out[...] = total
-
-
 def picking():
     count = OWNERS * CAP
     pick = np.zeros((4 * count, OWNERS * LINES), np.float32)
@@ -216,6 +203,15 @@
     return jnp.asarray(pick, BF16)
 
 
+def answer_kernel(answers, owner_row, rank_row, out):
+    mine = owner_row[...] == iota((OWNERS, ROWS), 0)
+    total = jnp.zeros((1, ROWS), F32)
+    for s in range(CAP):
+        value = jnp.sum(jnp.where(mine, answers[:, s : s + 1], 0.0), axis=0, keepdims=True)
+        total = jnp.where(rank_row[...] == s, value, total)
+    out[...] = total
+
+
 def shift(value, axis, step):
     return lax.ppermute(value, axis, [(i, (i + step) % 4) for i in range(4)])
 
@@ -227,7 +223,7 @@
 def prepared(*arrays):
     return pl.pallas_call(
         prepare_kernel,
-        out_shape=(sds((4, PACK, BLOCK), BF16), sds((UNIT, EMB), BF16)),
+        out_shape=(pltpu.VMEM((4, PACK, BLOCK), BF16), sds((UNIT, EMB), BF16)),
         in_specs=[HBM] * 5,
         out_specs=(VMEM, VMEM),
         scratch_shapes=[
@@ -242,38 +238,6 @@
     )(*arrays)
 
 
-KEPT = [pltpu.VMEM((ROWS, EMB), F32), pltpu.SemaphoreType.DMA((1,))]
-
-
-def head(*arrays):
-    piece = sds((ROWS, EMB), BF16)
-    return pl.pallas_call(
-        head_kernel,
-        out_shape=(pltpu.HBM((ROWS, EMB), F32), piece, piece, piece),
-        in_specs=[HBM] * 4 + [VMEM] * 2,
-        out_specs=(HBM, VMEM, VMEM, VMEM),
-        scratch_shapes=[
-            pltpu.VMEM((4 * ROWS, HID), BF16),
-            pltpu.VMEM((ROWS, EMB), F32),
-            pltpu.SemaphoreType.DMA((5,)),
-        ],
-        name="head",
-        compiler_params=PARAMS,
-    )(*arrays)
-
-
-def query(*arrays):
-    return pl.pallas_call(
-        query_kernel,
-        out_shape=sds((OWNERS, LINES, CHUNK), BF16),
-        in_specs=[HBM] + [VMEM] * 5,
-        out_specs=VMEM,
-        scratch_shapes=KEPT,
-        name="query",
-        compiler_params=PARAMS,
-    )(*arrays)
-
-
 def score(arrived, pick, units):
     return pl.pallas_call(
         score_kernel,
@@ -286,6 +250,22 @@
     )(arrived, pick, units)
 
 
+def first(*arrays):
+    return pl.pallas_call(
+        first_kernel,
+        out_shape=(pltpu.VMEM((4 * ROWS, 4 * BLOCK), F32), pltpu.VMEM((4 * ROWS, HALF), BF16)),
+        in_specs=[HBM] * 5 + [VMEM],
+        out_specs=(VMEM, VMEM),
+        scratch_shapes=[pltpu.VMEM((4 * ROWS, HID), BF16), pltpu.SemaphoreType.DMA((5,))],
+        name="first",
+        compiler_params=PARAMS,
+    )(*arrays)
+
+
+def near(value):
+    return pltpu.with_memory_space_constraint(value, pltpu.VMEM)
+
+
 def stay(value):
     return pltpu.with_memory_space_constraint(value, pltpu.HBM)
 
@@ -296,32 +276,35 @@
 
 def body(features, w_hidden, w_embed, members, doc_owner, doc_local, member_cluster, member_valid):
     dp = ("z", "core")
-    steps = (1, -1, 2)
     half, unit = prepared(*map(stay, (w_hidden, w_embed, members, member_cluster, member_valid)))
     units = lax.all_gather(unit, ("y", "x"), axis=0, tiled=True)
-    mine = lax.all_to_all(half, "y", 0, 0, tiled=True)
-    docs = [shift(features, "x", k) for k in steps]
-    mine, *docs = lax.optimization_barrier((mine, *docs))
-    other = swap(mine)
-    mark = swap(member_cluster)
-
-    first = lax.axis_index(("y", "x")) * ROWS
-    owner = lax.dynamic_slice_in_dim(doc_owner[:, 0], first, ROWS, 0)
-    local = lax.dynamic_slice_in_dim(doc_local, first, ROWS, 0)
+    mine = lax.all_to_all(near(half), "y", 0, 0, tiled=True)
+    left, right = shift(features, "x", 1), shift(features, "x", -1)
+    cut = 48
+    docs = [left, right, shift(left[:cut], "x", 1), shift(right[cut:], "x", -1)]
+
+    start = lax.axis_index(("y", "x")) * ROWS
+    owner = lax.dynamic_slice_in_dim(doc_owner[:, 0], start, ROWS, 0)
+    local = lax.dynamic_slice_in_dim(doc_local, start, ROWS, 0)
     owner_row = owner.reshape(1, ROWS)
     place, tags, rank_row = call(
         slots_kernel,
         (
-            sds((4, OWNERS * LINES, ROWS), BF16),
-            sds((ROWS, CHUNK), BF16),
+            pltpu.VMEM((4, OWNERS * LINES, ROWS), BF16),
+            pltpu.VMEM((ROWS, CHUNK), BF16),
             sds((1, ROWS), I32),
         ),
         "slots",
-    )(owner_row, owner.reshape(ROWS, 1), local.reshape(ROWS, 1), mark)
-
-    own, *parts = head(*map(stay, (features, *docs)), mine, other)
-    parts = [shift(p, "x", -k) for p, k in zip(parts, steps)]
-    outgoing = query(stay(own), *parts, place, tags)
+    )(owner_row, owner.reshape(ROWS, 1), local.reshape(ROWS, 1))
+
+    mine, place, *docs = lax.optimization_barrier((mine, place, *docs))
+    other = swap(mine)
+    pre, rest = first(*map(stay, (features, *docs)), mine)
+    partial = call(head_kernel, sds((4, ROWS, EMB), BF16), "head")(near(pre), near(rest), mine, other)
+    partial = lax.all_to_all(partial, "x", 0, 0, tiled=True)
+    outgoing = call(query_kernel, sds((OWNERS, LINES, CHUNK), BF16), "query")(
+        partial, near(place), near(tags)
+    )
     arrived = lax.all_to_all(outgoing, dp, 0, 0, tiled=True)
     best = score(arrived, picking(), stay(units))
     answers = lax.all_to_all(best, dp, 0, 0, tiled=True)

time: 128 us -> 124 us (0.969)
  blocking collectives: 52.9 us -> 65.1 us
  starting transfers between devices: 36.1 us -> 28 us
  waiting for transfers between devices: 9.89 us -> 3.81 us
  Pallas kernels: 12.4 us -> 11 us
    all_to_all x0 -> x1, blocking collectives: none -> 13 us  [body(): partial = lax.all_to_all(partial, 'x', 0, 0, tiled=True)]
    ppermute x6 -> x4, waiting for transfers between devices: 9.75 us -> 2.84 us  [shift(): return lax.ppermute(value, axis, [(i, (i + step) % 4) for i in range(4)])]
    ppermute x6 -> x4, starting transfers between devices: 20.4 us -> 14.1 us  [shift(): return lax.ppermute(value, axis, [(i, (i + step) % 4) for i in range(4)])]
    pallas_call x3 -> x2, Pallas kernels: 7.88 us -> 4.94 us  [the longest x1 3.11 us: prepared(): pl.pallas_call(prepare_kernel, out_shape=(pltpu.VMEM((4, PACK, BLOCK), BF...]
    ppermute x2 -> x1, starting transfers between devices: 10.6 us -> 8.77 us  [swap(): return lax.ppermute(value, 'core', [(0, 1), (1, 0)])]
    pallas_call x2 -> x4, Pallas kernels: 1.05 us -> 2.65 us  [run(): pl.pallas_call(body, out_shape=out, in_specs=specs, out_specs=outs, name=...]
  transfers between devices with their start and end apart: 10 -> 7, of which waited for: 5 -> 3; matrix products, arithmetic and copies ran while one was open for 1% -> 1% of each run, Pallas kernels for 4% -> 3%
where the time goes in v3:
time: 124 us; the launch traced here: 123 us
  blocking collectives  65.1 us (52%)
  starting transfers between devices  28 us (23%)
  between operations  13.6 us (11%)
  Pallas kernels  11 us (9%)
  waiting for transfers between devices  3.81 us (3%)
  local copies, waits for them, and re-layouts  1.85 us (1%)
    all_to_all x1, blocking collectives, body(): arrived = lax.all_to_all(outgoing, dp, 0, 0, tiled=True)  36.5 us
    all_to_all x1, blocking collectives, body(): answers = lax.all_to_all(best, dp, 0, 0, tiled=True)  15.5 us
    ppermute x4, starting transfers between devices, shift(): return lax.ppermute(value, axis, [(i, (i + step) % 4) for i in range(4)])  14.1 us
    all_to_all x1, blocking collectives, body(): partial = lax.all_to_all(partial, 'x', 0, 0, tiled=True)  13 us
    ppermute x1, starting transfers between devices, swap(): return lax.ppermute(value, 'core', [(0, 1), (1, 0)])  8.77 us
    all_to_all x1, starting transfers between devices, body(): mine = lax.all_to_all(near(half), 'y', 0, 0, tiled=True)  5.16 us
    pallas_call x1, Pallas kernels, score(): pl.pallas_call(score_kernel, out_shape=sds((OWNERS, SLOTS), F32), in_spec...  3.46 us
    pallas_call x1, Pallas kernels, prepared(): pl.pallas_call(prepare_kernel, out_shape=(pltpu.VMEM((4, PACK, BLOCK), BF...  3.11 us
  transfers between devices with their start and end apart: 7, of which 3 were waited for; matrix products, arithmetic and copies ran while one was open for 1% of the time, Pallas kernels for 3%

profile of v3, /device:TPU:1, one launch (start us, length us, event | category | flops | bytes accessed | tf_op | source)
XLA Modules:
  0.0 123.3 jit_solution(7211316011613191811)
XLA Ops:
  6.5 0.0 copy-start
  6.5 0.0 all-gather.2.cloned.1.call-start
  6.5 3.1 %prepare.1 = (bf16[4,1408,128]{2,1,0:T(8,128)(2,1)}, bf16[136,768]{1,0:T(8,128)(2,1)}) custom-call(bf16[2048,128]{1,0:T(8,128)(2,1)} %w_hidden.1, bf16[128,768]{1,0:T(8,128)(2,1)} %w_embed.1, bf16[1,128,768]{2,1,0:T(8,128)(2,1)} %members.1, s32[1,128]{1,0:T(1,128)} %cluster.1, s32[1,128]{1,0:T(1,128)} %valid.1), custom_call_target="tpu_custom_call" | custom-call | tf_op jit(solution)/shard_map/prepare/pallas_call | solution.py:224
  9.7 0.0 all-gather.2.cloned.1.call-update
  9.7 0.0 copy-start.4
  9.7 5.2 %all-to-all-start = ((bf16[4,1408,128]{2,1,0:T(8,128)(2,1)}), bf16[4,1408,128]{2,1,0:T(8,128)(2,1)S(1)}, u32[]{:S(2)}, u32[]{:S(2)}) async-start(bf16[4,1408,128]{2,1,0:T(8,128)(2,1)} %get-tuple-element.18), calls=%async_computation | async-start | bytes 2883584 | tf_op jit(solution)/shard_map/all_to_all | solution.py:281
  14.8 0.0 copy-done.4
  14.9 3.1 %collective-permute-start = (bf16[80,2048]{1,0:T(8,128)(2,1)S(1)}, bf16[80,2048]{1,0:T(8,128)(2,1)S(1)}, u32[]{:S(2)}, u32[]{:S(2)}) collective-permute-start(bf16[80,2048]{1,0:T(8,128)(2,1)S(1)} %copy-done.4), channel_id=1, source_target_pairs={{0,1},{1,2},{2,3},{3,0},{4,5},{5,6},{6,7},{7,4},{8,9},{9,10},{10,1... | collective-permute-start | bytes 983048 | tf_op jit(solution)/shard_map/ppermute | solution.py:216
  18.0 3.4 %collective-permute-start.1 = (bf16[80,2048]{1,0:T(8,128)(2,1)S(1)}, bf16[80,2048]{1,0:T(8,128)(2,1)S(1)}, u32[]{:S(2)}, u32[]{:S(2)}) collective-permute-start(bf16[80,2048]{1,0:T(8,128)(2,1)S(1)} %copy-done.4), channel_id=1, source_target_pairs={{0,3},{1,0},{2,1},{3,2},{4,7},{5,4},{6,5},{7,6},{8,11},{9,8},{10,9... | collective-permute-start | bytes 983048 | tf_op jit(solution)/shard_map/ppermute | solution.py:216
  21.4 0.0 copy-done
  21.4 0.1 dynamic-slice_bitcast_fusion
  21.4 2.4 %collective-permute-done.left = bf16[80,2048]{1,0:T(8,128)(2,1)S(1)} collective-permute-done((bf16[80,2048]{1,0:T(8,128)(2,1)S(1)}, bf16[80,2048]{1,0:T(8,128)(2,1)S(1)}, u32[]{:S(2)}, u32[]{:S(2)}) %collective-permute-start) | collective-permute-done | bytes 327712 | tf_op jit(solution)/shard_map/ppermute | solution.py:216
  23.9 0.0 copy-start.2
  23.9 3.4 %collective-permute-start.2 = (bf16[48,2048]{1,0:T(8,128)(2,1)S(1)}, bf16[48,2048]{1,0:T(8,128)(2,1)S(1)}, u32[]{:S(2)}, u32[]{:S(2)}) collective-permute-start(bf16[48,2048]{1,0:T(8,128)(2,1)S(1)} %slice.8), channel_id=1, source_target_pairs={{0,1},{1,2},{2,3},{3,0},{4,5},{5,6},{6,7},{7,4},{8,9},{9,10},{10,1... | collective-permute-start | bytes 589832 | tf_op jit(solution)/shard_map/ppermute | solution.py:216
  27.3 0.0 collective-permute-done.1.right
  27.3 0.0 copy-start.3
  27.3 4.2 %collective-permute-start.3 = (bf16[32,2048]{1,0:T(8,128)(2,1)S(1)}, bf16[32,2048]{1,0:T(8,128)(2,1)S(1)}, u32[]{:S(2)}, u32[]{:S(2)}) collective-permute-start(bf16[32,2048]{1,0:T(8,128)(2,1)S(1)} %slice.9), channel_id=1, source_target_pairs={{0,3},{1,0},{2,1},{3,2},{4,7},{5,4},{6,5},{7,6},{8,11},{9,8},{10,9... | collective-permute-start | bytes 393224 | tf_op jit(solution)/shard_map/ppermute | solution.py:216
  31.5 0.8 constant_dynamic-slice_fusion
  32.3 0.1 copy.15.local_col
  32.4 0.1 copy.17.owner_col
  32.5 0.8 fusion.owner_row
  33.2 0.4 slots.1
  33.7 0.4 collective-permute-done.3.far_b
  34.1 0.0 copy-start.6
  34.1 0.0 collective-permute-done.2.far_a
  34.1 0.0 copy-start.5
  34.1 0.0 all-to-all-done.mine
  34.1 8.8 %collective-permute-start.4 = (bf16[4,1408,128]{2,1,0:T(8,128)(2,1)S(1)}, bf16[4,1408,128]{2,1,0:T(8,128)(2,1)S(1)}, u32[]{:S(2)}, u32[]{:S(2)}) collective-permute-start(bf16[4,1408,128]{2,1,0:T(8,128)(2,1)S(1)} %all-to-all-done.mine), channel_id=1, source_target_pairs={{0,16},{16,0},{1,17},{17,1},{2,18},{18,2},{3,19},{19,3},{4,20},{20... | collective-permute-start | bytes 4325384 | tf_op jit(solution)/shard_map/ppermute | solution.py:274
  42.9 0.0 copy-done.2
  42.9 0.0 copy-done.3
  42.9 0.0 copy-done.6
  42.9 0.0 copy-done.5
  42.9 1.8 %first.1 = (f32[320,512]{1,0:T(8,128)S(1)}, bf16[320,1024]{1,0:T(8,128)(2,1)S(1)}) custom-call(bf16[80,2048]{1,0:T(8,128)(2,1)} %own.1, bf16[80,2048]{1,0:T(8,128)(2,1)} %copy-done.2, bf16[80,2048]{1,0:T(8,128)(2,1)} %copy-done.3, bf16[48,2048]{1,0:T(8,128)(2,1)} %copy-done.5, bf16[32,2048]{1,0:T(8,128)(2,1)} %copy-done.6, ...), custom_call_target="tpu_custom_call" | custom-call | tf_op jit(solution)/shard_map/first/pallas_call | solution.py:254
  44.8 1.0 collective-permute-done.4.other
  45.7 1.0 head.1
  46.7 0.0 copy-start.1
  46.8 13.0 %all_to_all.26.partial = bf16[4,80,768]{2,1,0:T(8,128)(2,1)S(1)} all-to-all(bf16[4,80,768]{2,1,0:T(8,128)(2,1)S(1)} %head.1), channel_id=1, replica_groups=mesh['z'=16,'core'=2,'y'=4,'x'=4] {'x'}, dimensions={0} | all-to-all | bytes 983040 | tf_op jit(solution)/shard_map/all_to_all | solution.py:304
  59.8 0.6 query.1
  60.4 36.5 %all_to_all.27.arrived = bf16[32,16,256]{2,1,0:T(8,128)(2,1)S(1)} all-to-all(bf16[32,16,256]{2,1,0:T(8,128)(2,1)S(1)} %query.1), channel_id=1, replica_groups=mesh['z'=16,'core'=2,'y'=4,'x'=4] {'z','core'}, dimensions={0} | all-to-all | bytes 524288 | tf_op jit(solution)/shard_map/all_to_all | solution.py:308
  96.9 0.0 all-gather.2.cloned.1.call-done.units
  96.9 0.0 copy-done.1
  96.9 3.5 %score.1 = f32[32,128]{1,0:T(8,128)S(1)} custom-call(bf16[32,16,256]{2,1,0:T(8,128)(2,1)S(1)} %all_to_all.27.arrived, bf16[640,512]{1,0:T(8,128)(2,1)S(1)} %copy-done.1, bf16[2176,768]{1,0:T(8,128)(2,1)} %all-gather.2.cloned.1.call-done.units), custom_call_target="tpu_custom_call" | custom-call | tf_op jit(solution)/shard_map/score/pallas_call | solution.py:242
  100.4 15.5 %all_to_all.28 = f32[32,1,128]{2,1,0:T(1,128)S(1)} all-to-all(f32[32,1,128]{2,1,0:T(1,128)S(1)} %bitcast.10), channel_id=1, replica_groups=mesh['z'=16,'core'=2,'y'=4,'x'=4] {'z','core'}, dimensions={0} | all-to-all | bytes 32768 | tf_op jit(solution)/shard_map/all_to_all | solution.py:310
  115.9 0.6 answer.1
  (2 shorter events, 0.0 us)
Async XLA Ops:
  6.5 14.8 %copy-start = (s32[1280]{0:T(1024)S(1)}, s32[1280]{0:T(1024)}, u32[]{:S(2)}) copy-start(s32[1280]{0:T(1024)} %param.14) | copy-start | bytes 15364
  6.5 90.4 %all-gather.2.cloned.1.call-start = ((), (), s32[]{:S(2)}) async-start(), calls=%async_computation.4 | async-start | bytes 3551232 | tf_op jit(solution)/shard_map/all_gather | solution.py:280
  9.7 5.2 %copy-start.4 = (bf16[80,2048]{1,0:T(8,128)(2,1)S(1)}, bf16[80,2048]{1,0:T(8,128)(2,1)}, u32[]{:S(2)}) copy-start(bf16[80,2048]{1,0:T(8,128)(2,1)} %own.1) | copy-start | bytes 983044
  9.7 24.4 %all-to-all-start = ((bf16[4,1408,128]{2,1,0:T(8,128)(2,1)}), bf16[4,1408,128]{2,1,0:T(8,128)(2,1)S(1)}, u32[]{:S(2)}, u32[]{:S(2)}) async-start(bf16[4,1408,128]{2,1,0:T(8,128)(2,1)} %get-tuple-element.18), calls=%async_computation | async-start | bytes 2883584 | tf_op jit(solution)/shard_map/all_to_all | solution.py:281
  14.9 9.0 %collective-permute-start = (bf16[80,2048]{1,0:T(8,128)(2,1)S(1)}, bf16[80,2048]{1,0:T(8,128)(2,1)S(1)}, u32[]{:S(2)}, u32[]{:S(2)}) collective-permute-start(bf16[80,2048]{1,0:T(8,128)(2,1)S(1)} %copy-done.4), channel_id=1, source_target_pairs={{0,1},{1,2},{2,3},{3,0},{4,5},{5,6},{6,7},{7,4},{8,9},{9,10},{10,1... | collective-permute-start | bytes 983048 | tf_op jit(solution)/shard_map/ppermute | solution.py:216
  18.0 9.3 %collective-permute-start.1 = (bf16[80,2048]{1,0:T(8,128)(2,1)S(1)}, bf16[80,2048]{1,0:T(8,128)(2,1)S(1)}, u32[]{:S(2)}, u32[]{:S(2)}) collective-permute-start(bf16[80,2048]{1,0:T(8,128)(2,1)S(1)} %copy-done.4), channel_id=1, source_target_pairs={{0,3},{1,0},{2,1},{3,2},{4,7},{5,4},{6,5},{7,6},{8,11},{9,8},{10,9... | collective-permute-start | bytes 983048 | tf_op jit(solution)/shard_map/ppermute | solution.py:216
  23.9 19.0 %copy-start.2 = (bf16[80,2048]{1,0:T(8,128)(2,1)}, bf16[80,2048]{1,0:T(8,128)(2,1)S(1)}, u32[]{:S(2)}) copy-start(bf16[80,2048]{1,0:T(8,128)(2,1)S(1)} %collective-permute-done.left) | copy-start | bytes 983044
  23.9 10.2 %collective-permute-start.2 = (bf16[48,2048]{1,0:T(8,128)(2,1)S(1)}, bf16[48,2048]{1,0:T(8,128)(2,1)S(1)}, u32[]{:S(2)}, u32[]{:S(2)}) collective-permute-start(bf16[48,2048]{1,0:T(8,128)(2,1)S(1)} %slice.8), channel_id=1, source_target_pairs={{0,1},{1,2},{2,3},{3,0},{4,5},{5,6},{6,7},{7,4},{8,9},{9,10},{10,1... | collective-permute-start | bytes 589832 | tf_op jit(solution)/shard_map/ppermute | solution.py:216
  27.3 15.6 %copy-start.3 = (bf16[80,2048]{1,0:T(8,128)(2,1)}, bf16[80,2048]{1,0:T(8,128)(2,1)S(1)}, u32[]{:S(2)}) copy-start(bf16[80,2048]{1,0:T(8,128)(2,1)S(1)} %collective-permute-done.1.right) | copy-start | bytes 983044
  27.3 6.8 %collective-permute-start.3 = (bf16[32,2048]{1,0:T(8,128)(2,1)S(1)}, bf16[32,2048]{1,0:T(8,128)(2,1)S(1)}, u32[]{:S(2)}, u32[]{:S(2)}) collective-permute-start(bf16[32,2048]{1,0:T(8,128)(2,1)S(1)} %slice.9), channel_id=1, source_target_pairs={{0,3},{1,0},{2,1},{3,2},{4,7},{5,4},{6,5},{7,6},{8,11},{9,8},{10,9... | collective-permute-start | bytes 393224 | tf_op jit(solution)/shard_map/ppermute | solution.py:216
  34.1 8.8 %copy-start.6 = (bf16[32,2048]{1,0:T(8,128)(2,1)}, bf16[32,2048]{1,0:T(8,128)(2,1)S(1)}, u32[]{:S(2)}) copy-start(bf16[32,2048]{1,0:T(8,128)(2,1)S(1)} %collective-permute-done.3.far_b) | copy-start | bytes 393220
  34.1 8.8 %copy-start.5 = (bf16[48,2048]{1,0:T(8,128)(2,1)}, bf16[48,2048]{1,0:T(8,128)(2,1)S(1)}, u32[]{:S(2)}) copy-start(bf16[48,2048]{1,0:T(8,128)(2,1)S(1)} %collective-permute-done.2.far_a) | copy-start | bytes 589828
  34.1 11.6 %collective-permute-start.4 = (bf16[4,1408,128]{2,1,0:T(8,128)(2,1)S(1)}, bf16[4,1408,128]{2,1,0:T(8,128)(2,1)S(1)}, u32[]{:S(2)}, u32[]{:S(2)}) collective-permute-start(bf16[4,1408,128]{2,1,0:T(8,128)(2,1)S(1)} %all-to-all-done.mine), channel_id=1, source_target_pairs={{0,16},{16,0},{1,17},{17,1},{2,18},{18,2},{3,19},{19,3},{4,20},{20... | collective-permute-start | bytes 4325384 | tf_op jit(solution)/shard_map/ppermute | solution.py:274
  46.7 50.2 %copy-start.1 = (bf16[640,512]{1,0:T(8,128)(2,1)S(1)}, bf16[640,512]{1,0:T(8,128)(2,1)}, u32[]{:S(2)}) copy-start(bf16[640,512]{1,0:T(8,128)(2,1)} %constant.18.clone.pick) | copy-start | bytes 1966084
Sparse Core Ops, SparseCore 0:
  10.4 69.5 all-gather.1

commit v4 on v3

--- a/solution.py
+++ b/solution.py
@@ -12,8 +12,7 @@
 PACK = HALF + 3 * BLOCK
 CHUNK = 256
 LINES = 16
-UNIT = SLOTS + 8
-PARTS = 4
+UNIT = SLOTS + 16
 F32, BF16, I32 = jnp.float32, jnp.bfloat16, jnp.int32
 PARAMS = pltpu.CompilerParams(vmem_limit_bytes=16 << 20)
 
@@ -40,7 +39,7 @@
 
 
 def prepare_kernel(
-    w_hidden, w_embed, members, cluster, valid, half, unit, held, slots, live, sem, sems
+    w_hidden, w_embed, members, cluster, valid, half, unit, held, slots, live, upper, lower, sem, sems
 ):
     c = lax.axis_index("core")
     first = [
@@ -48,23 +47,14 @@
         pltpu.make_async_copy(cluster, slots, sem.at[1]),
         pltpu.make_async_copy(valid, live, sem.at[2]),
     ]
-    rest = []
-    for j in range(4):
-        rest.append(
-            pltpu.make_async_copy(
-                w_hidden.at[pl.ds(pl.multiple_of(c * HALF, HALF), HALF), :],
-                half.at[j, 0:HALF, :],
-                sems.at[j, 3],
-            )
-        )
-        for i in range(3):
-            rest.append(
-                pltpu.make_async_copy(
-                    w_embed.at[:, pl.ds(pl.multiple_of((3 * c + i) * BLOCK, BLOCK), BLOCK)],
-                    half.at[j, HALF + i * BLOCK : HALF + (i + 1) * BLOCK, :],
-                    sems.at[j, i],
-                )
-            )
+    rest = [
+        pltpu.make_async_copy(
+            w_hidden.at[pl.ds(pl.multiple_of(c * HALF, HALF), HALF), :], upper, sems.at[0]
+        ),
+        pltpu.make_async_copy(
+            w_embed.at[:, pl.ds(pl.multiple_of(c * 3 * BLOCK, BLOCK), 3 * BLOCK)], lower, sems.at[1]
+        ),
+    ]
     for copy in first + rest:
         copy.start()
     for copy in first:
@@ -74,24 +64,24 @@
     unit[0:SLOTS, :] = (values * (1.0 / jnp.sqrt(norm + EPS))).astype(BF16)
     tag = jnp.where(live[...] == 1, slots[...] + 1, 0).astype(F32)
     tag = jnp.concatenate([tag] * (EMB // SLOTS), axis=1)
-    unit[SLOTS:UNIT, :] = jnp.broadcast_to(tag, (8, EMB)).astype(BF16)
+    unit[SLOTS:UNIT, :] = jnp.broadcast_to(tag, (UNIT - SLOTS, EMB)).astype(BF16)
     for copy in rest:
         copy.wait()
-
-
-def slots_kernel(owner_row, owner_col, local_col, place, tags, rank_row):
+    for j in range(4):
+        half[j, 0:HALF, :] = upper[...]
+        for i in range(3):
+            half[j, HALF + i * BLOCK : HALF + (i + 1) * BLOCK, :] = lower[
+                :, i * BLOCK : (i + 1) * BLOCK
+            ]
+
+
+def slots_kernel(owner_row, owner_col, local_col, tags, rank_row):
     row, col = owner_row[...], owner_col[...]
     same = row == col
     up, across = iota((ROWS, ROWS), 0), iota((ROWS, ROWS), 1)
     ranks = jnp.sum(jnp.where(same & (up < across), 1, 0), axis=0, keepdims=True)
     ranks_col = jnp.sum(jnp.where(same & (across < up), 1, 0), axis=1, keepdims=True)
     rank_row[...] = ranks
-    line = iota((OWNERS * LINES, ROWS), 0)
-    mine = row == line // LINES
-    inner = line % LINES
-    parts = [mine & (inner == k * CAP + ranks) for k in range(3)] + [mine & (inner == LINES - 1)]
-    for k in range(4):
-        place[k] = jnp.where(parts[k], 1.0, 0.0).astype(BF16)
     lane = iota((ROWS, CHUNK), 1)
     tags[...] = jnp.where(lane == ranks_col, local_col[...] + 1, 0).astype(F32).astype(BF16)
 
@@ -129,7 +119,13 @@
             out[lax.rem(x + step, 4), :, cut] = total[j * ROWS : (j + 1) * ROWS].astype(BF16)
 
 
-def query_kernel(partial, place, tags, out):
+def query_kernel(partial, owner_row, rank_row, tags, out):
+    line = iota((OWNERS * LINES, ROWS), 0)
+    inner = jnp.where(owner_row[...] == line // LINES, line % LINES, -1)
+    place = [
+        jnp.where(inner == (k * CAP + rank_row[...] if k < 3 else LINES - 1), 1.0, 0.0).astype(BF16)
+        for k in range(4)
+    ]
     proj = partial[0].astype(F32)
     for j in range(1, 4):
         proj = proj + partial[j].astype(F32)
@@ -148,18 +144,26 @@
     out[...] = total.astype(BF16).reshape(OWNERS, LINES, CHUNK)
 
 
-def score_kernel(arrived, pick, units, out, held, sem):
-    rows = 16 * UNIT // PARTS
+def column_kernel(own, left, right, far, out):
+    for i, part in enumerate((own, left, right, far)):
+        out[i * UNIT : (i + 1) * UNIT, :] = part[...]
+
+
+def score_kernel(arrived, own, left, right, top, bottom, out, held, sem):
     copies = [
-        pltpu.make_async_copy(
-            units.at[i * rows : (i + 1) * rows, :], held.at[i * rows : (i + 1) * rows, :], sem.at[i]
-        )
-        for i in range(PARTS)
+        pltpu.make_async_copy(top, held.at[0 : 2 * UNIT, :], sem.at[0]),
+        pltpu.make_async_copy(bottom, held.at[2 * UNIT :, :], sem.at[1]),
     ]
     for copy in copies:
         copy.start()
+    parts = (own, left, right, held)
+    row = iota((4 * OWNERS * CAP, 1), 0)
+    kind, slot = row // (OWNERS * CAP), row % (OWNERS * CAP)
+    line = jnp.where(kind < 3, kind * CAP + slot // OWNERS, LINES - 1)
+    target = slot % OWNERS * LINES + line
+    pick = jnp.where(iota((4 * OWNERS * CAP, OWNERS * LINES), 1) == target, 1.0, 0.0).astype(BF16)
     flat = arrived[...].reshape(OWNERS * LINES, CHUNK)
-    moved = jnp.dot(pick[...], flat, preferred_element_type=F32)
+    moved = jnp.dot(pick, flat, preferred_element_type=F32)
     count = OWNERS * CAP
     query = jnp.concatenate(
         [moved[k * count : (k + 1) * count].astype(BF16) for k in range(3)], axis=1
@@ -169,13 +173,15 @@
         jnp.where(iota((count, CHUNK), 1) == slot, moved[3 * count :], 0.0), axis=1, keepdims=True
     )
     best = jnp.full((count, 2 * SLOTS), -1.0, F32)
+    where = [(part, i * UNIT) for part in parts for i in range(part.shape[0] // UNIT)]
     for j in range(0, 16, 2):
-        if j % (16 // PARTS) == 0:
-            copies[j // (16 // PARTS)].wait()
+        if j == 12:
+            for copy in copies:
+                copy.wait()
         blocks, marks = [], []
-        for i in (j, j + 1):
-            blocks.append(held[i * UNIT : i * UNIT + SLOTS, :])
-            marks.append(held[i * UNIT + SLOTS : (i + 1) * UNIT, 0:SLOTS].astype(F32)[0:1])
+        for part, row in where[j : j + 2]:
+            blocks.append(part[row : row + SLOTS, :])
+            marks.append(part[row + SLOTS : row + UNIT, 0:SLOTS].astype(F32)[0:1])
         scores = lax.dot_general(
             query,
             jnp.concatenate(blocks, axis=0),
@@ -192,17 +198,6 @@
     out[...] = result
 
 
-def picking():
-    count = OWNERS * CAP
-    pick = np.zeros((4 * count, OWNERS * LINES), np.float32)
-    for s in range(CAP):
-        for o in range(OWNERS):
-            for k in range(3):
-                pick[k * count + s * OWNERS + o, o * LINES + k * CAP + s] = 1
-            pick[3 * count + s * OWNERS + o, o * LINES + LINES - 1] = 1
-    return jnp.asarray(pick, BF16)
-
-
 def answer_kernel(answers, owner_row, rank_row, out):
     mine = owner_row[...] == iota((OWNERS, ROWS), 0)
     total = jnp.zeros((1, ROWS), F32)
@@ -214,6 +209,20 @@
 
 def shift(value, axis, step):
     return lax.ppermute(value, axis, [(i, (i + step) % 4) for i in range(4)])
+
+
+def turn(value, step, turned):
+    pairs = []
+    for c in range(2):
+        for y in range(4):
+            for x in range(4):
+                to = (y, (x + step) % 4) if (c == 1) == turned else ((y + step) % 4, x)
+                pairs.append((c * 16 + y * 4 + x, c * 16 + to[0] * 4 + to[1]))
+    return lax.ppermute(value, ("core", "y", "x"), pairs)
+
+
+def gather(value, turned):
+    return [value] + [turn(value, step, turned) for step in (1, -1, 2)]
 
 
 HBM = pl.BlockSpec(memory_space=pltpu.HBM)
@@ -230,24 +239,14 @@
             pltpu.VMEM((SLOTS, EMB), BF16),
             pltpu.VMEM((1, SLOTS), I32),
             pltpu.VMEM((1, SLOTS), I32),
+            pltpu.VMEM((HALF, BLOCK), BF16),
+            pltpu.VMEM((BLOCK, 3 * BLOCK), BF16),
             pltpu.SemaphoreType.DMA((3,)),
-            pltpu.SemaphoreType.DMA((4, 4)),
+            pltpu.SemaphoreType.DMA((2,)),
         ],
         name="prepare",
         compiler_params=PARAMS,
     )(*arrays)
-
-
-def score(arrived, pick, units):
-    return pl.pallas_call(
-        score_kernel,
-        out_shape=sds((OWNERS, SLOTS), F32),
-        in_specs=[VMEM, VMEM, HBM],
-        out_specs=VMEM,
-        scratch_shapes=[pltpu.VMEM((16 * UNIT, EMB), BF16), pltpu.SemaphoreType.DMA((PARTS,))],
-        name="score",
-        compiler_params=PARAMS,
-    )(arrived, pick, units)
 
 
 def first(*arrays):
@@ -266,6 +265,18 @@
     return pltpu.with_memory_space_constraint(value, pltpu.VMEM)
 
 
+def score(*arrays):
+    return pl.pallas_call(
+        score_kernel,
+        out_shape=sds((OWNERS, SLOTS), F32),
+        in_specs=[VMEM] * 4 + [HBM] * 2,
+        out_specs=VMEM,
+        scratch_shapes=[pltpu.VMEM((4 * UNIT, EMB), BF16), pltpu.SemaphoreType.DMA((2,))],
+        name="score",
+        compiler_params=PARAMS,
+    )(*arrays)
+
+
 def stay(value):
     return pltpu.with_memory_space_constraint(value, pltpu.HBM)
 
@@ -277,36 +288,39 @@
 def body(features, w_hidden, w_embed, members, doc_owner, doc_local, member_cluster, member_valid):
     dp = ("z", "core")
     half, unit = prepared(*map(stay, (w_hidden, w_embed, members, member_cluster, member_valid)))
-    units = lax.all_gather(unit, ("y", "x"), axis=0, tiled=True)
+    units = gather(unit, False)
     mine = lax.all_to_all(near(half), "y", 0, 0, tiled=True)
-    left, right = shift(features, "x", 1), shift(features, "x", -1)
+    docs = [shift(features, "x", 1), shift(features, "x", -1)]
     cut = 48
-    docs = [left, right, shift(left[:cut], "x", 1), shift(right[cut:], "x", -1)]
+    docs += [shift(docs[0][:cut], "x", 1), shift(docs[1][cut:], "x", -1)]
 
     start = lax.axis_index(("y", "x")) * ROWS
     owner = lax.dynamic_slice_in_dim(doc_owner[:, 0], start, ROWS, 0)
     local = lax.dynamic_slice_in_dim(doc_local, start, ROWS, 0)
     owner_row = owner.reshape(1, ROWS)
-    place, tags, rank_row = call(
+    tags, rank_row = call(
         slots_kernel,
         (
-            pltpu.VMEM((4, OWNERS * LINES, ROWS), BF16),
-            pltpu.VMEM((ROWS, CHUNK), BF16),
+            sds((ROWS, CHUNK), BF16),
             sds((1, ROWS), I32),
         ),
         "slots",
     )(owner_row, owner.reshape(ROWS, 1), local.reshape(ROWS, 1))
 
-    mine, place, *docs = lax.optimization_barrier((mine, place, *docs))
+    mine, tags, docs, units[1:] = lax.optimization_barrier((mine, tags, docs, units[1:]))
     other = swap(mine)
+    column = call(column_kernel, sds((4 * UNIT, EMB), BF16), "column")(*map(near, units))
+    left, right = turn(column, 1, True), turn(column, -1, True)
+    top, bottom = turn(left[: 2 * UNIT], 1, True), turn(right[2 * UNIT :], -1, True)
+    columns = [column, left, right, top, bottom]
     pre, rest = first(*map(stay, (features, *docs)), mine)
     partial = call(head_kernel, sds((4, ROWS, EMB), BF16), "head")(near(pre), near(rest), mine, other)
     partial = lax.all_to_all(partial, "x", 0, 0, tiled=True)
     outgoing = call(query_kernel, sds((OWNERS, LINES, CHUNK), BF16), "query")(
-        partial, near(place), near(tags)
+        partial, owner_row, rank_row, tags
     )
     arrived = lax.all_to_all(outgoing, dp, 0, 0, tiled=True)
-    best = score(arrived, picking(), stay(units))
+    best = score(arrived, *map(near, columns[:3]), *map(stay, columns[3:]))
     answers = lax.all_to_all(best, dp, 0, 0, tiled=True)
     result = call(answer_kernel, sds((1, ROWS), F32), "answer")(answers, owner_row, rank_row)
     return result.reshape(ROWS)

time: 124 us -> 117 us (0.944)
  blocking collectives: 65.1 us -> 16.1 us
  starting transfers between devices: 28 us -> 65.9 us
  waiting for transfers between devices: 3.81 us -> 20.2 us
  between operations: 13.6 us -> 0.28 us
  local copies, waits for them, and re-layouts: 1.85 us -> 3.38 us
    all_to_all x2 -> x0, blocking collectives: 49.6 us -> none  [the longest x1 36.5 us: body(): arrived = lax.all_to_all(outgoing, dp, 0, 0, tiled=True)]
    ppermute x0 -> x7, starting transfers between devices: none -> 23.2 us  [turn(): return lax.ppermute(value, ('core', 'y', 'x'), pairs)]
    all_to_all x0 -> x2, starting transfers between devices: none -> 18 us  [the longest x1 14 us: body(): arrived = lax.all_to_all(outgoing, dp, 0, 0, tiled=True)]
    all_to_all x0 -> x2, waiting for transfers between devices: none -> 12.1 us  [the longest x1 10.2 us: body(): arrived = lax.all_to_all(outgoing, dp, 0, 0, tiled=True)]
    ppermute x0 -> x7, waiting for transfers between devices: none -> 4.47 us  [turn(): return lax.ppermute(value, ('core', 'y', 'x'), pairs)]
    ppermute x1, starting transfers between devices: 8.77 us -> 6.63 us  [swap(): return lax.ppermute(value, 'core', [(0, 1), (1, 0)])]
    pallas_call x1, Pallas kernels: 3.46 us -> 2.11 us  [score(): pl.pallas_call(score_kernel, out_shape=sds((OWNERS, SLOTS), F32), in_spec...]
    pallas_call x4 -> x5, Pallas kernels: 2.65 us -> 3.99 us  [run(): pl.pallas_call(body, out_shape=out, in_specs=specs, out_specs=outs, name=...]
  transfers between devices with their start and end apart: 7 -> 15, of which waited for: 3 -> 7; matrix products, arithmetic and copies ran while one was open for 1% -> 2% of each run, Pallas kernels for 3% -> 3%
where the time goes in v4:
time: 117 us; the launch traced here: 116 us
  starting transfers between devices  65.9 us (56%)
  waiting for transfers between devices  20.2 us (17%)
  blocking collectives  16.1 us (14%)
  Pallas kernels  10.4 us (9%)
  local copies, waits for them, and re-layouts  3.38 us (3%)
    ppermute x7, starting transfers between devices, turn(): return lax.ppermute(value, ('core', 'y', 'x'), pairs)  23.2 us
    all_to_all x1, blocking collectives, body(): answers = lax.all_to_all(best, dp, 0, 0, tiled=True)  16.1 us
    all_to_all x1, starting transfers between devices, body(): arrived = lax.all_to_all(outgoing, dp, 0, 0, tiled=True)  14 us
    ppermute x4, starting transfers between devices, shift(): return lax.ppermute(value, axis, [(i, (i + step) % 4) for i in range(4)])  13 us
    all_to_all x1, waiting for transfers between devices, body(): arrived = lax.all_to_all(outgoing, dp, 0, 0, tiled=True)  10.2 us
    ppermute x1, starting transfers between devices, swap(): return lax.ppermute(value, 'core', [(0, 1), (1, 0)])  6.63 us
    all_to_all x1, starting transfers between devices, body(): mine = lax.all_to_all(near(half), 'y', 0, 0, tiled=True)  5.16 us
    ppermute x7, waiting for transfers between devices, turn(): return lax.ppermute(value, ('core', 'y', 'x'), pairs)  4.47 us
  transfers between devices with their start and end apart: 15, of which 7 were waited for; matrix products, arithmetic and copies ran while one was open for 2% of the time, Pallas kernels for 3%

profile of v4, /device:TPU:1, one launch (start us, length us, event | category | flops | bytes accessed | tf_op | source)
XLA Modules:
  0.0 116.2 jit_solution(14175446571815714875)
XLA Ops:
  0.0 0.0 copy-start
  0.0 2.5 %prepare.1 = (bf16[4,1408,128]{2,1,0:T(8,128)(2,1)}, bf16[144,768]{1,0:T(8,128)(2,1)S(1)}) custom-call(bf16[2048,128]{1,0:T(8,128)(2,1)} %w_hidden.1, bf16[128,768]{1,0:T(8,128)(2,1)} %w_embed.1, bf16[1,128,768]{2,1,0:T(8,128)(2,1)} %members.1, s32[1,128]{1,0:T(1,128)} %cluster.1, s32[1,128]{1,0:T(1,128)} %valid.1), custom_call_target="tpu_custom_call" | custom-call | tf_op jit(solution)/shard_map/prepare/pallas_call | solution.py:233
  2.5 0.0 copy-start.4
  2.5 5.2 %all-to-all-start = ((bf16[4,1408,128]{2,1,0:T(8,128)(2,1)}), bf16[4,1408,128]{2,1,0:T(8,128)(2,1)S(1)}, u32[]{:S(2)}, u32[]{:S(2)}) async-start(bf16[4,1408,128]{2,1,0:T(8,128)(2,1)} %get-tuple-element.20), calls=%async_computation | async-start | bytes 2883584 | tf_op jit(solution)/shard_map/all_to_all | solution.py:292
  7.6 3.1 %collective-permute-start = (bf16[80,2048]{1,0:T(8,128)(2,1)S(1)}, bf16[80,2048]{1,0:T(8,128)(2,1)S(1)}, u32[]{:S(2)}, u32[]{:S(2)}) collective-permute-start(bf16[80,2048]{1,0:T(8,128)(2,1)S(1)} %copy-done.4), channel_id=1, source_target_pairs={{0,1},{1,2},{2,3},{3,0},{4,5},{5,6},{6,7},{7,4},{8,9},{9,10},{10,1... | collective-permute-start | bytes 983048 | tf_op jit(solution)/shard_map/ppermute | solution.py:211
  10.8 3.4 %collective-permute-start.1 = (bf16[80,2048]{1,0:T(8,128)(2,1)S(1)}, bf16[80,2048]{1,0:T(8,128)(2,1)S(1)}, u32[]{:S(2)}, u32[]{:S(2)}) collective-permute-start(bf16[80,2048]{1,0:T(8,128)(2,1)S(1)} %copy-done.4), channel_id=1, source_target_pairs={{0,3},{1,0},{2,1},{3,2},{4,7},{5,4},{6,5},{7,6},{8,11},{9,8},{10,9... | collective-permute-start | bytes 983048 | tf_op jit(solution)/shard_map/ppermute | solution.py:211
  14.1 3.4 %collective-permute-start.4 = (bf16[144,768]{1,0:T(8,128)(2,1)S(1)}, bf16[144,768]{1,0:T(8,128)(2,1)S(1)}, u32[]{:S(2)}, u32[]{:S(2)}) collective-permute-start(bf16[144,768]{1,0:T(8,128)(2,1)S(1)} %get-tuple-element.22.own), channel_id=1, source_target_pairs={{0,1},{1,2},{2,3},{3,0},{4,5},{5,6},{6,7},{7,4},{8,9},{9,10},{10,1... | collective-permute-start | bytes 663560 | tf_op jit(solution)/shard_map/ppermute | solution.py:221
  17.5 3.1 %collective-permute-start.5 = (bf16[144,768]{1,0:T(8,128)(2,1)S(1)}, bf16[144,768]{1,0:T(8,128)(2,1)S(1)}, u32[]{:S(2)}, u32[]{:S(2)}) collective-permute-start(bf16[144,768]{1,0:T(8,128)(2,1)S(1)} %get-tuple-element.22.own), channel_id=1, source_target_pairs={{0,3},{1,0},{2,1},{3,2},{4,7},{5,4},{6,5},{7,6},{8,11},{9,8},{10,9... | collective-permute-start | bytes 663560 | tf_op jit(solution)/shard_map/ppermute | solution.py:221
  20.7 3.7 %collective-permute-start.6 = (bf16[144,768]{1,0:T(8,128)(2,1)S(1)}, bf16[144,768]{1,0:T(8,128)(2,1)S(1)}, u32[]{:S(2)}, u32[]{:S(2)}) collective-permute-start(bf16[144,768]{1,0:T(8,128)(2,1)S(1)} %get-tuple-element.22.own), channel_id=1, source_target_pairs={{0,2},{1,3},{2,0},{3,1},{4,6},{5,7},{6,4},{7,5},{8,10},{9,11},{10,... | collective-permute-start | bytes 663560 | tf_op jit(solution)/shard_map/ppermute | solution.py:221
  24.3 0.8 constant_dynamic-slice_fusion
  25.1 0.0 collective-permute-done.left
  25.1 0.7 slice.16
  25.8 1.9 %collective-permute-start.2 = (bf16[48,2048]{1,0:T(8,128)(2,1)}, bf16[48,2048]{1,0:T(8,128)(2,1)}, u32[]{:S(2)}, u32[]{:S(2)}) collective-permute-start(bf16[48,2048]{1,0:T(8,128)(2,1)} %slice.16), channel_id=1, source_target_pairs={{0,1},{1,2},{2,3},{3,0},{4,5},{5,6},{6,7},{7,4},{8,9},{9,10},{10,1... | collective-permute-start | bytes 589832 | tf_op jit(solution)/shard_map/ppermute | solution.py:211
  27.7 0.0 collective-permute-done.1.right
  27.8 4.6 %collective-permute-start.3 = (bf16[32,2048]{1,0:T(8,128)(2,1)S(1)}, bf16[32,2048]{1,0:T(8,128)(2,1)S(1)}, u32[]{:S(2)}, u32[]{:S(2)}) collective-permute-start(bf16[32,2048]{1,0:T(8,128)(2,1)S(1)} %slice.17), channel_id=1, source_target_pairs={{0,3},{1,0},{2,1},{3,2},{4,7},{5,4},{6,5},{7,6},{8,11},{9,8},{10,9... | collective-permute-start | bytes 393224 | tf_op jit(solution)/shard_map/ppermute | solution.py:211
  32.4 0.1 dynamic-slice_bitcast_fusion
  32.5 0.1 copy.16.owner_col
  32.6 0.1 copy.14.local_col
  32.7 0.8 fusion.owner_row
  33.4 0.2 slots.1
  33.6 0.0 collective-permute-done.4.left
  33.6 0.0 collective-permute-done.5.right
  33.6 0.0 collective-permute-done.6.far
  33.6 1.3 %collective-permute-done.3.far_b = bf16[32,2048]{1,0:T(8,128)(2,1)S(1)} collective-permute-done((bf16[32,2048]{1,0:T(8,128)(2,1)S(1)}, bf16[32,2048]{1,0:T(8,128)(2,1)S(1)}, u32[]{:S(2)}, u32[]{:S(2)}) %collective-permute-start.3) | collective-permute-done | bytes 131104 | tf_op jit(solution)/shard_map/ppermute | solution.py:211
  34.9 1.2 %collective-permute-done.2.far_a = bf16[48,2048]{1,0:T(8,128)(2,1)} collective-permute-done((bf16[48,2048]{1,0:T(8,128)(2,1)}, bf16[48,2048]{1,0:T(8,128)(2,1)}, u32[]{:S(2)}, u32[]{:S(2)}) %collective-permute-start.2) | collective-permute-done | bytes 196640 | tf_op jit(solution)/shard_map/ppermute | solution.py:211
  36.2 0.0 all-to-all-done.mine
  36.2 6.6 %collective-permute-start.7 = (bf16[4,1408,128]{2,1,0:T(8,128)(2,1)S(1)}, bf16[4,1408,128]{2,1,0:T(8,128)(2,1)S(1)}, u32[]{:S(2)}, u32[]{:S(2)}) collective-permute-start(bf16[4,1408,128]{2,1,0:T(8,128)(2,1)S(1)} %all-to-all-done.mine), channel_id=1, source_target_pairs={{0,16},{16,0},{1,17},{17,1},{2,18},{18,2},{3,19},{19,3},{4,20},{20... | collective-permute-start | bytes 4325384 | tf_op jit(solution)/shard_map/ppermute | solution.py:285
  42.9 1.8 %first.1 = (f32[320,512]{1,0:T(8,128)S(1)}, bf16[320,1024]{1,0:T(8,128)(2,1)S(1)}) custom-call(bf16[80,2048]{1,0:T(8,128)(2,1)} %own.1, bf16[80,2048]{1,0:T(8,128)(2,1)} %copy-done.1, bf16[80,2048]{1,0:T(8,128)(2,1)} %copy-done.2, bf16[48,2048]{1,0:T(8,128)(2,1)} %collective-permute-done.2.far_a, bf16[32,2048]{1,0:T(8,128)(2,1)} %copy-done.5, ...), custom_call_target="tpu_custom_call" | custom-call | tf_op jit(solution)/shard_map/first/pallas_call | solution.py:253
  44.7 1.0 collective-permute-done.7.other
  45.7 1.8 %head.1 = bf16[4,80,768]{2,1,0:T(8,128)(2,1)} custom-call(f32[320,512]{1,0:T(8,128)S(1)} %get-tuple-element.28.pre, bf16[320,1024]{1,0:T(8,128)(2,1)S(1)} %get-tuple-element.29.rest, bf16[4,1408,128]{2,1,0:T(8,128)(2,1)S(1)} %all-to-all-done.mine, bf16[4,1408,128]{2,1,0:T(8,128)(2,1)S(1)} %collective-permute-done.7.other), custom_call_target="tpu_custom_call" | custom-call | tf_op jit(solution)/shard_map/head/pallas_call | solution.py:34
  47.5 4.0 %all-to-all-start.1 = ((bf16[4,80,768]{2,1,0:T(8,128)(2,1)}), bf16[4,80,768]{2,1,0:T(8,128)(2,1)S(1)}, u32[]{:S(2)}, u32[]{:S(2)}) async-start(bf16[4,80,768]{2,1,0:T(8,128)(2,1)} %head.1), calls=%async_computation.1 | async-start | bytes 983040 | tf_op jit(solution)/shard_map/all_to_all | solution.py:318
  51.5 0.1 column.1.own
  51.5 3.4 %collective-permute-start.8 = (bf16[576,768]{1,0:T(8,128)(2,1)S(1)}, bf16[576,768]{1,0:T(8,128)(2,1)S(1)}, u32[]{:S(2)}, u32[]{:S(2)}) collective-permute-start(bf16[576,768]{1,0:T(8,128)(2,1)S(1)} %column.1.own), channel_id=1, source_target_pairs={{0,4},{1,5},{2,6},{3,7},{4,8},{5,9},{6,10},{7,11},{8,12},{9,13},{1... | collective-permute-start | bytes 2654216 | tf_op jit(solution)/shard_map/ppermute | solution.py:221
  54.9 3.1 %collective-permute-start.9 = (bf16[576,768]{1,0:T(8,128)(2,1)S(1)}, bf16[576,768]{1,0:T(8,128)(2,1)S(1)}, u32[]{:S(2)}, u32[]{:S(2)}) collective-permute-start(bf16[576,768]{1,0:T(8,128)(2,1)S(1)} %column.1.own), channel_id=1, source_target_pairs={{0,12},{1,13},{2,14},{3,15},{4,0},{5,1},{6,2},{7,3},{8,4},{9,5},{1... | collective-permute-start | bytes 2654216 | tf_op jit(solution)/shard_map/ppermute | solution.py:221
  58.1 2.0 %all-to-all-done.1.partial = bf16[4,80,768]{2,1,0:T(8,128)(2,1)S(1)} async-done(((bf16[4,80,768]{2,1,0:T(8,128)(2,1)}), bf16[4,80,768]{2,1,0:T(8,128)(2,1)S(1)}, u32[]{:S(2)}, u32[]{:S(2)}) %all-to-all-start.1) | async-done | bytes 491552 | tf_op jit(solution)/shard_map/all_to_all | solution.py:318
  60.1 1.3 %query.1 = bf16[32,16,256]{2,1,0:T(8,128)(2,1)} custom-call(bf16[4,80,768]{2,1,0:T(8,128)(2,1)S(1)} %all-to-all-done.1.partial, s32[1,80]{1,0:T(1,128)S(1)} %fusion.owner_row, s32[1,80]{1,0:T(1,128)S(1)} %get-tuple-element.30.rank_row, bf16[80,256]{1,0:T(8,128)(2,1)S(1)} %get-tuple-element.31.tags), custom_call_target="tpu_custom_call" | custom-call | tf_op jit(solution)/shard_map/query/pallas_call | solution.py:34
  61.4 14.0 %all-to-all-start.2 = ((bf16[32,16,256]{2,1,0:T(8,128)(2,1)}), bf16[32,16,256]{2,1,0:T(8,128)(2,1)S(1)}, u32[]{:S(2)}, u32[]{:S(2)}) async-start(bf16[32,16,256]{2,1,0:T(8,128)(2,1)} %query.1), calls=%async_computation.2 | async-start | bytes 524288 | tf_op jit(solution)/shard_map/all_to_all | solution.py:322
  75.3 0.0 collective-permute-done.8.left
  75.4 1.9 %collective-permute-start.10 = (bf16[288,768]{1,0:T(8,128)(2,1)S(1)}, bf16[288,768]{1,0:T(8,128)(2,1)S(1)}, u32[]{:S(2)}, u32[]{:S(2)}) collective-permute-start(bf16[288,768]{1,0:T(8,128)(2,1)S(1)} %slice.18), channel_id=1, source_target_pairs={{0,4},{1,5},{2,6},{3,7},{4,8},{5,9},{6,10},{7,11},{8,12},{9,13},{1... | collective-permute-start | bytes 1327112 | tf_op jit(solution)/shard_map/ppermute | solution.py:221
  77.3 0.0 collective-permute-done.9.right
  77.4 4.6 %collective-permute-start.11 = (bf16[288,768]{1,0:T(8,128)(2,1)S(1)}, bf16[288,768]{1,0:T(8,128)(2,1)}, u32[]{:S(2)}, u32[]{:S(2)}) collective-permute-start(bf16[288,768]{1,0:T(8,128)(2,1)S(1)} %slice.19), channel_id=1, source_target_pairs={{0,12},{1,13},{2,14},{3,15},{4,0},{5,1},{6,2},{7,3},{8,4},{9,5},{1... | collective-permute-start | bytes 1327112 | tf_op jit(solution)/shard_map/ppermute | solution.py:221
  82.0 4.0 %collective-permute-done.10.top = bf16[288,768]{1,0:T(8,128)(2,1)S(1)} collective-permute-done((bf16[288,768]{1,0:T(8,128)(2,1)S(1)}, bf16[288,768]{1,0:T(8,128)(2,1)S(1)}, u32[]{:S(2)}, u32[]{:S(2)}) %collective-permute-start.10) | collective-permute-done | bytes 442400 | tf_op jit(solution)/shard_map/ppermute | solution.py:221
  86.0 0.8 copy-done.3
  86.7 0.5 collective-permute-done.11.bottom
  87.2 10.2 %all-to-all-done.2.arrived = bf16[32,16,256]{2,1,0:T(8,128)(2,1)S(1)} async-done(((bf16[32,16,256]{2,1,0:T(8,128)(2,1)}), bf16[32,16,256]{2,1,0:T(8,128)(2,1)S(1)}, u32[]{:S(2)}, u32[]{:S(2)}) %all-to-all-start.2) | async-done | bytes 262176 | tf_op jit(solution)/shard_map/all_to_all | solution.py:322
  97.3 2.1 %score.1 = f32[32,128]{1,0:T(8,128)S(1)} custom-call(bf16[32,16,256]{2,1,0:T(8,128)(2,1)S(1)} %all-to-all-done.2.arrived, bf16[576,768]{1,0:T(8,128)(2,1)S(1)} %column.1.own, bf16[576,768]{1,0:T(8,128)(2,1)S(1)} %collective-permute-done.8.left, bf16[576,768]{1,0:T(8,128)(2,1)S(1)} %collective-permute-done.9.right, bf16[288,768]{1,0:T(8,128)(2,1)} %copy-done.3, ...), custom_call_target="tpu_custom_call" | custom-call | tf_op jit(solution)/shard_map/score/pallas_call | solution.py:269
  99.5 16.1 %all_to_all.26 = f32[32,1,128]{2,1,0:T(1,128)S(1)} all-to-all(f32[32,1,128]{2,1,0:T(1,128)S(1)} %bitcast.10), channel_id=1, replica_groups=mesh['z'=16,'core'=2,'y'=4,'x'=4] {'z','core'}, dimensions={0} | all-to-all | bytes 32768 | tf_op jit(solution)/shard_map/all_to_all | solution.py:324
  115.6 0.6 answer.1
  (12 shorter events, 0.1 us)
Async XLA Ops:
  0.0 32.4 %copy-start = (s32[1280]{0:T(1024)S(1)}, s32[1280]{0:T(1024)}, u32[]{:S(2)}) copy-start(s32[1280]{0:T(1024)} %param.13) | copy-start | bytes 15364
  2.5 5.2 %copy-start.4 = (bf16[80,2048]{1,0:T(8,128)(2,1)S(1)}, bf16[80,2048]{1,0:T(8,128)(2,1)}, u32[]{:S(2)}) copy-start(bf16[80,2048]{1,0:T(8,128)(2,1)} %own.1) | copy-start | bytes 983044
  2.5 33.7 %all-to-all-start = ((bf16[4,1408,128]{2,1,0:T(8,128)(2,1)}), bf16[4,1408,128]{2,1,0:T(8,128)(2,1)S(1)}, u32[]{:S(2)}, u32[]{:S(2)}) async-start(bf16[4,1408,128]{2,1,0:T(8,128)(2,1)} %get-tuple-element.20), calls=%async_computation | async-start | bytes 2883584 | tf_op jit(solution)/shard_map/all_to_all | solution.py:292
  7.6 17.4 %collective-permute-start = (bf16[80,2048]{1,0:T(8,128)(2,1)S(1)}, bf16[80,2048]{1,0:T(8,128)(2,1)S(1)}, u32[]{:S(2)}, u32[]{:S(2)}) collective-permute-start(bf16[80,2048]{1,0:T(8,128)(2,1)S(1)} %copy-done.4), channel_id=1, source_target_pairs={{0,1},{1,2},{2,3},{3,0},{4,5},{5,6},{6,7},{7,4},{8,9},{9,10},{10,1... | collective-permute-start | bytes 983048 | tf_op jit(solution)/shard_map/ppermute | solution.py:211
  10.8 17.0 %collective-permute-start.1 = (bf16[80,2048]{1,0:T(8,128)(2,1)S(1)}, bf16[80,2048]{1,0:T(8,128)(2,1)S(1)}, u32[]{:S(2)}, u32[]{:S(2)}) collective-permute-start(bf16[80,2048]{1,0:T(8,128)(2,1)S(1)} %copy-done.4), channel_id=1, source_target_pairs={{0,3},{1,0},{2,1},{3,2},{4,7},{5,4},{6,5},{7,6},{8,11},{9,8},{10,9... | collective-permute-start | bytes 983048 | tf_op jit(solution)/shard_map/ppermute | solution.py:211
  14.1 19.4 %collective-permute-start.4 = (bf16[144,768]{1,0:T(8,128)(2,1)S(1)}, bf16[144,768]{1,0:T(8,128)(2,1)S(1)}, u32[]{:S(2)}, u32[]{:S(2)}) collective-permute-start(bf16[144,768]{1,0:T(8,128)(2,1)S(1)} %get-tuple-element.22.own), channel_id=1, source_target_pairs={{0,1},{1,2},{2,3},{3,0},{4,5},{5,6},{6,7},{7,4},{8,9},{9,10},{10,1... | collective-permute-start | bytes 663560 | tf_op jit(solution)/shard_map/ppermute | solution.py:221
  17.5 16.1 %collective-permute-start.5 = (bf16[144,768]{1,0:T(8,128)(2,1)S(1)}, bf16[144,768]{1,0:T(8,128)(2,1)S(1)}, u32[]{:S(2)}, u32[]{:S(2)}) collective-permute-start(bf16[144,768]{1,0:T(8,128)(2,1)S(1)} %get-tuple-element.22.own), channel_id=1, source_target_pairs={{0,3},{1,0},{2,1},{3,2},{4,7},{5,4},{6,5},{7,6},{8,11},{9,8},{10,9... | collective-permute-start | bytes 663560 | tf_op jit(solution)/shard_map/ppermute | solution.py:221
  20.7 12.9 %collective-permute-start.6 = (bf16[144,768]{1,0:T(8,128)(2,1)S(1)}, bf16[144,768]{1,0:T(8,128)(2,1)S(1)}, u32[]{:S(2)}, u32[]{:S(2)}) collective-permute-start(bf16[144,768]{1,0:T(8,128)(2,1)S(1)} %get-tuple-element.22.own), channel_id=1, source_target_pairs={{0,2},{1,3},{2,0},{3,1},{4,6},{5,7},{6,4},{7,5},{8,10},{9,11},{10,... | collective-permute-start | bytes 663560 | tf_op jit(solution)/shard_map/ppermute | solution.py:221
  25.1 17.7 %copy-start.1 = (bf16[80,2048]{1,0:T(8,128)(2,1)}, bf16[80,2048]{1,0:T(8,128)(2,1)S(1)}, u32[]{:S(2)}) copy-start(bf16[80,2048]{1,0:T(8,128)(2,1)S(1)} %collective-permute-done.left) | copy-start | bytes 983044
  25.8 10.4 %collective-permute-start.2 = (bf16[48,2048]{1,0:T(8,128)(2,1)}, bf16[48,2048]{1,0:T(8,128)(2,1)}, u32[]{:S(2)}, u32[]{:S(2)}) collective-permute-start(bf16[48,2048]{1,0:T(8,128)(2,1)} %slice.16), channel_id=1, source_target_pairs={{0,1},{1,2},{2,3},{3,0},{4,5},{5,6},{6,7},{7,4},{8,9},{9,10},{10,1... | collective-permute-start | bytes 589832 | tf_op jit(solution)/shard_map/ppermute | solution.py:211
  27.8 15.1 %copy-start.2 = (bf16[80,2048]{1,0:T(8,128)(2,1)}, bf16[80,2048]{1,0:T(8,128)(2,1)S(1)}, u32[]{:S(2)}) copy-start(bf16[80,2048]{1,0:T(8,128)(2,1)S(1)} %collective-permute-done.1.right) | copy-start | bytes 983044
  27.8 7.2 %collective-permute-start.3 = (bf16[32,2048]{1,0:T(8,128)(2,1)S(1)}, bf16[32,2048]{1,0:T(8,128)(2,1)S(1)}, u32[]{:S(2)}, u32[]{:S(2)}) collective-permute-start(bf16[32,2048]{1,0:T(8,128)(2,1)S(1)} %slice.17), channel_id=1, source_target_pairs={{0,3},{1,0},{2,1},{3,2},{4,7},{5,4},{6,5},{7,6},{8,11},{9,8},{10,9... | collective-permute-start | bytes 393224 | tf_op jit(solution)/shard_map/ppermute | solution.py:211
  34.9 7.9 %copy-start.5 = (bf16[32,2048]{1,0:T(8,128)(2,1)}, bf16[32,2048]{1,0:T(8,128)(2,1)S(1)}, u32[]{:S(2)}) copy-start(bf16[32,2048]{1,0:T(8,128)(2,1)S(1)} %collective-permute-done.3.far_b) | copy-start | bytes 393220
  36.2 9.5 %collective-permute-start.7 = (bf16[4,1408,128]{2,1,0:T(8,128)(2,1)S(1)}, bf16[4,1408,128]{2,1,0:T(8,128)(2,1)S(1)}, u32[]{:S(2)}, u32[]{:S(2)}) collective-permute-start(bf16[4,1408,128]{2,1,0:T(8,128)(2,1)S(1)} %all-to-all-done.mine), channel_id=1, source_target_pairs={{0,16},{16,0},{1,17},{17,1},{2,18},{18,2},{3,19},{19,3},{4,20},{20... | collective-permute-start | bytes 4325384 | tf_op jit(solution)/shard_map/ppermute | solution.py:285
  47.5 12.5 %all-to-all-start.1 = ((bf16[4,80,768]{2,1,0:T(8,128)(2,1)}), bf16[4,80,768]{2,1,0:T(8,128)(2,1)S(1)}, u32[]{:S(2)}, u32[]{:S(2)}) async-start(bf16[4,80,768]{2,1,0:T(8,128)(2,1)} %head.1), calls=%async_computation.1 | async-start | bytes 983040 | tf_op jit(solution)/shard_map/all_to_all | solution.py:318
  51.5 23.8 %collective-permute-start.8 = (bf16[576,768]{1,0:T(8,128)(2,1)S(1)}, bf16[576,768]{1,0:T(8,128)(2,1)S(1)}, u32[]{:S(2)}, u32[]{:S(2)}) collective-permute-start(bf16[576,768]{1,0:T(8,128)(2,1)S(1)} %column.1.own), channel_id=1, source_target_pairs={{0,4},{1,5},{2,6},{3,7},{4,8},{5,9},{6,10},{7,11},{8,12},{9,13},{1... | collective-permute-start | bytes 2654216 | tf_op jit(solution)/shard_map/ppermute | solution.py:221
  54.9 22.4 %collective-permute-start.9 = (bf16[576,768]{1,0:T(8,128)(2,1)S(1)}, bf16[576,768]{1,0:T(8,128)(2,1)S(1)}, u32[]{:S(2)}, u32[]{:S(2)}) collective-permute-start(bf16[576,768]{1,0:T(8,128)(2,1)S(1)} %column.1.own), channel_id=1, source_target_pairs={{0,12},{1,13},{2,14},{3,15},{4,0},{5,1},{6,2},{7,3},{8,4},{9,5},{1... | collective-permute-start | bytes 2654216 | tf_op jit(solution)/shard_map/ppermute | solution.py:221
  61.4 36.0 %all-to-all-start.2 = ((bf16[32,16,256]{2,1,0:T(8,128)(2,1)}), bf16[32,16,256]{2,1,0:T(8,128)(2,1)S(1)}, u32[]{:S(2)}, u32[]{:S(2)}) async-start(bf16[32,16,256]{2,1,0:T(8,128)(2,1)} %query.1), calls=%async_computation.2 | async-start | bytes 524288 | tf_op jit(solution)/shard_map/all_to_all | solution.py:322
  75.4 10.6 %collective-permute-start.10 = (bf16[288,768]{1,0:T(8,128)(2,1)S(1)}, bf16[288,768]{1,0:T(8,128)(2,1)S(1)}, u32[]{:S(2)}, u32[]{:S(2)}) collective-permute-start(bf16[288,768]{1,0:T(8,128)(2,1)S(1)} %slice.18), channel_id=1, source_target_pairs={{0,4},{1,5},{2,6},{3,7},{4,8},{5,9},{6,10},{7,11},{8,12},{9,13},{1... | collective-permute-start | bytes 1327112 | tf_op jit(solution)/shard_map/ppermute | solution.py:221
  77.4 9.8 %collective-permute-start.11 = (bf16[288,768]{1,0:T(8,128)(2,1)S(1)}, bf16[288,768]{1,0:T(8,128)(2,1)}, u32[]{:S(2)}, u32[]{:S(2)}) collective-permute-start(bf16[288,768]{1,0:T(8,128)(2,1)S(1)} %slice.19), channel_id=1, source_target_pairs={{0,12},{1,13},{2,14},{3,15},{4,0},{5,1},{6,2},{7,3},{8,4},{9,5},{1... | collective-permute-start | bytes 1327112 | tf_op jit(solution)/shard_map/ppermute | solution.py:221
  86.0 0.8 copy-start.3

commit v5 on v4

--- a/solution.py
+++ b/solution.py
@@ -38,26 +38,37 @@
     return run
 
 
-def prepare_kernel(
-    w_hidden, w_embed, members, cluster, valid, half, unit, held, slots, live, upper, lower, sem, sems
-):
+def weights_kernel(w_hidden, w_embed, half, upper, lower, sem):
     c = lax.axis_index("core")
-    first = [
+    copies = [
+        pltpu.make_async_copy(
+            w_hidden.at[pl.ds(pl.multiple_of(c * HALF, HALF), HALF), :], upper, sem.at[0]
+        ),
+        pltpu.make_async_copy(
+            w_embed.at[:, pl.ds(pl.multiple_of(c * 3 * BLOCK, BLOCK), 3 * BLOCK)], lower, sem.at[1]
+        ),
+    ]
+    for copy in copies:
+        copy.start()
+    for copy in copies:
+        copy.wait()
+    for j in range(4):
+        half[j, 0:HALF, :] = upper[...]
+        for i in range(3):
+            half[j, HALF + i * BLOCK : HALF + (i + 1) * BLOCK, :] = lower[
+                :, i * BLOCK : (i + 1) * BLOCK
+            ]
+
+
+def unit_kernel(members, cluster, valid, unit, held, slots, live, sem):
+    copies = [
         pltpu.make_async_copy(members.at[0], held, sem.at[0]),
         pltpu.make_async_copy(cluster, slots, sem.at[1]),
         pltpu.make_async_copy(valid, live, sem.at[2]),
     ]
-    rest = [
-        pltpu.make_async_copy(
-            w_hidden.at[pl.ds(pl.multiple_of(c * HALF, HALF), HALF), :], upper, sems.at[0]
-        ),
-        pltpu.make_async_copy(
-            w_embed.at[:, pl.ds(pl.multiple_of(c * 3 * BLOCK, BLOCK), 3 * BLOCK)], lower, sems.at[1]
-        ),
-    ]
-    for copy in first + rest:
+    for copy in copies:
         copy.start()
-    for copy in first:
+    for copy in copies:
         copy.wait()
     values = held[...].astype(F32)
     norm = jnp.sum(values * values, axis=1, keepdims=True)
@@ -65,14 +76,6 @@
     tag = jnp.where(live[...] == 1, slots[...] + 1, 0).astype(F32)
     tag = jnp.concatenate([tag] * (EMB // SLOTS), axis=1)
     unit[SLOTS:UNIT, :] = jnp.broadcast_to(tag, (UNIT - SLOTS, EMB)).astype(BF16)
-    for copy in rest:
-        copy.wait()
-    for j in range(4):
-        half[j, 0:HALF, :] = upper[...]
-        for i in range(3):
-            half[j, HALF + i * BLOCK : HALF + (i + 1) * BLOCK, :] = lower[
-                :, i * BLOCK : (i + 1) * BLOCK
-            ]
 
 
 def slots_kernel(owner_row, owner_col, local_col, tags, rank_row):
@@ -144,19 +147,16 @@
     out[...] = total.astype(BF16).reshape(OWNERS, LINES, CHUNK)
 
 
-def column_kernel(own, left, right, far, out):
-    for i, part in enumerate((own, left, right, far)):
-        out[i * UNIT : (i + 1) * UNIT, :] = part[...]
+def join_kernel(low, high, out):
+    rows = low.shape[0]
+    out[0:rows, :] = low[...]
+    out[rows:, :] = high[...]
 
 
 def score_kernel(arrived, own, left, right, top, bottom, out, held, sem):
-    copies = [
-        pltpu.make_async_copy(top, held.at[0 : 2 * UNIT, :], sem.at[0]),
-        pltpu.make_async_copy(bottom, held.at[2 * UNIT :, :], sem.at[1]),
-    ]
-    for copy in copies:
-        copy.start()
-    parts = (own, left, right, held)
+    copy = pltpu.make_async_copy(bottom, held, sem.at[0])
+    copy.start()
+    parts = (own, left, right, top, held)
     row = iota((4 * OWNERS * CAP, 1), 0)
     kind, slot = row // (OWNERS * CAP), row % (OWNERS * CAP)
     line = jnp.where(kind < 3, kind * CAP + slot // OWNERS, LINES - 1)
@@ -175,9 +175,8 @@
     best = jnp.full((count, 2 * SLOTS), -1.0, F32)
     where = [(part, i * UNIT) for part in parts for i in range(part.shape[0] // UNIT)]
     for j in range(0, 16, 2):
-        if j == 12:
-            for copy in copies:
-                copy.wait()
+        if j == 14:
+            copy.wait()
         blocks, marks = [], []
         for part, row in where[j : j + 2]:
             blocks.append(part[row : row + SLOTS, :])
@@ -211,42 +210,59 @@
     return lax.ppermute(value, axis, [(i, (i + step) % 4) for i in range(4)])
 
 
-def turn(value, step, turned):
+def turn(value, move, turned):
     pairs = []
     for c in range(2):
         for y in range(4):
             for x in range(4):
-                to = (y, (x + step) % 4) if (c == 1) == turned else ((y + step) % 4, x)
+                to = (y, move(x)) if (c == 1) == turned else (move(y), x)
                 pairs.append((c * 16 + y * 4 + x, c * 16 + to[0] * 4 + to[1]))
     return lax.ppermute(value, ("core", "y", "x"), pairs)
 
 
-def gather(value, turned):
-    return [value] + [turn(value, step, turned) for step in (1, -1, 2)]
+def up(place):
+    return (place + 1) % 4
+
+
+def down(place):
+    return (place + 3) % 4
 
 
 HBM = pl.BlockSpec(memory_space=pltpu.HBM)
 VMEM = pl.BlockSpec(memory_space=pltpu.VMEM)
 
 
-def prepared(*arrays):
+def halved(*arrays):
     return pl.pallas_call(
-        prepare_kernel,
-        out_shape=(pltpu.VMEM((4, PACK, BLOCK), BF16), sds((UNIT, EMB), BF16)),
-        in_specs=[HBM] * 5,
-        out_specs=(VMEM, VMEM),
+        weights_kernel,
+        out_shape=pltpu.VMEM((4, PACK, BLOCK), BF16),
+        in_specs=[HBM] * 2,
+        out_specs=VMEM,
+        scratch_shapes=[
+            pltpu.VMEM((HALF, BLOCK), BF16),
+            pltpu.VMEM((BLOCK, 3 * BLOCK), BF16),
+            pltpu.SemaphoreType.DMA((2,)),
+        ],
+        name="weights",
+        compiler_params=PARAMS,
+    )(*map(stay, arrays))
+
+
+def normalised(*arrays):
+    return pl.pallas_call(
+        unit_kernel,
+        out_shape=sds((UNIT, EMB), BF16),
+        in_specs=[HBM] * 3,
+        out_specs=VMEM,
         scratch_shapes=[
             pltpu.VMEM((SLOTS, EMB), BF16),
             pltpu.VMEM((1, SLOTS), I32),
             pltpu.VMEM((1, SLOTS), I32),
-            pltpu.VMEM((HALF, BLOCK), BF16),
-            pltpu.VMEM((BLOCK, 3 * BLOCK), BF16),
             pltpu.SemaphoreType.DMA((3,)),
-            pltpu.SemaphoreType.DMA((2,)),
         ],
-        name="prepare",
+        name="unit",
         compiler_params=PARAMS,
-    )(*arrays)
+    )(*map(stay, arrays))
 
 
 def first(*arrays):
@@ -261,6 +277,10 @@
     )(*arrays)
 
 
+def joined(blocks, *parts):
+    return call(join_kernel, sds((blocks * UNIT, EMB), BF16), "join")(*map(near, parts))
+
+
 def near(value):
     return pltpu.with_memory_space_constraint(value, pltpu.VMEM)
 
@@ -269,9 +289,9 @@
     return pl.pallas_call(
         score_kernel,
         out_shape=sds((OWNERS, SLOTS), F32),
-        in_specs=[VMEM] * 4 + [HBM] * 2,
+        in_specs=[VMEM] * 5 + [HBM],
         out_specs=VMEM,
-        scratch_shapes=[pltpu.VMEM((4 * UNIT, EMB), BF16), pltpu.SemaphoreType.DMA((2,))],
+        scratch_shapes=[pltpu.VMEM((2 * UNIT, EMB), BF16), pltpu.SemaphoreType.DMA((1,))],
         name="score",
         compiler_params=PARAMS,
     )(*arrays)
@@ -287,10 +307,10 @@
 
 def body(features, w_hidden, w_embed, members, doc_owner, doc_local, member_cluster, member_valid):
     dp = ("z", "core")
-    half, unit = prepared(*map(stay, (w_hidden, w_embed, members, member_cluster, member_valid)))
-    units = gather(unit, False)
-    mine = lax.all_to_all(near(half), "y", 0, 0, tiled=True)
+    mine = lax.all_to_all(near(halved(w_hidden, w_embed)), "y", 0, 0, tiled=True)
     docs = [shift(features, "x", 1), shift(features, "x", -1)]
+    unit = normalised(members, member_cluster, member_valid)
+    beside = turn(unit, lambda place: place ^ 1, False)
     cut = 48
     docs += [shift(docs[0][:cut], "x", 1), shift(docs[1][cut:], "x", -1)]
 
@@ -307,20 +327,22 @@
         "slots",
     )(owner_row, owner.reshape(ROWS, 1), local.reshape(ROWS, 1))
 
-    mine, tags, docs, units[1:] = lax.optimization_barrier((mine, tags, docs, units[1:]))
+    mine, tags, docs, beside = lax.optimization_barrier((mine, tags, docs, beside))
+    pair = joined(2, unit, beside)
+    opposite = turn(pair, lambda place: 3 - place, False)
     other = swap(mine)
-    column = call(column_kernel, sds((4 * UNIT, EMB), BF16), "column")(*map(near, units))
-    left, right = turn(column, 1, True), turn(column, -1, True)
-    top, bottom = turn(left[: 2 * UNIT], 1, True), turn(right[2 * UNIT :], -1, True)
+    column = joined(4, pair, opposite)
+    left, right = turn(column, up, True), turn(column, down, True)
+    top, bottom = turn(left[: 2 * UNIT], up, True), turn(right[2 * UNIT :], down, True)
     columns = [column, left, right, top, bottom]
     pre, rest = first(*map(stay, (features, *docs)), mine)
-    partial = call(head_kernel, sds((4, ROWS, EMB), BF16), "head")(near(pre), near(rest), mine, other)
-    partial = lax.all_to_all(partial, "x", 0, 0, tiled=True)
-    outgoing = call(query_kernel, sds((OWNERS, LINES, CHUNK), BF16), "query")(
+    partial = call(head_kernel, pltpu.VMEM((4, ROWS, EMB), BF16), "head")(near(pre), near(rest), mine, other)
+    partial = lax.all_to_all(near(partial), "x", 0, 0, tiled=True)
+    outgoing = call(query_kernel, pltpu.VMEM((OWNERS, LINES, CHUNK), BF16), "query")(
         partial, owner_row, rank_row, tags
     )
-    arrived = lax.all_to_all(outgoing, dp, 0, 0, tiled=True)
-    best = score(arrived, *map(near, columns[:3]), *map(stay, columns[3:]))
+    arrived = lax.all_to_all(near(outgoing), dp, 0, 0, tiled=True)
+    best = score(arrived, *map(near, columns[:4]), stay(columns[4]))
     answers = lax.all_to_all(best, dp, 0, 0, tiled=True)
     result = call(answer_kernel, sds((1, ROWS), F32), "answer")(answers, owner_row, rank_row)
     return result.reshape(ROWS)

time: 117 us -> 115 us (0.983)
  starting transfers between devices: 65.9 us -> 63.3 us
  Pallas kernels: 10.4 us -> 11.7 us
    ppermute x7 -> x6, starting transfers between devices: 23.2 us -> 21.2 us  [turn(): return lax.ppermute(value, ('core', 'y', 'x'), pairs)]
    all_to_all x3, starting transfers between devices: 23.1 us -> 21.2 us  [the longest x1 12.6 us: body(): arrived = lax.all_to_all(near(outgoing), dp, 0, 0, tiled=True)]
    ppermute x1, starting transfers between devices: 6.63 us -> 8.01 us  [swap(): return lax.ppermute(value, 'core', [(0, 1), (1, 0)])]
    pallas_call x1 -> x2, Pallas kernels: 2.46 us -> 3.41 us  [the longest x1 2.31 us: halved(): pl.pallas_call(weights_kernel, out_shape=pltpu.VMEM((4, PACK, BLOCK), BF1...]
    ppermute x7 -> x6, waiting for transfers between devices: 4.47 us -> 5.24 us  [turn(): return lax.ppermute(value, ('core', 'y', 'x'), pairs)]
    pallas_call x5 -> x6, Pallas kernels: 3.99 us -> 4 us  [run(): pl.pallas_call(body, out_shape=out, in_specs=specs, out_specs=outs, name=...]
  transfers between devices with their start and end apart: 15 -> 14, of which waited for: 7 -> 5; matrix products, arithmetic and copies ran while one was open for 2% -> 2% of each run, Pallas kernels for 3% -> 6%
where the time goes in v5:
time: 115 us; the launch traced here: 114 us
  starting transfers between devices  63.3 us (55%)
  waiting for transfers between devices  20 us (17%)
  blocking collectives  15.9 us (14%)
  Pallas kernels  11.7 us (10%)
  local copies, waits for them, and re-layouts  2.6 us (2%)
    ppermute x6, starting transfers between devices, turn(): return lax.ppermute(value, ('core', 'y', 'x'), pairs)  21.2 us
    all_to_all x1, blocking collectives, body(): answers = lax.all_to_all(best, dp, 0, 0, tiled=True)  15.9 us
    ppermute x4, starting transfers between devices, shift(): return lax.ppermute(value, axis, [(i, (i + step) % 4) for i in range(4)])  13 us
    all_to_all x1, starting transfers between devices, body(): arrived = lax.all_to_all(near(outgoing), dp, 0, 0, tiled=True)  12.6 us
    all_to_all x1, waiting for transfers between devices, body(): arrived = lax.all_to_all(near(outgoing), dp, 0, 0, tiled=True)  10.2 us
    ppermute x1, starting transfers between devices, swap(): return lax.ppermute(value, 'core', [(0, 1), (1, 0)])  8.01 us
    ppermute x6, waiting for transfers between devices, turn(): return lax.ppermute(value, ('core', 'y', 'x'), pairs)  5.24 us
    all_to_all x1, starting transfers between devices, body(): lax.all_to_all(near(halved(w_hidden, w_embed)), 'y', 0, 0, tiled=True)  5.16 us
  transfers between devices with their start and end apart: 14, of which 5 were waited for; matrix products, arithmetic and copies ran while one was open for 2% of the time, Pallas kernels for 6%

profile of v5, /device:TPU:1, one launch (start us, length us, event | category | flops | bytes accessed | tf_op | source)
XLA Modules:
  0.0 113.8 jit_solution(3811261208242457154)
XLA Ops:
  0.0 2.3 %weights.1 = bf16[4,1408,128]{2,1,0:T(8,128)(2,1)} custom-call(bf16[2048,128]{1,0:T(8,128)(2,1)} %w_hidden.1, bf16[128,768]{1,0:T(8,128)(2,1)} %w_embed.1), custom_call_target="tpu_custom_call" | custom-call | tf_op jit(solution)/shard_map/weights/pallas_call | solution.py:236
  2.3 0.0 copy-start.3
  2.3 5.2 %all-to-all-start = ((bf16[4,1408,128]{2,1,0:T(8,128)(2,1)}), bf16[4,1408,128]{2,1,0:T(8,128)(2,1)S(1)}, u32[]{:S(2)}, u32[]{:S(2)}) async-start(bf16[4,1408,128]{2,1,0:T(8,128)(2,1)} %weights.1), calls=%async_computation | async-start | bytes 2883584 | tf_op jit(solution)/shard_map/all_to_all | solution.py:310
  7.5 3.1 %collective-permute-start = (bf16[80,2048]{1,0:T(8,128)(2,1)S(1)}, bf16[80,2048]{1,0:T(8,128)(2,1)S(1)}, u32[]{:S(2)}, u32[]{:S(2)}) collective-permute-start(bf16[80,2048]{1,0:T(8,128)(2,1)S(1)} %copy-done.3), channel_id=1, source_target_pairs={{0,1},{1,2},{2,3},{3,0},{4,5},{5,6},{6,7},{7,4},{8,9},{9,10},{10,1... | collective-permute-start | bytes 983048 | tf_op jit(solution)/shard_map/ppermute | solution.py:210
  10.6 3.4 %collective-permute-start.1 = (bf16[80,2048]{1,0:T(8,128)(2,1)S(1)}, bf16[80,2048]{1,0:T(8,128)(2,1)S(1)}, u32[]{:S(2)}, u32[]{:S(2)}) collective-permute-start(bf16[80,2048]{1,0:T(8,128)(2,1)S(1)} %copy-done.3), channel_id=1, source_target_pairs={{0,3},{1,0},{2,1},{3,2},{4,7},{5,4},{6,5},{7,6},{8,11},{9,8},{10,9... | collective-permute-start | bytes 983048 | tf_op jit(solution)/shard_map/ppermute | solution.py:210
  14.0 1.1 unit.1.low
  15.1 3.4 %collective-permute-start.4 = (bf16[144,768]{1,0:T(8,128)(2,1)S(1)}, bf16[144,768]{1,0:T(8,128)(2,1)S(1)}, u32[]{:S(2)}, u32[]{:S(2)}) collective-permute-start(bf16[144,768]{1,0:T(8,128)(2,1)S(1)} %unit.1.low), channel_id=1, source_target_pairs={{0,1},{1,0},{2,3},{3,2},{4,5},{5,4},{6,7},{7,6},{8,9},{9,8},{10,11... | collective-permute-start | bytes 663560 | tf_op jit(solution)/shard_map/ppermute | solution.py:220
  18.5 0.8 constant_dynamic-slice_fusion
  19.2 0.0 collective-permute-done.left
  19.2 0.7 slice.16
  20.0 1.9 %collective-permute-start.2 = (bf16[48,2048]{1,0:T(8,128)(2,1)}, bf16[48,2048]{1,0:T(8,128)(2,1)}, u32[]{:S(2)}, u32[]{:S(2)}) collective-permute-start(bf16[48,2048]{1,0:T(8,128)(2,1)} %slice.16), channel_id=1, source_target_pairs={{0,1},{1,2},{2,3},{3,0},{4,5},{5,6},{6,7},{7,4},{8,9},{9,10},{10,1... | collective-permute-start | bytes 589832 | tf_op jit(solution)/shard_map/ppermute | solution.py:210
  21.9 0.0 collective-permute-done.1.right
  21.9 4.6 %collective-permute-start.3 = (bf16[32,2048]{1,0:T(8,128)(2,1)S(1)}, bf16[32,2048]{1,0:T(8,128)(2,1)S(1)}, u32[]{:S(2)}, u32[]{:S(2)}) collective-permute-start(bf16[32,2048]{1,0:T(8,128)(2,1)S(1)} %slice.17), channel_id=1, source_target_pairs={{0,3},{1,0},{2,1},{3,2},{4,7},{5,4},{6,5},{7,6},{8,11},{9,8},{10,9... | collective-permute-start | bytes 393224 | tf_op jit(solution)/shard_map/ppermute | solution.py:210
  26.5 0.1 dynamic-slice_bitcast_fusion
  26.6 0.1 copy.16.owner_col
  26.7 0.1 copy.14.local_col
  26.8 0.8 fusion.owner_row
  27.5 0.2 slots.1
  27.7 0.0 collective-permute-done.4.high
  27.7 1.5 %collective-permute-done.3.far_b = bf16[32,2048]{1,0:T(8,128)(2,1)S(1)} collective-permute-done((bf16[32,2048]{1,0:T(8,128)(2,1)S(1)}, bf16[32,2048]{1,0:T(8,128)(2,1)S(1)}, u32[]{:S(2)}, u32[]{:S(2)}) %collective-permute-start.3) | collective-permute-done | bytes 131104 | tf_op jit(solution)/shard_map/ppermute | solution.py:210
  29.2 0.0 collective-permute-done.2.far_a
  29.2 0.0 all-to-all-done.mine
  29.3 8.0 %collective-permute-start.5 = (bf16[4,1408,128]{2,1,0:T(8,128)(2,1)S(1)}, bf16[4,1408,128]{2,1,0:T(8,128)(2,1)S(1)}, u32[]{:S(2)}, u32[]{:S(2)}) collective-permute-start(bf16[4,1408,128]{2,1,0:T(8,128)(2,1)S(1)} %all-to-all-done.mine), channel_id=1, source_target_pairs={{0,16},{16,0},{1,17},{17,1},{2,18},{18,2},{3,19},{19,3},{4,20},{20... | collective-permute-start | bytes 4325384 | tf_op jit(solution)/shard_map/ppermute | solution.py:305
  37.3 4.8 %collective-permute-start.6 = (bf16[288,768]{1,0:T(8,128)(2,1)S(1)}, bf16[288,768]{1,0:T(8,128)(2,1)S(1)}, u32[]{:S(2)}, u32[]{:S(2)}) collective-permute-start(bf16[288,768]{1,0:T(8,128)(2,1)S(1)} %join.2.low), channel_id=1, source_target_pairs={{0,3},{1,2},{2,1},{3,0},{4,7},{5,6},{6,5},{7,4},{8,11},{9,10},{10,... | collective-permute-start | bytes 1327112 | tf_op jit(solution)/shard_map/ppermute | solution.py:220
  42.1 0.0 copy-done.1
  42.1 0.0 copy-done.2
  42.1 0.0 copy-done.4
  42.2 1.8 %first.1 = (f32[320,512]{1,0:T(8,128)S(1)}, bf16[320,1024]{1,0:T(8,128)(2,1)S(1)}) custom-call(bf16[80,2048]{1,0:T(8,128)(2,1)} %own.1, bf16[80,2048]{1,0:T(8,128)(2,1)} %copy-done.1, bf16[80,2048]{1,0:T(8,128)(2,1)} %copy-done.2, bf16[48,2048]{1,0:T(8,128)(2,1)} %collective-permute-done.2.far_a, bf16[32,2048]{1,0:T(8,128)(2,1)} %copy-done.4, ...), custom_call_target="tpu_custom_call" | custom-call | tf_op jit(solution)/shard_map/first/pallas_call | solution.py:269
  44.0 0.0 collective-permute-done.5.other
  44.0 1.8 %head.1 = bf16[4,80,768]{2,1,0:T(8,128)(2,1)} custom-call(f32[320,512]{1,0:T(8,128)S(1)} %get-tuple-element.22.pre, bf16[320,1024]{1,0:T(8,128)(2,1)S(1)} %get-tuple-element.23.rest, bf16[4,1408,128]{2,1,0:T(8,128)(2,1)S(1)} %all-to-all-done.mine, bf16[4,1408,128]{2,1,0:T(8,128)(2,1)S(1)} %collective-permute-done.5.other), custom_call_target="tpu_custom_call" | custom-call | tf_op jit(solution)/shard_map/head/pallas_call | solution.py:34
  45.8 3.5 %all-to-all-start.1 = ((bf16[4,80,768]{2,1,0:T(8,128)(2,1)}), bf16[4,80,768]{2,1,0:T(8,128)(2,1)S(1)}, u32[]{:S(2)}, u32[]{:S(2)}) async-start(bf16[4,80,768]{2,1,0:T(8,128)(2,1)} %head.1), calls=%async_computation.1 | async-start | bytes 983040 | tf_op jit(solution)/shard_map/all_to_all | solution.py:340
  49.3 0.0 collective-permute-done.6.high
  49.3 0.1 join.3.own
  49.4 3.3 %collective-permute-start.7 = (bf16[576,768]{1,0:T(8,128)(2,1)S(1)}, bf16[576,768]{1,0:T(8,128)(2,1)S(1)}, u32[]{:S(2)}, u32[]{:S(2)}) collective-permute-start(bf16[576,768]{1,0:T(8,128)(2,1)S(1)} %join.3.own), channel_id=1, source_target_pairs={{0,4},{1,5},{2,6},{3,7},{4,8},{5,9},{6,10},{7,11},{8,12},{9,13},{1... | collective-permute-start | bytes 2654216 | tf_op jit(solution)/shard_map/ppermute | solution.py:220
  52.7 3.2 %collective-permute-start.8 = (bf16[576,768]{1,0:T(8,128)(2,1)S(1)}, bf16[576,768]{1,0:T(8,128)(2,1)S(1)}, u32[]{:S(2)}, u32[]{:S(2)}) collective-permute-start(bf16[576,768]{1,0:T(8,128)(2,1)S(1)} %join.3.own), channel_id=1, source_target_pairs={{0,12},{1,13},{2,14},{3,15},{4,0},{5,1},{6,2},{7,3},{8,4},{9,5},{1... | collective-permute-start | bytes 2654216 | tf_op jit(solution)/shard_map/ppermute | solution.py:220
  55.9 3.1 %all-to-all-done.1.partial = bf16[4,80,768]{2,1,0:T(8,128)(2,1)S(1)} async-done(((bf16[4,80,768]{2,1,0:T(8,128)(2,1)}), bf16[4,80,768]{2,1,0:T(8,128)(2,1)S(1)}, u32[]{:S(2)}, u32[]{:S(2)}) %all-to-all-start.1) | async-done | bytes 491552 | tf_op jit(solution)/shard_map/all_to_all | solution.py:340
  59.0 1.3 %query.1 = bf16[32,16,256]{2,1,0:T(8,128)(2,1)} custom-call(bf16[4,80,768]{2,1,0:T(8,128)(2,1)S(1)} %all-to-all-done.1.partial, s32[1,80]{1,0:T(1,128)S(1)} %fusion.owner_row, s32[1,80]{1,0:T(1,128)S(1)} %get-tuple-element.24.rank_row, bf16[80,256]{1,0:T(8,128)(2,1)S(1)} %get-tuple-element.25.tags), custom_call_target="tpu_custom_call" | custom-call | tf_op jit(solution)/shard_map/query/pallas_call | solution.py:34
  60.3 12.6 %all-to-all-start.2 = ((bf16[32,16,256]{2,1,0:T(8,128)(2,1)}), bf16[32,16,256]{2,1,0:T(8,128)(2,1)S(1)}, u32[]{:S(2)}, u32[]{:S(2)}) async-start(bf16[32,16,256]{2,1,0:T(8,128)(2,1)} %query.1), calls=%async_computation.2 | async-start | bytes 524288 | tf_op jit(solution)/shard_map/all_to_all | solution.py:344
  72.9 0.0 collective-permute-done.7.left
  72.9 2.0 %collective-permute-start.9 = (bf16[288,768]{1,0:T(8,128)(2,1)S(1)}, bf16[288,768]{1,0:T(8,128)(2,1)S(1)}, u32[]{:S(2)}, u32[]{:S(2)}) collective-permute-start(bf16[288,768]{1,0:T(8,128)(2,1)S(1)} %slice.18), channel_id=1, source_target_pairs={{0,4},{1,5},{2,6},{3,7},{4,8},{5,9},{6,10},{7,11},{8,12},{9,13},{1... | collective-permute-start | bytes 1327112 | tf_op jit(solution)/shard_map/ppermute | solution.py:220
  74.9 0.0 collective-permute-done.8.right
  74.9 4.5 %collective-permute-start.10 = (bf16[288,768]{1,0:T(8,128)(2,1)S(1)}, bf16[288,768]{1,0:T(8,128)(2,1)}, u32[]{:S(2)}, u32[]{:S(2)}) collective-permute-start(bf16[288,768]{1,0:T(8,128)(2,1)S(1)} %slice.19), channel_id=1, source_target_pairs={{0,12},{1,13},{2,14},{3,15},{4,0},{5,1},{6,2},{7,3},{8,4},{9,5},{1... | collective-permute-start | bytes 1327112 | tf_op jit(solution)/shard_map/ppermute | solution.py:220
  79.5 4.0 %collective-permute-done.9.top = bf16[288,768]{1,0:T(8,128)(2,1)S(1)} collective-permute-done((bf16[288,768]{1,0:T(8,128)(2,1)S(1)}, bf16[288,768]{1,0:T(8,128)(2,1)S(1)}, u32[]{:S(2)}, u32[]{:S(2)}) %collective-permute-start.9) | collective-permute-done | bytes 442400 | tf_op jit(solution)/shard_map/ppermute | solution.py:220
  83.5 1.2 %collective-permute-done.10.bottom = bf16[288,768]{1,0:T(8,128)(2,1)} collective-permute-done((bf16[288,768]{1,0:T(8,128)(2,1)S(1)}, bf16[288,768]{1,0:T(8,128)(2,1)}, u32[]{:S(2)}, u32[]{:S(2)}) %collective-permute-start.10) | collective-permute-done | bytes 442400 | tf_op jit(solution)/shard_map/ppermute | solution.py:220
  84.7 10.2 %all-to-all-done.2.arrived = bf16[32,16,256]{2,1,0:T(8,128)(2,1)S(1)} async-done(((bf16[32,16,256]{2,1,0:T(8,128)(2,1)}), bf16[32,16,256]{2,1,0:T(8,128)(2,1)S(1)}, u32[]{:S(2)}, u32[]{:S(2)}) %all-to-all-start.2) | async-done | bytes 262176 | tf_op jit(solution)/shard_map/all_to_all | solution.py:344
  94.8 2.5 %score.1 = f32[32,128]{1,0:T(8,128)S(1)} custom-call(bf16[32,16,256]{2,1,0:T(8,128)(2,1)S(1)} %all-to-all-done.2.arrived, bf16[576,768]{1,0:T(8,128)(2,1)S(1)} %join.3.own, bf16[576,768]{1,0:T(8,128)(2,1)S(1)} %collective-permute-done.7.left, bf16[576,768]{1,0:T(8,128)(2,1)S(1)} %collective-permute-done.8.right, ...), custom_call_target="tpu_custom_call" | custom-call | tf_op jit(solution)/shard_map/score/pallas_call | solution.py:289
  97.3 15.9 %all_to_all.26 = f32[32,1,128]{2,1,0:T(1,128)S(1)} all-to-all(f32[32,1,128]{2,1,0:T(1,128)S(1)} %bitcast.10), channel_id=1, replica_groups=mesh['z'=16,'core'=2,'y'=4,'x'=4] {'z','core'}, dimensions={0} | all-to-all | bytes 32768 | tf_op jit(solution)/shard_map/all_to_all | solution.py:346
  113.2 0.6 answer.1
  (10 shorter events, 0.1 us)
Async XLA Ops:
  0.0 26.5 %copy-start = (s32[1280]{0:T(1024)S(1)}, s32[1280]{0:T(1024)}, u32[]{:S(2)}) copy-start(s32[1280]{0:T(1024)} %param.13) | copy-start | bytes 15364
  2.3 5.2 %copy-start.3 = (bf16[80,2048]{1,0:T(8,128)(2,1)S(1)}, bf16[80,2048]{1,0:T(8,128)(2,1)}, u32[]{:S(2)}) copy-start(bf16[80,2048]{1,0:T(8,128)(2,1)} %own.1) | copy-start | bytes 983044
  2.3 26.9 %all-to-all-start = ((bf16[4,1408,128]{2,1,0:T(8,128)(2,1)}), bf16[4,1408,128]{2,1,0:T(8,128)(2,1)S(1)}, u32[]{:S(2)}, u32[]{:S(2)}) async-start(bf16[4,1408,128]{2,1,0:T(8,128)(2,1)} %weights.1), calls=%async_computation | async-start | bytes 2883584 | tf_op jit(solution)/shard_map/all_to_all | solution.py:310
  7.5 11.8 %collective-permute-start = (bf16[80,2048]{1,0:T(8,128)(2,1)S(1)}, bf16[80,2048]{1,0:T(8,128)(2,1)S(1)}, u32[]{:S(2)}, u32[]{:S(2)}) collective-permute-start(bf16[80,2048]{1,0:T(8,128)(2,1)S(1)} %copy-done.3), channel_id=1, source_target_pairs={{0,1},{1,2},{2,3},{3,0},{4,5},{5,6},{6,7},{7,4},{8,9},{9,10},{10,1... | collective-permute-start | bytes 983048 | tf_op jit(solution)/shard_map/ppermute | solution.py:210
  10.6 11.3 %collective-permute-start.1 = (bf16[80,2048]{1,0:T(8,128)(2,1)S(1)}, bf16[80,2048]{1,0:T(8,128)(2,1)S(1)}, u32[]{:S(2)}, u32[]{:S(2)}) collective-permute-start(bf16[80,2048]{1,0:T(8,128)(2,1)S(1)} %copy-done.3), channel_id=1, source_target_pairs={{0,3},{1,0},{2,1},{3,2},{4,7},{5,4},{6,5},{7,6},{8,11},{9,8},{10,9... | collective-permute-start | bytes 983048 | tf_op jit(solution)/shard_map/ppermute | solution.py:210
  15.1 12.6 %collective-permute-start.4 = (bf16[144,768]{1,0:T(8,128)(2,1)S(1)}, bf16[144,768]{1,0:T(8,128)(2,1)S(1)}, u32[]{:S(2)}, u32[]{:S(2)}) collective-permute-start(bf16[144,768]{1,0:T(8,128)(2,1)S(1)} %unit.1.low), channel_id=1, source_target_pairs={{0,1},{1,0},{2,3},{3,2},{4,5},{5,4},{6,7},{7,6},{8,9},{9,8},{10,11... | collective-permute-start | bytes 663560 | tf_op jit(solution)/shard_map/ppermute | solution.py:220
  19.2 22.9 %copy-start.1 = (bf16[80,2048]{1,0:T(8,128)(2,1)}, bf16[80,2048]{1,0:T(8,128)(2,1)S(1)}, u32[]{:S(2)}) copy-start(bf16[80,2048]{1,0:T(8,128)(2,1)S(1)} %collective-permute-done.left) | copy-start | bytes 983044
  20.0 9.3 %collective-permute-start.2 = (bf16[48,2048]{1,0:T(8,128)(2,1)}, bf16[48,2048]{1,0:T(8,128)(2,1)}, u32[]{:S(2)}, u32[]{:S(2)}) collective-permute-start(bf16[48,2048]{1,0:T(8,128)(2,1)} %slice.16), channel_id=1, source_target_pairs={{0,1},{1,2},{2,3},{3,0},{4,5},{5,6},{6,7},{7,4},{8,9},{9,10},{10,1... | collective-permute-start | bytes 589832 | tf_op jit(solution)/shard_map/ppermute | solution.py:210
  21.9 20.2 %copy-start.2 = (bf16[80,2048]{1,0:T(8,128)(2,1)}, bf16[80,2048]{1,0:T(8,128)(2,1)S(1)}, u32[]{:S(2)}) copy-start(bf16[80,2048]{1,0:T(8,128)(2,1)S(1)} %collective-permute-done.1.right) | copy-start | bytes 983044
  21.9 7.3 %collective-permute-start.3 = (bf16[32,2048]{1,0:T(8,128)(2,1)S(1)}, bf16[32,2048]{1,0:T(8,128)(2,1)S(1)}, u32[]{:S(2)}, u32[]{:S(2)}) collective-permute-start(bf16[32,2048]{1,0:T(8,128)(2,1)S(1)} %slice.17), channel_id=1, source_target_pairs={{0,3},{1,0},{2,1},{3,2},{4,7},{5,4},{6,5},{7,6},{8,11},{9,8},{10,9... | collective-permute-start | bytes 393224 | tf_op jit(solution)/shard_map/ppermute | solution.py:210
  29.2 12.9 %copy-start.4 = (bf16[32,2048]{1,0:T(8,128)(2,1)}, bf16[32,2048]{1,0:T(8,128)(2,1)S(1)}, u32[]{:S(2)}) copy-start(bf16[32,2048]{1,0:T(8,128)(2,1)S(1)} %collective-permute-done.3.far_b) | copy-start | bytes 393220
  29.3 14.7 %collective-permute-start.5 = (bf16[4,1408,128]{2,1,0:T(8,128)(2,1)S(1)}, bf16[4,1408,128]{2,1,0:T(8,128)(2,1)S(1)}, u32[]{:S(2)}, u32[]{:S(2)}) collective-permute-start(bf16[4,1408,128]{2,1,0:T(8,128)(2,1)S(1)} %all-to-all-done.mine), channel_id=1, source_target_pairs={{0,16},{16,0},{1,17},{17,1},{2,18},{18,2},{3,19},{19,3},{4,20},{20... | collective-permute-start | bytes 4325384 | tf_op jit(solution)/shard_map/ppermute | solution.py:305
  37.3 12.0 %collective-permute-start.6 = (bf16[288,768]{1,0:T(8,128)(2,1)S(1)}, bf16[288,768]{1,0:T(8,128)(2,1)S(1)}, u32[]{:S(2)}, u32[]{:S(2)}) collective-permute-start(bf16[288,768]{1,0:T(8,128)(2,1)S(1)} %join.2.low), channel_id=1, source_target_pairs={{0,3},{1,2},{2,1},{3,0},{4,7},{5,6},{6,5},{7,4},{8,11},{9,10},{10,... | collective-permute-start | bytes 1327112 | tf_op jit(solution)/shard_map/ppermute | solution.py:220
  45.8 13.2 %all-to-all-start.1 = ((bf16[4,80,768]{2,1,0:T(8,128)(2,1)}), bf16[4,80,768]{2,1,0:T(8,128)(2,1)S(1)}, u32[]{:S(2)}, u32[]{:S(2)}) async-start(bf16[4,80,768]{2,1,0:T(8,128)(2,1)} %head.1), calls=%async_computation.1 | async-start | bytes 983040 | tf_op jit(solution)/shard_map/all_to_all | solution.py:340
  49.4 23.5 %collective-permute-start.7 = (bf16[576,768]{1,0:T(8,128)(2,1)S(1)}, bf16[576,768]{1,0:T(8,128)(2,1)S(1)}, u32[]{:S(2)}, u32[]{:S(2)}) collective-permute-start(bf16[576,768]{1,0:T(8,128)(2,1)S(1)} %join.3.own), channel_id=1, source_target_pairs={{0,4},{1,5},{2,6},{3,7},{4,8},{5,9},{6,10},{7,11},{8,12},{9,13},{1... | collective-permute-start | bytes 2654216 | tf_op jit(solution)/shard_map/ppermute | solution.py:220
  52.7 22.2 %collective-permute-start.8 = (bf16[576,768]{1,0:T(8,128)(2,1)S(1)}, bf16[576,768]{1,0:T(8,128)(2,1)S(1)}, u32[]{:S(2)}, u32[]{:S(2)}) collective-permute-start(bf16[576,768]{1,0:T(8,128)(2,1)S(1)} %join.3.own), channel_id=1, source_target_pairs={{0,12},{1,13},{2,14},{3,15},{4,0},{5,1},{6,2},{7,3},{8,4},{9,5},{1... | collective-permute-start | bytes 2654216 | tf_op jit(solution)/shard_map/ppermute | solution.py:220
  60.3 34.6 %all-to-all-start.2 = ((bf16[32,16,256]{2,1,0:T(8,128)(2,1)}), bf16[32,16,256]{2,1,0:T(8,128)(2,1)S(1)}, u32[]{:S(2)}, u32[]{:S(2)}) async-start(bf16[32,16,256]{2,1,0:T(8,128)(2,1)} %query.1), calls=%async_computation.2 | async-start | bytes 524288 | tf_op jit(solution)/shard_map/all_to_all | solution.py:344
  72.9 10.6 %collective-permute-start.9 = (bf16[288,768]{1,0:T(8,128)(2,1)S(1)}, bf16[288,768]{1,0:T(8,128)(2,1)S(1)}, u32[]{:S(2)}, u32[]{:S(2)}) collective-permute-start(bf16[288,768]{1,0:T(8,128)(2,1)S(1)} %slice.18), channel_id=1, source_target_pairs={{0,4},{1,5},{2,6},{3,7},{4,8},{5,9},{6,10},{7,11},{8,12},{9,13},{1... | collective-permute-start | bytes 1327112 | tf_op jit(solution)/shard_map/ppermute | solution.py:220
  74.9 9.8 %collective-permute-start.10 = (bf16[288,768]{1,0:T(8,128)(2,1)S(1)}, bf16[288,768]{1,0:T(8,128)(2,1)}, u32[]{:S(2)}, u32[]{:S(2)}) collective-permute-start(bf16[288,768]{1,0:T(8,128)(2,1)S(1)} %slice.19), channel_id=1, source_target_pairs={{0,12},{1,13},{2,14},{3,15},{4,0},{5,1},{6,2},{7,3},{8,4},{9,5},{1... | collective-permute-start | bytes 1327112 | tf_op jit(solution)/shard_map/ppermute | solution.py:220

commit v6 on v5

--- a/solution.py
+++ b/solution.py
@@ -273,6 +273,7 @@
         out_specs=(VMEM, VMEM),
         scratch_shapes=[pltpu.VMEM((4 * ROWS, HID), BF16), pltpu.SemaphoreType.DMA((5,))],
         name="first",
+        cost_estimate=pl.CostEstimate(flops=30 << 30, bytes_accessed=4 << 20, transcendentals=0),
         compiler_params=PARAMS,
     )(*arrays)
 
@@ -327,7 +328,7 @@
         "slots",
     )(owner_row, owner.reshape(ROWS, 1), local.reshape(ROWS, 1))
 
-    mine, tags, docs, beside = lax.optimization_barrier((mine, tags, docs, beside))
+    mine, tags, docs[:2], beside = lax.optimization_barrier((mine, tags, docs[:2], beside))
     pair = joined(2, unit, beside)
     opposite = turn(pair, lambda place: 3 - place, False)
     other = swap(mine)

time: 115 us -> 112 us (0.974)
  waiting for transfers between devices: 20 us -> 16.9 us
    all_to_all x1, starting transfers between devices: 12.6 us -> 14.6 us  [body(): arrived = lax.all_to_all(near(outgoing), dp, 0, 0, tiled=True)]
    all_to_all x1, waiting for transfers between devices: 3.1 us -> 1.46 us  [body(): partial = lax.all_to_all(near(partial), 'x', 0, 0, tiled=True)]
    ppermute x4, waiting for transfers between devices: 1.51 us -> 0.01 us  [shift(): return lax.ppermute(value, axis, [(i, (i + step) % 4) for i in range(4)])]
  transfers between devices with their start and end apart: 14 -> 14, of which waited for: 5 -> 4; matrix products, arithmetic and copies ran while one was open for 2% -> 2% of each run, Pallas kernels for 6% -> 6%
where the time goes in v6:
time: 112 us; the launch traced here: 111 us
  starting transfers between devices  64.4 us (58%)
  waiting for transfers between devices  16.9 us (15%)
  blocking collectives  15.5 us (14%)
  Pallas kernels  11.7 us (10%)
  local copies, waits for them, and re-layouts  2.52 us (2%)
    ppermute x6, starting transfers between devices, turn(): return lax.ppermute(value, ('core', 'y', 'x'), pairs)  21.2 us
    all_to_all x1, blocking collectives, body(): answers = lax.all_to_all(best, dp, 0, 0, tiled=True)  15.5 us
    all_to_all x1, starting transfers between devices, body(): arrived = lax.all_to_all(near(outgoing), dp, 0, 0, tiled=True)  14.6 us
    ppermute x4, starting transfers between devices, shift(): return lax.ppermute(value, axis, [(i, (i + step) % 4) for i in range(4)])  13 us
    all_to_all x1, waiting for transfers between devices, body(): arrived = lax.all_to_all(near(outgoing), dp, 0, 0, tiled=True)  10.2 us
    ppermute x1, starting transfers between devices, swap(): return lax.ppermute(value, 'core', [(0, 1), (1, 0)])  7.02 us
    ppermute x6, waiting for transfers between devices, turn(): return lax.ppermute(value, ('core', 'y', 'x'), pairs)  5.24 us
    all_to_all x1, starting transfers between devices, body(): lax.all_to_all(near(halved(w_hidden, w_embed)), 'y', 0, 0, tiled=True)  5.16 us
  transfers between devices with their start and end apart: 14, of which 4 were waited for; matrix products, arithmetic and copies ran while one was open for 2% of the time, Pallas kernels for 6%

profile of v6, /device:TPU:1, one launch (start us, length us, event | category | flops | bytes accessed | tf_op | source)
XLA Modules:
  0.0 111.3 jit_solution(10861592894721864901)
XLA Ops:
  0.0 0.0 copy-start
  0.0 2.3 %weights.1 = bf16[4,1408,128]{2,1,0:T(8,128)(2,1)} custom-call(bf16[2048,128]{1,0:T(8,128)(2,1)} %w_hidden.1, bf16[128,768]{1,0:T(8,128)(2,1)} %w_embed.1), custom_call_target="tpu_custom_call" | custom-call | tf_op jit(solution)/shard_map/weights/pallas_call | solution.py:236
  2.3 0.0 copy-start.3
  2.3 5.2 %all-to-all-start = ((bf16[4,1408,128]{2,1,0:T(8,128)(2,1)}), bf16[4,1408,128]{2,1,0:T(8,128)(2,1)S(1)}, u32[]{:S(2)}, u32[]{:S(2)}) async-start(bf16[4,1408,128]{2,1,0:T(8,128)(2,1)} %weights.1), calls=%async_computation | async-start | bytes 2883584 | tf_op jit(solution)/shard_map/all_to_all | solution.py:311
  7.5 0.0 copy-done.3
  7.5 3.1 %collective-permute-start = (bf16[80,2048]{1,0:T(8,128)(2,1)S(1)}, bf16[80,2048]{1,0:T(8,128)(2,1)S(1)}, u32[]{:S(2)}, u32[]{:S(2)}) collective-permute-start(bf16[80,2048]{1,0:T(8,128)(2,1)S(1)} %copy-done.3), channel_id=1, source_target_pairs={{0,1},{1,2},{2,3},{3,0},{4,5},{5,6},{6,7},{7,4},{8,9},{9,10},{10,1... | collective-permute-start | bytes 983048 | tf_op jit(solution)/shard_map/ppermute | solution.py:210
  10.6 3.4 %collective-permute-start.1 = (bf16[80,2048]{1,0:T(8,128)(2,1)S(1)}, bf16[80,2048]{1,0:T(8,128)(2,1)S(1)}, u32[]{:S(2)}, u32[]{:S(2)}) collective-permute-start(bf16[80,2048]{1,0:T(8,128)(2,1)S(1)} %copy-done.3), channel_id=1, source_target_pairs={{0,3},{1,0},{2,1},{3,2},{4,7},{5,4},{6,5},{7,6},{8,11},{9,8},{10,9... | collective-permute-start | bytes 983048 | tf_op jit(solution)/shard_map/ppermute | solution.py:210
  14.0 1.1 unit.1.low
  15.1 3.4 %collective-permute-start.2 = (bf16[144,768]{1,0:T(8,128)(2,1)S(1)}, bf16[144,768]{1,0:T(8,128)(2,1)S(1)}, u32[]{:S(2)}, u32[]{:S(2)}) collective-permute-start(bf16[144,768]{1,0:T(8,128)(2,1)S(1)} %unit.1.low), channel_id=1, source_target_pairs={{0,1},{1,0},{2,3},{3,2},{4,5},{5,4},{6,7},{7,6},{8,9},{9,8},{10,11... | collective-permute-start | bytes 663560 | tf_op jit(solution)/shard_map/ppermute | solution.py:220
  18.5 0.8 constant_dynamic-slice_fusion
  19.2 0.0 collective-permute-done.left
  19.3 1.9 %collective-permute-start.3 = (bf16[48,2048]{1,0:T(8,128)(2,1)S(1)}, bf16[48,2048]{1,0:T(8,128)(2,1)}, u32[]{:S(2)}, u32[]{:S(2)}) collective-permute-start(bf16[48,2048]{1,0:T(8,128)(2,1)S(1)} %slice.16), channel_id=1, source_target_pairs={{0,1},{1,2},{2,3},{3,0},{4,5},{5,6},{6,7},{7,4},{8,9},{9,10},{10,1... | collective-permute-start | bytes 589832 | tf_op jit(solution)/shard_map/ppermute | solution.py:210
  21.2 0.0 collective-permute-done.1.right
  21.2 0.0 copy-start.2
  21.2 4.6 %collective-permute-start.4 = (bf16[32,2048]{1,0:T(8,128)(2,1)S(1)}, bf16[32,2048]{1,0:T(8,128)(2,1)S(1)}, u32[]{:S(2)}, u32[]{:S(2)}) collective-permute-start(bf16[32,2048]{1,0:T(8,128)(2,1)S(1)} %slice.17), channel_id=1, source_target_pairs={{0,3},{1,0},{2,1},{3,2},{4,7},{5,4},{6,5},{7,6},{8,11},{9,8},{10,9... | collective-permute-start | bytes 393224 | tf_op jit(solution)/shard_map/ppermute | solution.py:210
  25.8 0.1 dynamic-slice_bitcast_fusion
  25.9 0.1 copy.16.owner_col
  26.0 0.1 copy.14.local_col
  26.1 0.8 fusion.owner_row
  26.9 0.2 slots.1
  27.0 0.0 collective-permute-done.2.high
  27.1 0.0 all-to-all-done.mine
  27.1 7.0 %collective-permute-start.5 = (bf16[4,1408,128]{2,1,0:T(8,128)(2,1)S(1)}, bf16[4,1408,128]{2,1,0:T(8,128)(2,1)S(1)}, u32[]{:S(2)}, u32[]{:S(2)}) collective-permute-start(bf16[4,1408,128]{2,1,0:T(8,128)(2,1)S(1)} %all-to-all-done.mine), channel_id=1, source_target_pairs={{0,16},{16,0},{1,17},{17,1},{2,18},{18,2},{3,19},{19,3},{4,20},{20... | collective-permute-start | bytes 4325384 | tf_op jit(solution)/shard_map/ppermute | solution.py:306
  34.1 4.8 %collective-permute-start.6 = (bf16[288,768]{1,0:T(8,128)(2,1)S(1)}, bf16[288,768]{1,0:T(8,128)(2,1)S(1)}, u32[]{:S(2)}, u32[]{:S(2)}) collective-permute-start(bf16[288,768]{1,0:T(8,128)(2,1)S(1)} %join.2.low), channel_id=1, source_target_pairs={{0,3},{1,2},{2,1},{3,0},{4,7},{5,6},{6,5},{7,4},{8,11},{9,10},{10,... | collective-permute-start | bytes 1327112 | tf_op jit(solution)/shard_map/ppermute | solution.py:220
  39.0 0.0 collective-permute-done.4.far_b
  39.0 0.0 collective-permute-done.3.far_a
  39.0 0.6 copy-done.4
  39.6 1.8 %first.1 = (f32[320,512]{1,0:T(8,128)S(1)}, bf16[320,1024]{1,0:T(8,128)(2,1)S(1)}) custom-call(bf16[80,2048]{1,0:T(8,128)(2,1)} %own.1, bf16[80,2048]{1,0:T(8,128)(2,1)} %copy-done.1, bf16[80,2048]{1,0:T(8,128)(2,1)} %copy-done.2, bf16[48,2048]{1,0:T(8,128)(2,1)} %collective-permute-done.3.far_a, bf16[32,2048]{1,0:T(8,128)(2,1)} %copy-done.4, ...), custom_call_target="tpu_custom_call" | custom-call | flops 32212254720 | bytes 4194304 | tf_op jit(solution)/shard_map/first/pallas_call | solution.py:269
  41.4 0.0 collective-permute-done.5.other
  41.5 1.8 %head.1 = bf16[4,80,768]{2,1,0:T(8,128)(2,1)} custom-call(f32[320,512]{1,0:T(8,128)S(1)} %get-tuple-element.18.pre, bf16[320,1024]{1,0:T(8,128)(2,1)S(1)} %get-tuple-element.19.rest, bf16[4,1408,128]{2,1,0:T(8,128)(2,1)S(1)} %all-to-all-done.mine, bf16[4,1408,128]{2,1,0:T(8,128)(2,1)S(1)} %collective-permute-done.5.other), custom_call_target="tpu_custom_call" | custom-call | tf_op jit(solution)/shard_map/head/pallas_call | solution.py:34
  43.3 3.5 %all-to-all-start.1 = ((bf16[4,80,768]{2,1,0:T(8,128)(2,1)}), bf16[4,80,768]{2,1,0:T(8,128)(2,1)S(1)}, u32[]{:S(2)}, u32[]{:S(2)}) async-start(bf16[4,80,768]{2,1,0:T(8,128)(2,1)} %head.1), calls=%async_computation.1 | async-start | bytes 983040 | tf_op jit(solution)/shard_map/all_to_all | solution.py:341
  46.8 0.0 collective-permute-done.6.high
  46.8 0.1 join.3.own
  46.8 3.3 %collective-permute-start.7 = (bf16[576,768]{1,0:T(8,128)(2,1)S(1)}, bf16[576,768]{1,0:T(8,128)(2,1)S(1)}, u32[]{:S(2)}, u32[]{:S(2)}) collective-permute-start(bf16[576,768]{1,0:T(8,128)(2,1)S(1)} %join.3.own), channel_id=1, source_target_pairs={{0,4},{1,5},{2,6},{3,7},{4,8},{5,9},{6,10},{7,11},{8,12},{9,13},{1... | collective-permute-start | bytes 2654216 | tf_op jit(solution)/shard_map/ppermute | solution.py:220
  50.2 3.2 %collective-permute-start.8 = (bf16[576,768]{1,0:T(8,128)(2,1)S(1)}, bf16[576,768]{1,0:T(8,128)(2,1)S(1)}, u32[]{:S(2)}, u32[]{:S(2)}) collective-permute-start(bf16[576,768]{1,0:T(8,128)(2,1)S(1)} %join.3.own), channel_id=1, source_target_pairs={{0,12},{1,13},{2,14},{3,15},{4,0},{5,1},{6,2},{7,3},{8,4},{9,5},{1... | collective-permute-start | bytes 2654216 | tf_op jit(solution)/shard_map/ppermute | solution.py:220
  53.4 1.5 %all-to-all-done.1.partial = bf16[4,80,768]{2,1,0:T(8,128)(2,1)S(1)} async-done(((bf16[4,80,768]{2,1,0:T(8,128)(2,1)}), bf16[4,80,768]{2,1,0:T(8,128)(2,1)S(1)}, u32[]{:S(2)}, u32[]{:S(2)}) %all-to-all-start.1) | async-done | bytes 491552 | tf_op jit(solution)/shard_map/all_to_all | solution.py:341
  54.8 1.3 %query.1 = bf16[32,16,256]{2,1,0:T(8,128)(2,1)} custom-call(bf16[4,80,768]{2,1,0:T(8,128)(2,1)S(1)} %all-to-all-done.1.partial, s32[1,80]{1,0:T(1,128)S(1)} %fusion.owner_row, s32[1,80]{1,0:T(1,128)S(1)} %get-tuple-element.20.rank_row, bf16[80,256]{1,0:T(8,128)(2,1)S(1)} %get-tuple-element.21.tags), custom_call_target="tpu_custom_call" | custom-call | tf_op jit(solution)/shard_map/query/pallas_call | solution.py:34
  56.1 14.6 %all-to-all-start.2 = ((bf16[32,16,256]{2,1,0:T(8,128)(2,1)}), bf16[32,16,256]{2,1,0:T(8,128)(2,1)S(1)}, u32[]{:S(2)}, u32[]{:S(2)}) async-start(bf16[32,16,256]{2,1,0:T(8,128)(2,1)} %query.1), calls=%async_computation.2 | async-start | bytes 524288 | tf_op jit(solution)/shard_map/all_to_all | solution.py:345
  70.7 0.0 collective-permute-done.7.left
  70.7 1.9 %collective-permute-start.9 = (bf16[288,768]{1,0:T(8,128)(2,1)S(1)}, bf16[288,768]{1,0:T(8,128)(2,1)S(1)}, u32[]{:S(2)}, u32[]{:S(2)}) collective-permute-start(bf16[288,768]{1,0:T(8,128)(2,1)S(1)} %slice.18), channel_id=1, source_target_pairs={{0,4},{1,5},{2,6},{3,7},{4,8},{5,9},{6,10},{7,11},{8,12},{9,13},{1... | collective-permute-start | bytes 1327112 | tf_op jit(solution)/shard_map/ppermute | solution.py:220
  72.7 0.0 collective-permute-done.8.right
  72.7 4.6 %collective-permute-start.10 = (bf16[288,768]{1,0:T(8,128)(2,1)S(1)}, bf16[288,768]{1,0:T(8,128)(2,1)}, u32[]{:S(2)}, u32[]{:S(2)}) collective-permute-start(bf16[288,768]{1,0:T(8,128)(2,1)S(1)} %slice.19), channel_id=1, source_target_pairs={{0,12},{1,13},{2,14},{3,15},{4,0},{5,1},{6,2},{7,3},{8,4},{9,5},{1... | collective-permute-start | bytes 1327112 | tf_op jit(solution)/shard_map/ppermute | solution.py:220
  77.3 4.0 %collective-permute-done.9.top = bf16[288,768]{1,0:T(8,128)(2,1)S(1)} collective-permute-done((bf16[288,768]{1,0:T(8,128)(2,1)S(1)}, bf16[288,768]{1,0:T(8,128)(2,1)S(1)}, u32[]{:S(2)}, u32[]{:S(2)}) %collective-permute-start.9) | collective-permute-done | bytes 442400 | tf_op jit(solution)/shard_map/ppermute | solution.py:220
  81.3 1.2 %collective-permute-done.10.bottom = bf16[288,768]{1,0:T(8,128)(2,1)} collective-permute-done((bf16[288,768]{1,0:T(8,128)(2,1)S(1)}, bf16[288,768]{1,0:T(8,128)(2,1)}, u32[]{:S(2)}, u32[]{:S(2)}) %collective-permute-start.10) | collective-permute-done | bytes 442400 | tf_op jit(solution)/shard_map/ppermute | solution.py:220
  82.5 10.2 %all-to-all-done.2.arrived = bf16[32,16,256]{2,1,0:T(8,128)(2,1)S(1)} async-done(((bf16[32,16,256]{2,1,0:T(8,128)(2,1)}), bf16[32,16,256]{2,1,0:T(8,128)(2,1)S(1)}, u32[]{:S(2)}, u32[]{:S(2)}) %all-to-all-start.2) | async-done | bytes 262176 | tf_op jit(solution)/shard_map/all_to_all | solution.py:345
  92.7 2.5 %score.1 = f32[32,128]{1,0:T(8,128)S(1)} custom-call(bf16[32,16,256]{2,1,0:T(8,128)(2,1)S(1)} %all-to-all-done.2.arrived, bf16[576,768]{1,0:T(8,128)(2,1)S(1)} %join.3.own, bf16[576,768]{1,0:T(8,128)(2,1)S(1)} %collective-permute-done.7.left, bf16[576,768]{1,0:T(8,128)(2,1)S(1)} %collective-permute-done.8.right, ...), custom_call_target="tpu_custom_call" | custom-call | tf_op jit(solution)/shard_map/score/pallas_call | solution.py:290
  95.2 15.5 %all_to_all.26 = f32[32,1,128]{2,1,0:T(1,128)S(1)} all-to-all(f32[32,1,128]{2,1,0:T(1,128)S(1)} %bitcast.10), channel_id=1, replica_groups=mesh['z'=16,'core'=2,'y'=4,'x'=4] {'z','core'}, dimensions={0} | all-to-all | bytes 32768 | tf_op jit(solution)/shard_map/all_to_all | solution.py:347
  110.7 0.6 answer.1
  (10 shorter events, 0.1 us)
Async XLA Ops:
  0.0 25.8 %copy-start = (s32[1280]{0:T(1024)S(1)}, s32[1280]{0:T(1024)}, u32[]{:S(2)}) copy-start(s32[1280]{0:T(1024)} %param.13) | copy-start | bytes 15364
  2.3 5.2 %copy-start.3 = (bf16[80,2048]{1,0:T(8,128)(2,1)S(1)}, bf16[80,2048]{1,0:T(8,128)(2,1)}, u32[]{:S(2)}) copy-start(bf16[80,2048]{1,0:T(8,128)(2,1)} %own.1) | copy-start | bytes 983044
  2.3 24.7 %all-to-all-start = ((bf16[4,1408,128]{2,1,0:T(8,128)(2,1)}), bf16[4,1408,128]{2,1,0:T(8,128)(2,1)S(1)}, u32[]{:S(2)}, u32[]{:S(2)}) async-start(bf16[4,1408,128]{2,1,0:T(8,128)(2,1)} %weights.1), calls=%async_computation | async-start | bytes 2883584 | tf_op jit(solution)/shard_map/all_to_all | solution.py:311
  7.5 11.8 %collective-permute-start = (bf16[80,2048]{1,0:T(8,128)(2,1)S(1)}, bf16[80,2048]{1,0:T(8,128)(2,1)S(1)}, u32[]{:S(2)}, u32[]{:S(2)}) collective-permute-start(bf16[80,2048]{1,0:T(8,128)(2,1)S(1)} %copy-done.3), channel_id=1, source_target_pairs={{0,1},{1,2},{2,3},{3,0},{4,5},{5,6},{6,7},{7,4},{8,9},{9,10},{10,1... | collective-permute-start | bytes 983048 | tf_op jit(solution)/shard_map/ppermute | solution.py:210
  10.6 10.6 %collective-permute-start.1 = (bf16[80,2048]{1,0:T(8,128)(2,1)S(1)}, bf16[80,2048]{1,0:T(8,128)(2,1)S(1)}, u32[]{:S(2)}, u32[]{:S(2)}) collective-permute-start(bf16[80,2048]{1,0:T(8,128)(2,1)S(1)} %copy-done.3), channel_id=1, source_target_pairs={{0,3},{1,0},{2,1},{3,2},{4,7},{5,4},{6,5},{7,6},{8,11},{9,8},{10,9... | collective-permute-start | bytes 983048 | tf_op jit(solution)/shard_map/ppermute | solution.py:210
  15.1 12.0 %collective-permute-start.2 = (bf16[144,768]{1,0:T(8,128)(2,1)S(1)}, bf16[144,768]{1,0:T(8,128)(2,1)S(1)}, u32[]{:S(2)}, u32[]{:S(2)}) collective-permute-start(bf16[144,768]{1,0:T(8,128)(2,1)S(1)} %unit.1.low), channel_id=1, source_target_pairs={{0,1},{1,0},{2,3},{3,2},{4,5},{5,4},{6,7},{7,6},{8,9},{9,8},{10,11... | collective-permute-start | bytes 663560 | tf_op jit(solution)/shard_map/ppermute | solution.py:220
  19.2 19.7 %copy-start.1 = (bf16[80,2048]{1,0:T(8,128)(2,1)}, bf16[80,2048]{1,0:T(8,128)(2,1)S(1)}, u32[]{:S(2)}) copy-start(bf16[80,2048]{1,0:T(8,128)(2,1)S(1)} %collective-permute-done.left) | copy-start | bytes 983044
  19.3 19.7 %collective-permute-start.3 = (bf16[48,2048]{1,0:T(8,128)(2,1)S(1)}, bf16[48,2048]{1,0:T(8,128)(2,1)}, u32[]{:S(2)}, u32[]{:S(2)}) collective-permute-start(bf16[48,2048]{1,0:T(8,128)(2,1)S(1)} %slice.16), channel_id=1, source_target_pairs={{0,1},{1,2},{2,3},{3,0},{4,5},{5,6},{6,7},{7,4},{8,9},{9,10},{10,1... | collective-permute-start | bytes 589832 | tf_op jit(solution)/shard_map/ppermute | solution.py:210
  21.2 4.9 %copy-start.2 = (bf16[80,2048]{1,0:T(8,128)(2,1)}, bf16[80,2048]{1,0:T(8,128)(2,1)S(1)}, u32[]{:S(2)}) copy-start(bf16[80,2048]{1,0:T(8,128)(2,1)S(1)} %collective-permute-done.1.right) | copy-start | bytes 983044
  21.2 17.7 %collective-permute-start.4 = (bf16[32,2048]{1,0:T(8,128)(2,1)S(1)}, bf16[32,2048]{1,0:T(8,128)(2,1)S(1)}, u32[]{:S(2)}, u32[]{:S(2)}) collective-permute-start(bf16[32,2048]{1,0:T(8,128)(2,1)S(1)} %slice.17), channel_id=1, source_target_pairs={{0,3},{1,0},{2,1},{3,2},{4,7},{5,4},{6,5},{7,6},{8,11},{9,8},{10,9... | collective-permute-start | bytes 393224 | tf_op jit(solution)/shard_map/ppermute | solution.py:210
  27.1 14.4 %collective-permute-start.5 = (bf16[4,1408,128]{2,1,0:T(8,128)(2,1)S(1)}, bf16[4,1408,128]{2,1,0:T(8,128)(2,1)S(1)}, u32[]{:S(2)}, u32[]{:S(2)}) collective-permute-start(bf16[4,1408,128]{2,1,0:T(8,128)(2,1)S(1)} %all-to-all-done.mine), channel_id=1, source_target_pairs={{0,16},{16,0},{1,17},{17,1},{2,18},{18,2},{3,19},{19,3},{4,20},{20... | collective-permute-start | bytes 4325384 | tf_op jit(solution)/shard_map/ppermute | solution.py:306
  34.1 12.6 %collective-permute-start.6 = (bf16[288,768]{1,0:T(8,128)(2,1)S(1)}, bf16[288,768]{1,0:T(8,128)(2,1)S(1)}, u32[]{:S(2)}, u32[]{:S(2)}) collective-permute-start(bf16[288,768]{1,0:T(8,128)(2,1)S(1)} %join.2.low), channel_id=1, source_target_pairs={{0,3},{1,2},{2,1},{3,0},{4,7},{5,6},{6,5},{7,4},{8,11},{9,10},{10,... | collective-permute-start | bytes 1327112 | tf_op jit(solution)/shard_map/ppermute | solution.py:220
  39.0 0.7 copy-start.4
  43.3 11.5 %all-to-all-start.1 = ((bf16[4,80,768]{2,1,0:T(8,128)(2,1)}), bf16[4,80,768]{2,1,0:T(8,128)(2,1)S(1)}, u32[]{:S(2)}, u32[]{:S(2)}) async-start(bf16[4,80,768]{2,1,0:T(8,128)(2,1)} %head.1), calls=%async_computation.1 | async-start | bytes 983040 | tf_op jit(solution)/shard_map/all_to_all | solution.py:341
  46.8 23.9 %collective-permute-start.7 = (bf16[576,768]{1,0:T(8,128)(2,1)S(1)}, bf16[576,768]{1,0:T(8,128)(2,1)S(1)}, u32[]{:S(2)}, u32[]{:S(2)}) collective-permute-start(bf16[576,768]{1,0:T(8,128)(2,1)S(1)} %join.3.own), channel_id=1, source_target_pairs={{0,4},{1,5},{2,6},{3,7},{4,8},{5,9},{6,10},{7,11},{8,12},{9,13},{1... | collective-permute-start | bytes 2654216 | tf_op jit(solution)/shard_map/ppermute | solution.py:220
  50.2 22.5 %collective-permute-start.8 = (bf16[576,768]{1,0:T(8,128)(2,1)S(1)}, bf16[576,768]{1,0:T(8,128)(2,1)S(1)}, u32[]{:S(2)}, u32[]{:S(2)}) collective-permute-start(bf16[576,768]{1,0:T(8,128)(2,1)S(1)} %join.3.own), channel_id=1, source_target_pairs={{0,12},{1,13},{2,14},{3,15},{4,0},{5,1},{6,2},{7,3},{8,4},{9,5},{1... | collective-permute-start | bytes 2654216 | tf_op jit(solution)/shard_map/ppermute | solution.py:220
  56.1 36.6 %all-to-all-start.2 = ((bf16[32,16,256]{2,1,0:T(8,128)(2,1)}), bf16[32,16,256]{2,1,0:T(8,128)(2,1)S(1)}, u32[]{:S(2)}, u32[]{:S(2)}) async-start(bf16[32,16,256]{2,1,0:T(8,128)(2,1)} %query.1), calls=%async_computation.2 | async-start | bytes 524288 | tf_op jit(solution)/shard_map/all_to_all | solution.py:345
  70.7 10.6 %collective-permute-start.9 = (bf16[288,768]{1,0:T(8,128)(2,1)S(1)}, bf16[288,768]{1,0:T(8,128)(2,1)S(1)}, u32[]{:S(2)}, u32[]{:S(2)}) collective-permute-start(bf16[288,768]{1,0:T(8,128)(2,1)S(1)} %slice.18), channel_id=1, source_target_pairs={{0,4},{1,5},{2,6},{3,7},{4,8},{5,9},{6,10},{7,11},{8,12},{9,13},{1... | collective-permute-start | bytes 1327112 | tf_op jit(solution)/shard_map/ppermute | solution.py:220
  72.7 9.8 %collective-permute-start.10 = (bf16[288,768]{1,0:T(8,128)(2,1)S(1)}, bf16[288,768]{1,0:T(8,128)(2,1)}, u32[]{:S(2)}, u32[]{:S(2)}) collective-permute-start(bf16[288,768]{1,0:T(8,128)(2,1)S(1)} %slice.19), channel_id=1, source_target_pairs={{0,12},{1,13},{2,14},{3,15},{4,0},{5,1},{6,2},{7,3},{8,4},{9,5},{1... | collective-permute-start | bytes 1327112 | tf_op jit(solution)/shard_map/ppermute | solution.py:220

commit v7 on v6

--- a/solution.py
+++ b/solution.py
@@ -92,12 +92,15 @@
 def first_kernel(own, left, right, far_a, far_b, mine, pre, rest, docs, sem):
     c = lax.axis_index("core")
     copies, row = [], 0
-    for i, part in enumerate((own, left, right, far_a, far_b)):
+    for i, part in enumerate((own, left, right)):
         rows = part.shape[0]
         copies.append(pltpu.make_async_copy(part, docs.at[row : row + rows, :], sem.at[i]))
         row += rows
     for copy in copies:
         copy.start()
+    for part in (far_a, far_b):
+        docs[row : row + part.shape[0], :] = part[...]
+        row += part.shape[0]
     w = jnp.concatenate([mine[j, 0:HALF, :] for j in range(4)], axis=1)
     for copy in copies:
         copy.wait()
@@ -154,9 +157,13 @@
 
 
 def score_kernel(arrived, own, left, right, top, bottom, out, held, sem):
-    copy = pltpu.make_async_copy(bottom, held, sem.at[0])
-    copy.start()
-    parts = (own, left, right, top, held)
+    copies = [
+        pltpu.make_async_copy(top, held.at[0 : 2 * UNIT, :], sem.at[0]),
+        pltpu.make_async_copy(bottom, held.at[2 * UNIT :, :], sem.at[1]),
+    ]
+    for copy in copies:
+        copy.start()
+    parts = (own, left, right, held)
     row = iota((4 * OWNERS * CAP, 1), 0)
     kind, slot = row // (OWNERS * CAP), row % (OWNERS * CAP)
     line = jnp.where(kind < 3, kind * CAP + slot // OWNERS, LINES - 1)
@@ -175,8 +182,9 @@
     best = jnp.full((count, 2 * SLOTS), -1.0, F32)
     where = [(part, i * UNIT) for part in parts for i in range(part.shape[0] // UNIT)]
     for j in range(0, 16, 2):
-        if j == 14:
-            copy.wait()
+        if j == 12:
+            for copy in copies:
+                copy.wait()
         blocks, marks = [], []
         for part, row in where[j : j + 2]:
             blocks.append(part[row : row + SLOTS, :])
@@ -269,9 +277,9 @@
     return pl.pallas_call(
         first_kernel,
         out_shape=(pltpu.VMEM((4 * ROWS, 4 * BLOCK), F32), pltpu.VMEM((4 * ROWS, HALF), BF16)),
-        in_specs=[HBM] * 5 + [VMEM],
+        in_specs=[HBM] * 3 + [VMEM] * 3,
         out_specs=(VMEM, VMEM),
-        scratch_shapes=[pltpu.VMEM((4 * ROWS, HID), BF16), pltpu.SemaphoreType.DMA((5,))],
+        scratch_shapes=[pltpu.VMEM((4 * ROWS, HID), BF16), pltpu.SemaphoreType.DMA((3,))],
         name="first",
         cost_estimate=pl.CostEstimate(flops=30 << 30, bytes_accessed=4 << 20, transcendentals=0),
         compiler_params=PARAMS,
@@ -290,9 +298,9 @@
     return pl.pallas_call(
         score_kernel,
         out_shape=sds((OWNERS, SLOTS), F32),
-        in_specs=[VMEM] * 5 + [HBM],
+        in_specs=[VMEM] * 4 + [HBM] * 2,
         out_specs=VMEM,
-        scratch_shapes=[pltpu.VMEM((2 * UNIT, EMB), BF16), pltpu.SemaphoreType.DMA((1,))],
+        scratch_shapes=[pltpu.VMEM((4 * UNIT, EMB), BF16), pltpu.SemaphoreType.DMA((2,))],
         name="score",
         compiler_params=PARAMS,
     )(*arrays)
@@ -336,14 +344,14 @@
     left, right = turn(column, up, True), turn(column, down, True)
     top, bottom = turn(left[: 2 * UNIT], up, True), turn(right[2 * UNIT :], down, True)
     columns = [column, left, right, top, bottom]
-    pre, rest = first(*map(stay, (features, *docs)), mine)
+    pre, rest = first(*map(stay, (features, *docs[:2])), *map(near, docs[2:]), mine)
     partial = call(head_kernel, pltpu.VMEM((4, ROWS, EMB), BF16), "head")(near(pre), near(rest), mine, other)
     partial = lax.all_to_all(near(partial), "x", 0, 0, tiled=True)
     outgoing = call(query_kernel, pltpu.VMEM((OWNERS, LINES, CHUNK), BF16), "query")(
         partial, owner_row, rank_row, tags
     )
     arrived = lax.all_to_all(near(outgoing), dp, 0, 0, tiled=True)
-    best = score(arrived, *map(near, columns[:4]), stay(columns[4]))
+    best = score(arrived, *map(near, columns[:3]), *map(stay, columns[3:]))
     answers = lax.all_to_all(best, dp, 0, 0, tiled=True)
     result = call(answer_kernel, sds((1, ROWS), F32), "answer")(answers, owner_row, rank_row)
     return result.reshape(ROWS)

time: 112 us -> 111 us (level)
  no operation moved by 1% of the time
where the time goes in v7:
time: 111 us; the launch traced here: 110 us
  starting transfers between devices  64.4 us (58%)
  waiting for transfers between devices  16.1 us (15%)
  blocking collectives  15.5 us (14%)
  Pallas kernels  11.3 us (10%)
  local copies, waits for them, and re-layouts  2.67 us (2%)
    ppermute x6, starting transfers between devices, turn(): return lax.ppermute(value, ('core', 'y', 'x'), pairs)  21.2 us
    all_to_all x1, blocking collectives, body(): answers = lax.all_to_all(best, dp, 0, 0, tiled=True)  15.5 us
    all_to_all x1, starting transfers between devices, body(): arrived = lax.all_to_all(near(outgoing), dp, 0, 0, tiled=True)  14.6 us
    ppermute x4, starting transfers between devices, shift(): return lax.ppermute(value, axis, [(i, (i + step) % 4) for i in range(4)])  13 us
    all_to_all x1, waiting for transfers between devices, body(): arrived = lax.all_to_all(near(outgoing), dp, 0, 0, tiled=True)  10.2 us
    ppermute x1, starting transfers between devices, swap(): return lax.ppermute(value, 'core', [(0, 1), (1, 0)])  7.02 us
    all_to_all x1, starting transfers between devices, body(): lax.all_to_all(near(halved(w_hidden, w_embed)), 'y', 0, 0, tiled=True)  5.16 us
    ppermute x6, waiting for transfers between devices, turn(): return lax.ppermute(value, ('core', 'y', 'x'), pairs)  4.46 us
  transfers between devices with their start and end apart: 14, of which 4 were waited for; matrix products, arithmetic and copies ran while one was open for 2% of the time, Pallas kernels for 6%

profile of v7, /device:TPU:1, one launch (start us, length us, event | category | flops | bytes accessed | tf_op | source)
XLA Modules:
  0.0 110.2 jit_solution(14935207413682794313)
XLA Ops:
  0.0 0.0 copy-start
  0.0 2.3 %weights.1 = bf16[4,1408,128]{2,1,0:T(8,128)(2,1)} custom-call(bf16[2048,128]{1,0:T(8,128)(2,1)} %w_hidden.1, bf16[128,768]{1,0:T(8,128)(2,1)} %w_embed.1), custom_call_target="tpu_custom_call" | custom-call | tf_op jit(solution)/shard_map/weights/pallas_call | solution.py:244
  2.3 0.0 copy-start.4
  2.3 5.2 %all-to-all-start = ((bf16[4,1408,128]{2,1,0:T(8,128)(2,1)}), bf16[4,1408,128]{2,1,0:T(8,128)(2,1)S(1)}, u32[]{:S(2)}, u32[]{:S(2)}) async-start(bf16[4,1408,128]{2,1,0:T(8,128)(2,1)} %weights.1), calls=%async_computation | async-start | bytes 2883584 | tf_op jit(solution)/shard_map/all_to_all | solution.py:319
  7.5 3.1 %collective-permute-start = (bf16[80,2048]{1,0:T(8,128)(2,1)S(1)}, bf16[80,2048]{1,0:T(8,128)(2,1)S(1)}, u32[]{:S(2)}, u32[]{:S(2)}) collective-permute-start(bf16[80,2048]{1,0:T(8,128)(2,1)S(1)} %copy-done.4), channel_id=1, source_target_pairs={{0,1},{1,2},{2,3},{3,0},{4,5},{5,6},{6,7},{7,4},{8,9},{9,10},{10,1... | collective-permute-start | bytes 983048 | tf_op jit(solution)/shard_map/ppermute | solution.py:218
  10.6 3.4 %collective-permute-start.1 = (bf16[80,2048]{1,0:T(8,128)(2,1)S(1)}, bf16[80,2048]{1,0:T(8,128)(2,1)S(1)}, u32[]{:S(2)}, u32[]{:S(2)}) collective-permute-start(bf16[80,2048]{1,0:T(8,128)(2,1)S(1)} %copy-done.4), channel_id=1, source_target_pairs={{0,3},{1,0},{2,1},{3,2},{4,7},{5,4},{6,5},{7,6},{8,11},{9,8},{10,9... | collective-permute-start | bytes 983048 | tf_op jit(solution)/shard_map/ppermute | solution.py:218
  14.0 1.1 unit.1.low
  15.1 3.4 %collective-permute-start.2 = (bf16[144,768]{1,0:T(8,128)(2,1)S(1)}, bf16[144,768]{1,0:T(8,128)(2,1)S(1)}, u32[]{:S(2)}, u32[]{:S(2)}) collective-permute-start(bf16[144,768]{1,0:T(8,128)(2,1)S(1)} %unit.1.low), channel_id=1, source_target_pairs={{0,1},{1,0},{2,3},{3,2},{4,5},{5,4},{6,7},{7,6},{8,9},{9,8},{10,11... | collective-permute-start | bytes 663560 | tf_op jit(solution)/shard_map/ppermute | solution.py:228
  18.5 0.8 constant_dynamic-slice_fusion
  19.2 0.0 collective-permute-done.left
  19.3 1.9 %collective-permute-start.3 = (bf16[48,2048]{1,0:T(8,128)(2,1)S(1)}, bf16[48,2048]{1,0:T(8,128)(2,1)S(1)}, u32[]{:S(2)}, u32[]{:S(2)}) collective-permute-start(bf16[48,2048]{1,0:T(8,128)(2,1)S(1)} %slice.16), channel_id=1, source_target_pairs={{0,1},{1,2},{2,3},{3,0},{4,5},{5,6},{6,7},{7,4},{8,9},{9,10},{10,1... | collective-permute-start | bytes 589832 | tf_op jit(solution)/shard_map/ppermute | solution.py:218
  21.2 0.0 collective-permute-done.1.right
  21.2 4.6 %collective-permute-start.4 = (bf16[32,2048]{1,0:T(8,128)(2,1)S(1)}, bf16[32,2048]{1,0:T(8,128)(2,1)S(1)}, u32[]{:S(2)}, u32[]{:S(2)}) collective-permute-start(bf16[32,2048]{1,0:T(8,128)(2,1)S(1)} %slice.17), channel_id=1, source_target_pairs={{0,3},{1,0},{2,1},{3,2},{4,7},{5,4},{6,5},{7,6},{8,11},{9,8},{10,9... | collective-permute-start | bytes 393224 | tf_op jit(solution)/shard_map/ppermute | solution.py:218
  25.8 0.0 copy-done.3
  25.8 0.0 copy-done
  25.8 0.1 dynamic-slice_bitcast_fusion
  25.9 0.1 copy.16.owner_col
  26.0 0.1 copy.14.local_col
  26.1 0.8 fusion.owner_row
  26.9 0.2 slots.1
  27.0 0.0 collective-permute-done.2.high
  27.1 0.0 all-to-all-done.mine
  27.1 7.0 %collective-permute-start.5 = (bf16[4,1408,128]{2,1,0:T(8,128)(2,1)S(1)}, bf16[4,1408,128]{2,1,0:T(8,128)(2,1)S(1)}, u32[]{:S(2)}, u32[]{:S(2)}) collective-permute-start(bf16[4,1408,128]{2,1,0:T(8,128)(2,1)S(1)} %all-to-all-done.mine), channel_id=1, source_target_pairs={{0,16},{16,0},{1,17},{17,1},{2,18},{18,2},{3,19},{19,3},{4,20},{20... | collective-permute-start | bytes 4325384 | tf_op jit(solution)/shard_map/ppermute | solution.py:314
  34.1 4.8 %collective-permute-start.6 = (bf16[288,768]{1,0:T(8,128)(2,1)S(1)}, bf16[288,768]{1,0:T(8,128)(2,1)S(1)}, u32[]{:S(2)}, u32[]{:S(2)}) collective-permute-start(bf16[288,768]{1,0:T(8,128)(2,1)S(1)} %join.2.low), channel_id=1, source_target_pairs={{0,3},{1,2},{2,1},{3,0},{4,7},{5,6},{6,5},{7,4},{8,11},{9,10},{10,... | collective-permute-start | bytes 1327112 | tf_op jit(solution)/shard_map/ppermute | solution.py:228
  39.0 0.0 collective-permute-done.4.far_b
  39.0 0.0 collective-permute-done.3.far_a
  39.0 1.7 %first.1 = (f32[320,512]{1,0:T(8,128)S(1)}, bf16[320,1024]{1,0:T(8,128)(2,1)S(1)}) custom-call(bf16[80,2048]{1,0:T(8,128)(2,1)} %own.1, bf16[80,2048]{1,0:T(8,128)(2,1)} %copy-done.2, bf16[80,2048]{1,0:T(8,128)(2,1)} %copy-done.3, bf16[48,2048]{1,0:T(8,128)(2,1)S(1)} %collective-permute-done.3.far_a, bf16[32,2048]{1,0:T(8,128)(2,1)S(1)} %collective-permute-done.4.far_b, ...), custom_call_target="tpu_custom_call" | custom-call | flops 32212254720 | bytes 4194304 | tf_op jit(solution)/shard_map/first/pallas_call | solution.py:277
  40.7 0.0 collective-permute-done.5.other
  40.7 1.8 %head.1 = bf16[4,80,768]{2,1,0:T(8,128)(2,1)} custom-call(f32[320,512]{1,0:T(8,128)S(1)} %get-tuple-element.18.pre, bf16[320,1024]{1,0:T(8,128)(2,1)S(1)} %get-tuple-element.19.rest, bf16[4,1408,128]{2,1,0:T(8,128)(2,1)S(1)} %all-to-all-done.mine, bf16[4,1408,128]{2,1,0:T(8,128)(2,1)S(1)} %collective-permute-done.5.other), custom_call_target="tpu_custom_call" | custom-call | tf_op jit(solution)/shard_map/head/pallas_call | solution.py:34
  42.6 3.5 %all-to-all-start.1 = ((bf16[4,80,768]{2,1,0:T(8,128)(2,1)}), bf16[4,80,768]{2,1,0:T(8,128)(2,1)S(1)}, u32[]{:S(2)}, u32[]{:S(2)}) async-start(bf16[4,80,768]{2,1,0:T(8,128)(2,1)} %head.1), calls=%async_computation.1 | async-start | bytes 983040 | tf_op jit(solution)/shard_map/all_to_all | solution.py:349
  46.0 0.0 collective-permute-done.6.high
  46.0 0.1 join.3.own
  46.1 3.3 %collective-permute-start.7 = (bf16[576,768]{1,0:T(8,128)(2,1)S(1)}, bf16[576,768]{1,0:T(8,128)(2,1)S(1)}, u32[]{:S(2)}, u32[]{:S(2)}) collective-permute-start(bf16[576,768]{1,0:T(8,128)(2,1)S(1)} %join.3.own), channel_id=1, source_target_pairs={{0,4},{1,5},{2,6},{3,7},{4,8},{5,9},{6,10},{7,11},{8,12},{9,13},{1... | collective-permute-start | bytes 2654216 | tf_op jit(solution)/shard_map/ppermute | solution.py:228
  49.4 3.2 %collective-permute-start.8 = (bf16[576,768]{1,0:T(8,128)(2,1)S(1)}, bf16[576,768]{1,0:T(8,128)(2,1)S(1)}, u32[]{:S(2)}, u32[]{:S(2)}) collective-permute-start(bf16[576,768]{1,0:T(8,128)(2,1)S(1)} %join.3.own), channel_id=1, source_target_pairs={{0,12},{1,13},{2,14},{3,15},{4,0},{5,1},{6,2},{7,3},{8,4},{9,5},{1... | collective-permute-start | bytes 2654216 | tf_op jit(solution)/shard_map/ppermute | solution.py:228
  52.6 1.5 %all-to-all-done.1.partial = bf16[4,80,768]{2,1,0:T(8,128)(2,1)S(1)} async-done(((bf16[4,80,768]{2,1,0:T(8,128)(2,1)}), bf16[4,80,768]{2,1,0:T(8,128)(2,1)S(1)}, u32[]{:S(2)}, u32[]{:S(2)}) %all-to-all-start.1) | async-done | bytes 491552 | tf_op jit(solution)/shard_map/all_to_all | solution.py:349
  54.1 1.3 %query.1 = bf16[32,16,256]{2,1,0:T(8,128)(2,1)} custom-call(bf16[4,80,768]{2,1,0:T(8,128)(2,1)S(1)} %all-to-all-done.1.partial, s32[1,80]{1,0:T(1,128)S(1)} %fusion.owner_row, s32[1,80]{1,0:T(1,128)S(1)} %get-tuple-element.20.rank_row, bf16[80,256]{1,0:T(8,128)(2,1)S(1)} %get-tuple-element.21.tags), custom_call_target="tpu_custom_call" | custom-call | tf_op jit(solution)/shard_map/query/pallas_call | solution.py:34
  55.4 14.6 %all-to-all-start.2 = ((bf16[32,16,256]{2,1,0:T(8,128)(2,1)}), bf16[32,16,256]{2,1,0:T(8,128)(2,1)S(1)}, u32[]{:S(2)}, u32[]{:S(2)}) async-start(bf16[32,16,256]{2,1,0:T(8,128)(2,1)} %query.1), calls=%async_computation.2 | async-start | bytes 524288 | tf_op jit(solution)/shard_map/all_to_all | solution.py:353
  70.0 0.0 collective-permute-done.7.left
  70.0 1.9 %collective-permute-start.9 = (bf16[288,768]{1,0:T(8,128)(2,1)S(1)}, bf16[288,768]{1,0:T(8,128)(2,1)S(1)}, u32[]{:S(2)}, u32[]{:S(2)}) collective-permute-start(bf16[288,768]{1,0:T(8,128)(2,1)S(1)} %slice.18), channel_id=1, source_target_pairs={{0,4},{1,5},{2,6},{3,7},{4,8},{5,9},{6,10},{7,11},{8,12},{9,13},{1... | collective-permute-start | bytes 1327112 | tf_op jit(solution)/shard_map/ppermute | solution.py:228
  72.0 0.0 collective-permute-done.8.right
  72.0 4.6 %collective-permute-start.10 = (bf16[288,768]{1,0:T(8,128)(2,1)S(1)}, bf16[288,768]{1,0:T(8,128)(2,1)}, u32[]{:S(2)}, u32[]{:S(2)}) collective-permute-start(bf16[288,768]{1,0:T(8,128)(2,1)S(1)} %slice.19), channel_id=1, source_target_pairs={{0,12},{1,13},{2,14},{3,15},{4,0},{5,1},{6,2},{7,3},{8,4},{9,5},{1... | collective-permute-start | bytes 1327112 | tf_op jit(solution)/shard_map/ppermute | solution.py:228
  76.6 4.0 %collective-permute-done.9.top = bf16[288,768]{1,0:T(8,128)(2,1)S(1)} collective-permute-done((bf16[288,768]{1,0:T(8,128)(2,1)S(1)}, bf16[288,768]{1,0:T(8,128)(2,1)S(1)}, u32[]{:S(2)}, u32[]{:S(2)}) %collective-permute-start.9) | collective-permute-done | bytes 442400 | tf_op jit(solution)/shard_map/ppermute | solution.py:228
  80.6 0.8 copy-done.1
  81.4 0.5 collective-permute-done.10.bottom
  81.8 10.2 %all-to-all-done.2.arrived = bf16[32,16,256]{2,1,0:T(8,128)(2,1)S(1)} async-done(((bf16[32,16,256]{2,1,0:T(8,128)(2,1)}), bf16[32,16,256]{2,1,0:T(8,128)(2,1)S(1)}, u32[]{:S(2)}, u32[]{:S(2)}) %all-to-all-start.2) | async-done | bytes 262176 | tf_op jit(solution)/shard_map/all_to_all | solution.py:353
  92.0 2.1 %score.1 = f32[32,128]{1,0:T(8,128)S(1)} custom-call(bf16[32,16,256]{2,1,0:T(8,128)(2,1)S(1)} %all-to-all-done.2.arrived, bf16[576,768]{1,0:T(8,128)(2,1)S(1)} %join.3.own, bf16[576,768]{1,0:T(8,128)(2,1)S(1)} %collective-permute-done.7.left, bf16[576,768]{1,0:T(8,128)(2,1)S(1)} %collective-permute-done.8.right, bf16[288,768]{1,0:T(8,128)(2,1)} %copy-done.1, ...), custom_call_target="tpu_custom_call" | custom-call | tf_op jit(solution)/shard_map/score/pallas_call | solution.py:298
  94.1 15.5 %all_to_all.26 = f32[32,1,128]{2,1,0:T(1,128)S(1)} all-to-all(f32[32,1,128]{2,1,0:T(1,128)S(1)} %bitcast.10), channel_id=1, replica_groups=mesh['z'=16,'core'=2,'y'=4,'x'=4] {'z','core'}, dimensions={0} | all-to-all | bytes 32768 | tf_op jit(solution)/shard_map/all_to_all | solution.py:355
  109.6 0.6 answer.1
  (10 shorter events, 0.1 us)
Async XLA Ops:
  0.0 25.8 %copy-start = (s32[1280]{0:T(1024)S(1)}, s32[1280]{0:T(1024)}, u32[]{:S(2)}) copy-start(s32[1280]{0:T(1024)} %param.13) | copy-start | bytes 15364
  2.3 5.2 %copy-start.4 = (bf16[80,2048]{1,0:T(8,128)(2,1)S(1)}, bf16[80,2048]{1,0:T(8,128)(2,1)}, u32[]{:S(2)}) copy-start(bf16[80,2048]{1,0:T(8,128)(2,1)} %own.1) | copy-start | bytes 983044
  2.3 24.7 %all-to-all-start = ((bf16[4,1408,128]{2,1,0:T(8,128)(2,1)}), bf16[4,1408,128]{2,1,0:T(8,128)(2,1)S(1)}, u32[]{:S(2)}, u32[]{:S(2)}) async-start(bf16[4,1408,128]{2,1,0:T(8,128)(2,1)} %weights.1), calls=%async_computation | async-start | bytes 2883584 | tf_op jit(solution)/shard_map/all_to_all | solution.py:319
  7.5 11.8 %collective-permute-start = (bf16[80,2048]{1,0:T(8,128)(2,1)S(1)}, bf16[80,2048]{1,0:T(8,128)(2,1)S(1)}, u32[]{:S(2)}, u32[]{:S(2)}) collective-permute-start(bf16[80,2048]{1,0:T(8,128)(2,1)S(1)} %copy-done.4), channel_id=1, source_target_pairs={{0,1},{1,2},{2,3},{3,0},{4,5},{5,6},{6,7},{7,4},{8,9},{9,10},{10,1... | collective-permute-start | bytes 983048 | tf_op jit(solution)/shard_map/ppermute | solution.py:218
  10.6 10.6 %collective-permute-start.1 = (bf16[80,2048]{1,0:T(8,128)(2,1)S(1)}, bf16[80,2048]{1,0:T(8,128)(2,1)S(1)}, u32[]{:S(2)}, u32[]{:S(2)}) collective-permute-start(bf16[80,2048]{1,0:T(8,128)(2,1)S(1)} %copy-done.4), channel_id=1, source_target_pairs={{0,3},{1,0},{2,1},{3,2},{4,7},{5,4},{6,5},{7,6},{8,11},{9,8},{10,9... | collective-permute-start | bytes 983048 | tf_op jit(solution)/shard_map/ppermute | solution.py:218
  15.1 12.0 %collective-permute-start.2 = (bf16[144,768]{1,0:T(8,128)(2,1)S(1)}, bf16[144,768]{1,0:T(8,128)(2,1)S(1)}, u32[]{:S(2)}, u32[]{:S(2)}) collective-permute-start(bf16[144,768]{1,0:T(8,128)(2,1)S(1)} %unit.1.low), channel_id=1, source_target_pairs={{0,1},{1,0},{2,3},{3,2},{4,5},{5,4},{6,7},{7,6},{8,9},{9,8},{10,11... | collective-permute-start | bytes 663560 | tf_op jit(solution)/shard_map/ppermute | solution.py:228
  19.2 19.7 %copy-start.2 = (bf16[80,2048]{1,0:T(8,128)(2,1)}, bf16[80,2048]{1,0:T(8,128)(2,1)S(1)}, u32[]{:S(2)}) copy-start(bf16[80,2048]{1,0:T(8,128)(2,1)S(1)} %collective-permute-done.left) | copy-start | bytes 983044
  19.3 19.7 %collective-permute-start.3 = (bf16[48,2048]{1,0:T(8,128)(2,1)S(1)}, bf16[48,2048]{1,0:T(8,128)(2,1)S(1)}, u32[]{:S(2)}, u32[]{:S(2)}) collective-permute-start(bf16[48,2048]{1,0:T(8,128)(2,1)S(1)} %slice.16), channel_id=1, source_target_pairs={{0,1},{1,2},{2,3},{3,0},{4,5},{5,6},{6,7},{7,4},{8,9},{9,10},{10,1... | collective-permute-start | bytes 589832 | tf_op jit(solution)/shard_map/ppermute | solution.py:218
  21.2 4.6 %copy-start.3 = (bf16[80,2048]{1,0:T(8,128)(2,1)}, bf16[80,2048]{1,0:T(8,128)(2,1)S(1)}, u32[]{:S(2)}) copy-start(bf16[80,2048]{1,0:T(8,128)(2,1)S(1)} %collective-permute-done.1.right) | copy-start | bytes 983044
  21.2 17.7 %collective-permute-start.4 = (bf16[32,2048]{1,0:T(8,128)(2,1)S(1)}, bf16[32,2048]{1,0:T(8,128)(2,1)S(1)}, u32[]{:S(2)}, u32[]{:S(2)}) collective-permute-start(bf16[32,2048]{1,0:T(8,128)(2,1)S(1)} %slice.17), channel_id=1, source_target_pairs={{0,3},{1,0},{2,1},{3,2},{4,7},{5,4},{6,5},{7,6},{8,11},{9,8},{10,9... | collective-permute-start | bytes 393224 | tf_op jit(solution)/shard_map/ppermute | solution.py:218
  27.1 13.6 %collective-permute-start.5 = (bf16[4,1408,128]{2,1,0:T(8,128)(2,1)S(1)}, bf16[4,1408,128]{2,1,0:T(8,128)(2,1)S(1)}, u32[]{:S(2)}, u32[]{:S(2)}) collective-permute-start(bf16[4,1408,128]{2,1,0:T(8,128)(2,1)S(1)} %all-to-all-done.mine), channel_id=1, source_target_pairs={{0,16},{16,0},{1,17},{17,1},{2,18},{18,2},{3,19},{19,3},{4,20},{20... | collective-permute-start | bytes 4325384 | tf_op jit(solution)/shard_map/ppermute | solution.py:314
  34.1 11.9 %collective-permute-start.6 = (bf16[288,768]{1,0:T(8,128)(2,1)S(1)}, bf16[288,768]{1,0:T(8,128)(2,1)S(1)}, u32[]{:S(2)}, u32[]{:S(2)}) collective-permute-start(bf16[288,768]{1,0:T(8,128)(2,1)S(1)} %join.2.low), channel_id=1, source_target_pairs={{0,3},{1,2},{2,1},{3,0},{4,7},{5,6},{6,5},{7,4},{8,11},{9,10},{10,... | collective-permute-start | bytes 1327112 | tf_op jit(solution)/shard_map/ppermute | solution.py:228
  42.6 11.5 %all-to-all-start.1 = ((bf16[4,80,768]{2,1,0:T(8,128)(2,1)}), bf16[4,80,768]{2,1,0:T(8,128)(2,1)S(1)}, u32[]{:S(2)}, u32[]{:S(2)}) async-start(bf16[4,80,768]{2,1,0:T(8,128)(2,1)} %head.1), calls=%async_computation.1 | async-start | bytes 983040 | tf_op jit(solution)/shard_map/all_to_all | solution.py:349
  46.1 23.9 %collective-permute-start.7 = (bf16[576,768]{1,0:T(8,128)(2,1)S(1)}, bf16[576,768]{1,0:T(8,128)(2,1)S(1)}, u32[]{:S(2)}, u32[]{:S(2)}) collective-permute-start(bf16[576,768]{1,0:T(8,128)(2,1)S(1)} %join.3.own), channel_id=1, source_target_pairs={{0,4},{1,5},{2,6},{3,7},{4,8},{5,9},{6,10},{7,11},{8,12},{9,13},{1... | collective-permute-start | bytes 2654216 | tf_op jit(solution)/shard_map/ppermute | solution.py:228
  49.4 22.5 %collective-permute-start.8 = (bf16[576,768]{1,0:T(8,128)(2,1)S(1)}, bf16[576,768]{1,0:T(8,128)(2,1)S(1)}, u32[]{:S(2)}, u32[]{:S(2)}) collective-permute-start(bf16[576,768]{1,0:T(8,128)(2,1)S(1)} %join.3.own), channel_id=1, source_target_pairs={{0,12},{1,13},{2,14},{3,15},{4,0},{5,1},{6,2},{7,3},{8,4},{9,5},{1... | collective-permute-start | bytes 2654216 | tf_op jit(solution)/shard_map/ppermute | solution.py:228
  55.4 36.6 %all-to-all-start.2 = ((bf16[32,16,256]{2,1,0:T(8,128)(2,1)}), bf16[32,16,256]{2,1,0:T(8,128)(2,1)S(1)}, u32[]{:S(2)}, u32[]{:S(2)}) async-start(bf16[32,16,256]{2,1,0:T(8,128)(2,1)} %query.1), calls=%async_computation.2 | async-start | bytes 524288 | tf_op jit(solution)/shard_map/all_to_all | solution.py:353
  70.0 10.6 %collective-permute-start.9 = (bf16[288,768]{1,0:T(8,128)(2,1)S(1)}, bf16[288,768]{1,0:T(8,128)(2,1)S(1)}, u32[]{:S(2)}, u32[]{:S(2)}) collective-permute-start(bf16[288,768]{1,0:T(8,128)(2,1)S(1)} %slice.18), channel_id=1, source_target_pairs={{0,4},{1,5},{2,6},{3,7},{4,8},{5,9},{6,10},{7,11},{8,12},{9,13},{1... | collective-permute-start | bytes 1327112 | tf_op jit(solution)/shard_map/ppermute | solution.py:228
  72.0 9.8 %collective-permute-start.10 = (bf16[288,768]{1,0:T(8,128)(2,1)S(1)}, bf16[288,768]{1,0:T(8,128)(2,1)}, u32[]{:S(2)}, u32[]{:S(2)}) collective-permute-start(bf16[288,768]{1,0:T(8,128)(2,1)S(1)} %slice.19), channel_id=1, source_target_pairs={{0,12},{1,13},{2,14},{3,15},{4,0},{5,1},{6,2},{7,3},{8,4},{9,5},{1... | collective-permute-start | bytes 1327112 | tf_op jit(solution)/shard_map/ppermute | solution.py:228
  80.6 0.8 copy-start.1

commit v8 on v7

--- a/solution.py
+++ b/solution.py
@@ -127,11 +127,9 @@
 
 def query_kernel(partial, owner_row, rank_row, tags, out):
     line = iota((OWNERS * LINES, ROWS), 0)
-    inner = jnp.where(owner_row[...] == line // LINES, line % LINES, -1)
-    place = [
-        jnp.where(inner == (k * CAP + rank_row[...] if k < 3 else LINES - 1), 1.0, 0.0).astype(BF16)
-        for k in range(4)
-    ]
+    inner = line % LINES
+    mine = (inner == LINES - 1) | (inner % CAP == rank_row[...])
+    place = jnp.where(mine & (owner_row[...] == line // LINES), 1.0, 0.0).astype(BF16)
     proj = partial[0].astype(F32)
     for j in range(1, 4):
         proj = proj + partial[j].astype(F32)
@@ -142,11 +140,11 @@
     query = jnp.concatenate(
         [jnp.where(straight, low, high), jnp.where(straight, high, low)], axis=1
     ).astype(BF16)
-    total = jnp.dot(place[3], tags[...], preferred_element_type=F32)
+    total = jnp.dot(place, tags[...], preferred_element_type=F32)
+    rows = jnp.dot(place, query, preferred_element_type=F32)
+    chunk = iota((OWNERS * LINES, 1), 0) % LINES // CAP
     for k in range(3):
-        total = total + jnp.dot(
-            place[k], query[:, k * CHUNK : (k + 1) * CHUNK], preferred_element_type=F32
-        )
+        total = jnp.where(chunk == k, rows[:, k * CHUNK : (k + 1) * CHUNK], total)
     out[...] = total.astype(BF16).reshape(OWNERS, LINES, CHUNK)
 
 

time: 111 us -> 111 us (level)
  no operation moved by 1% of the time
where the time goes in v8:
time: 111 us; the launch traced here: 110 us
  starting transfers between devices  64.4 us (58%)
  waiting for transfers between devices  16.1 us (15%)
  blocking collectives  15.5 us (14%)
  Pallas kernels  11.3 us (10%)
  local copies, waits for them, and re-layouts  2.67 us (2%)
    ppermute x6, starting transfers between devices, turn(): return lax.ppermute(value, ('core', 'y', 'x'), pairs)  21.2 us
    all_to_all x1, blocking collectives, body(): answers = lax.all_to_all(best, dp, 0, 0, tiled=True)  15.5 us
    all_to_all x1, starting transfers between devices, body(): arrived = lax.all_to_all(near(outgoing), dp, 0, 0, tiled=True)  14.6 us
    ppermute x4, starting transfers between devices, shift(): return lax.ppermute(value, axis, [(i, (i + step) % 4) for i in range(4)])  13 us
    all_to_all x1, waiting for transfers between devices, body(): arrived = lax.all_to_all(near(outgoing), dp, 0, 0, tiled=True)  10.2 us
    ppermute x1, starting transfers between devices, swap(): return lax.ppermute(value, 'core', [(0, 1), (1, 0)])  7.02 us
    all_to_all x1, starting transfers between devices, body(): lax.all_to_all(near(halved(w_hidden, w_embed)), 'y', 0, 0, tiled=True)  5.16 us
    ppermute x6, waiting for transfers between devices, turn(): return lax.ppermute(value, ('core', 'y', 'x'), pairs)  4.46 us
  transfers between devices with their start and end apart: 14, of which 4 were waited for; matrix products, arithmetic and copies ran while one was open for 2% of the time, Pallas kernels for 6%

profile of v8, /device:TPU:1, one launch (start us, length us, event | category | flops | bytes accessed | tf_op | source)
XLA Modules:
  0.0 110.2 jit_solution(14909966598603973314)
XLA Ops:
  0.0 0.0 copy-start
  0.0 2.3 %weights.1 = bf16[4,1408,128]{2,1,0:T(8,128)(2,1)} custom-call(bf16[2048,128]{1,0:T(8,128)(2,1)} %w_hidden.1, bf16[128,768]{1,0:T(8,128)(2,1)} %w_embed.1), custom_call_target="tpu_custom_call" | custom-call | tf_op jit(solution)/shard_map/weights/pallas_call | solution.py:242
  2.3 0.0 copy-start.4
  2.3 5.2 %all-to-all-start = ((bf16[4,1408,128]{2,1,0:T(8,128)(2,1)}), bf16[4,1408,128]{2,1,0:T(8,128)(2,1)S(1)}, u32[]{:S(2)}, u32[]{:S(2)}) async-start(bf16[4,1408,128]{2,1,0:T(8,128)(2,1)} %weights.1), calls=%async_computation | async-start | bytes 2883584 | tf_op jit(solution)/shard_map/all_to_all | solution.py:317
  7.5 0.0 copy-done.4
  7.5 3.1 %collective-permute-start = (bf16[80,2048]{1,0:T(8,128)(2,1)S(1)}, bf16[80,2048]{1,0:T(8,128)(2,1)S(1)}, u32[]{:S(2)}, u32[]{:S(2)}) collective-permute-start(bf16[80,2048]{1,0:T(8,128)(2,1)S(1)} %copy-done.4), channel_id=1, source_target_pairs={{0,1},{1,2},{2,3},{3,0},{4,5},{5,6},{6,7},{7,4},{8,9},{9,10},{10,1... | collective-permute-start | bytes 983048 | tf_op jit(solution)/shard_map/ppermute | solution.py:216
  10.6 3.4 %collective-permute-start.1 = (bf16[80,2048]{1,0:T(8,128)(2,1)S(1)}, bf16[80,2048]{1,0:T(8,128)(2,1)S(1)}, u32[]{:S(2)}, u32[]{:S(2)}) collective-permute-start(bf16[80,2048]{1,0:T(8,128)(2,1)S(1)} %copy-done.4), channel_id=1, source_target_pairs={{0,3},{1,0},{2,1},{3,2},{4,7},{5,4},{6,5},{7,6},{8,11},{9,8},{10,9... | collective-permute-start | bytes 983048 | tf_op jit(solution)/shard_map/ppermute | solution.py:216
  14.0 1.1 unit.1.low
  15.1 3.4 %collective-permute-start.2 = (bf16[144,768]{1,0:T(8,128)(2,1)S(1)}, bf16[144,768]{1,0:T(8,128)(2,1)S(1)}, u32[]{:S(2)}, u32[]{:S(2)}) collective-permute-start(bf16[144,768]{1,0:T(8,128)(2,1)S(1)} %unit.1.low), channel_id=1, source_target_pairs={{0,1},{1,0},{2,3},{3,2},{4,5},{5,4},{6,7},{7,6},{8,9},{9,8},{10,11... | collective-permute-start | bytes 663560 | tf_op jit(solution)/shard_map/ppermute | solution.py:226
  18.5 0.8 constant_dynamic-slice_fusion
  19.2 0.0 collective-permute-done.left
  19.3 1.9 %collective-permute-start.3 = (bf16[48,2048]{1,0:T(8,128)(2,1)S(1)}, bf16[48,2048]{1,0:T(8,128)(2,1)S(1)}, u32[]{:S(2)}, u32[]{:S(2)}) collective-permute-start(bf16[48,2048]{1,0:T(8,128)(2,1)S(1)} %slice.16), channel_id=1, source_target_pairs={{0,1},{1,2},{2,3},{3,0},{4,5},{5,6},{6,7},{7,4},{8,9},{9,10},{10,1... | collective-permute-start | bytes 589832 | tf_op jit(solution)/shard_map/ppermute | solution.py:216
  21.2 0.0 collective-permute-done.1.right
  21.2 4.6 %collective-permute-start.4 = (bf16[32,2048]{1,0:T(8,128)(2,1)S(1)}, bf16[32,2048]{1,0:T(8,128)(2,1)S(1)}, u32[]{:S(2)}, u32[]{:S(2)}) collective-permute-start(bf16[32,2048]{1,0:T(8,128)(2,1)S(1)} %slice.17), channel_id=1, source_target_pairs={{0,3},{1,0},{2,1},{3,2},{4,7},{5,4},{6,5},{7,6},{8,11},{9,8},{10,9... | collective-permute-start | bytes 393224 | tf_op jit(solution)/shard_map/ppermute | solution.py:216
  25.8 0.1 dynamic-slice_bitcast_fusion
  25.9 0.1 copy.16.owner_col
  26.0 0.1 copy.14.local_col
  26.1 0.8 fusion.owner_row
  26.9 0.2 slots.1
  27.0 0.0 collective-permute-done.2.high
  27.1 0.0 all-to-all-done.mine
  27.1 7.0 %collective-permute-start.5 = (bf16[4,1408,128]{2,1,0:T(8,128)(2,1)S(1)}, bf16[4,1408,128]{2,1,0:T(8,128)(2,1)S(1)}, u32[]{:S(2)}, u32[]{:S(2)}) collective-permute-start(bf16[4,1408,128]{2,1,0:T(8,128)(2,1)S(1)} %all-to-all-done.mine), channel_id=1, source_target_pairs={{0,16},{16,0},{1,17},{17,1},{2,18},{18,2},{3,19},{19,3},{4,20},{20... | collective-permute-start | bytes 4325384 | tf_op jit(solution)/shard_map/ppermute | solution.py:312
  34.1 4.8 %collective-permute-start.6 = (bf16[288,768]{1,0:T(8,128)(2,1)S(1)}, bf16[288,768]{1,0:T(8,128)(2,1)S(1)}, u32[]{:S(2)}, u32[]{:S(2)}) collective-permute-start(bf16[288,768]{1,0:T(8,128)(2,1)S(1)} %join.2.low), channel_id=1, source_target_pairs={{0,3},{1,2},{2,1},{3,0},{4,7},{5,6},{6,5},{7,4},{8,11},{9,10},{10,... | collective-permute-start | bytes 1327112 | tf_op jit(solution)/shard_map/ppermute | solution.py:226
  39.0 0.0 collective-permute-done.4.far_b
  39.0 0.0 collective-permute-done.3.far_a
  39.0 0.0 copy-done.2
  39.0 1.7 %first.1 = (f32[320,512]{1,0:T(8,128)S(1)}, bf16[320,1024]{1,0:T(8,128)(2,1)S(1)}) custom-call(bf16[80,2048]{1,0:T(8,128)(2,1)} %own.1, bf16[80,2048]{1,0:T(8,128)(2,1)} %copy-done.2, bf16[80,2048]{1,0:T(8,128)(2,1)} %copy-done.3, bf16[48,2048]{1,0:T(8,128)(2,1)S(1)} %collective-permute-done.3.far_a, bf16[32,2048]{1,0:T(8,128)(2,1)S(1)} %collective-permute-done.4.far_b, ...), custom_call_target="tpu_custom_call" | custom-call | flops 32212254720 | bytes 4194304 | tf_op jit(solution)/shard_map/first/pallas_call | solution.py:275
  40.7 0.0 collective-permute-done.5.other
  40.7 1.8 %head.1 = bf16[4,80,768]{2,1,0:T(8,128)(2,1)} custom-call(f32[320,512]{1,0:T(8,128)S(1)} %get-tuple-element.18.pre, bf16[320,1024]{1,0:T(8,128)(2,1)S(1)} %get-tuple-element.19.rest, bf16[4,1408,128]{2,1,0:T(8,128)(2,1)S(1)} %all-to-all-done.mine, bf16[4,1408,128]{2,1,0:T(8,128)(2,1)S(1)} %collective-permute-done.5.other), custom_call_target="tpu_custom_call" | custom-call | tf_op jit(solution)/shard_map/head/pallas_call | solution.py:34
  42.6 3.5 %all-to-all-start.1 = ((bf16[4,80,768]{2,1,0:T(8,128)(2,1)}), bf16[4,80,768]{2,1,0:T(8,128)(2,1)S(1)}, u32[]{:S(2)}, u32[]{:S(2)}) async-start(bf16[4,80,768]{2,1,0:T(8,128)(2,1)} %head.1), calls=%async_computation.1 | async-start | bytes 983040 | tf_op jit(solution)/shard_map/all_to_all | solution.py:347
  46.0 0.0 collective-permute-done.6.high
  46.0 0.1 join.3.own
  46.1 3.3 %collective-permute-start.7 = (bf16[576,768]{1,0:T(8,128)(2,1)S(1)}, bf16[576,768]{1,0:T(8,128)(2,1)S(1)}, u32[]{:S(2)}, u32[]{:S(2)}) collective-permute-start(bf16[576,768]{1,0:T(8,128)(2,1)S(1)} %join.3.own), channel_id=1, source_target_pairs={{0,4},{1,5},{2,6},{3,7},{4,8},{5,9},{6,10},{7,11},{8,12},{9,13},{1... | collective-permute-start | bytes 2654216 | tf_op jit(solution)/shard_map/ppermute | solution.py:226
  49.4 3.2 %collective-permute-start.8 = (bf16[576,768]{1,0:T(8,128)(2,1)S(1)}, bf16[576,768]{1,0:T(8,128)(2,1)S(1)}, u32[]{:S(2)}, u32[]{:S(2)}) collective-permute-start(bf16[576,768]{1,0:T(8,128)(2,1)S(1)} %join.3.own), channel_id=1, source_target_pairs={{0,12},{1,13},{2,14},{3,15},{4,0},{5,1},{6,2},{7,3},{8,4},{9,5},{1... | collective-permute-start | bytes 2654216 | tf_op jit(solution)/shard_map/ppermute | solution.py:226
  52.6 1.5 %all-to-all-done.1.partial = bf16[4,80,768]{2,1,0:T(8,128)(2,1)S(1)} async-done(((bf16[4,80,768]{2,1,0:T(8,128)(2,1)}), bf16[4,80,768]{2,1,0:T(8,128)(2,1)S(1)}, u32[]{:S(2)}, u32[]{:S(2)}) %all-to-all-start.1) | async-done | bytes 491552 | tf_op jit(solution)/shard_map/all_to_all | solution.py:347
  54.1 1.3 %query.1 = bf16[32,16,256]{2,1,0:T(8,128)(2,1)} custom-call(bf16[4,80,768]{2,1,0:T(8,128)(2,1)S(1)} %all-to-all-done.1.partial, s32[1,80]{1,0:T(1,128)S(1)} %fusion.owner_row, s32[1,80]{1,0:T(1,128)S(1)} %get-tuple-element.20.rank_row, bf16[80,256]{1,0:T(8,128)(2,1)S(1)} %get-tuple-element.21.tags), custom_call_target="tpu_custom_call" | custom-call | tf_op jit(solution)/shard_map/query/pallas_call | solution.py:34
  55.4 14.6 %all-to-all-start.2 = ((bf16[32,16,256]{2,1,0:T(8,128)(2,1)}), bf16[32,16,256]{2,1,0:T(8,128)(2,1)S(1)}, u32[]{:S(2)}, u32[]{:S(2)}) async-start(bf16[32,16,256]{2,1,0:T(8,128)(2,1)} %query.1), calls=%async_computation.2 | async-start | bytes 524288 | tf_op jit(solution)/shard_map/all_to_all | solution.py:351
  70.0 0.0 collective-permute-done.7.left
  70.1 1.9 %collective-permute-start.9 = (bf16[288,768]{1,0:T(8,128)(2,1)S(1)}, bf16[288,768]{1,0:T(8,128)(2,1)S(1)}, u32[]{:S(2)}, u32[]{:S(2)}) collective-permute-start(bf16[288,768]{1,0:T(8,128)(2,1)S(1)} %slice.18), channel_id=1, source_target_pairs={{0,4},{1,5},{2,6},{3,7},{4,8},{5,9},{6,10},{7,11},{8,12},{9,13},{1... | collective-permute-start | bytes 1327112 | tf_op jit(solution)/shard_map/ppermute | solution.py:226
  72.0 0.0 collective-permute-done.8.right
  72.0 4.6 %collective-permute-start.10 = (bf16[288,768]{1,0:T(8,128)(2,1)S(1)}, bf16[288,768]{1,0:T(8,128)(2,1)}, u32[]{:S(2)}, u32[]{:S(2)}) collective-permute-start(bf16[288,768]{1,0:T(8,128)(2,1)S(1)} %slice.19), channel_id=1, source_target_pairs={{0,12},{1,13},{2,14},{3,15},{4,0},{5,1},{6,2},{7,3},{8,4},{9,5},{1... | collective-permute-start | bytes 1327112 | tf_op jit(solution)/shard_map/ppermute | solution.py:226
  76.6 4.0 %collective-permute-done.9.top = bf16[288,768]{1,0:T(8,128)(2,1)S(1)} collective-permute-done((bf16[288,768]{1,0:T(8,128)(2,1)S(1)}, bf16[288,768]{1,0:T(8,128)(2,1)S(1)}, u32[]{:S(2)}, u32[]{:S(2)}) %collective-permute-start.9) | collective-permute-done | bytes 442400 | tf_op jit(solution)/shard_map/ppermute | solution.py:226
  80.6 0.8 copy-done.1
  81.4 0.5 collective-permute-done.10.bottom
  81.8 10.2 %all-to-all-done.2.arrived = bf16[32,16,256]{2,1,0:T(8,128)(2,1)S(1)} async-done(((bf16[32,16,256]{2,1,0:T(8,128)(2,1)}), bf16[32,16,256]{2,1,0:T(8,128)(2,1)S(1)}, u32[]{:S(2)}, u32[]{:S(2)}) %all-to-all-start.2) | async-done | bytes 262176 | tf_op jit(solution)/shard_map/all_to_all | solution.py:351
  92.0 2.1 %score.1 = f32[32,128]{1,0:T(8,128)S(1)} custom-call(bf16[32,16,256]{2,1,0:T(8,128)(2,1)S(1)} %all-to-all-done.2.arrived, bf16[576,768]{1,0:T(8,128)(2,1)S(1)} %join.3.own, bf16[576,768]{1,0:T(8,128)(2,1)S(1)} %collective-permute-done.7.left, bf16[576,768]{1,0:T(8,128)(2,1)S(1)} %collective-permute-done.8.right, bf16[288,768]{1,0:T(8,128)(2,1)} %copy-done.1, ...), custom_call_target="tpu_custom_call" | custom-call | tf_op jit(solution)/shard_map/score/pallas_call | solution.py:296
  94.1 15.5 %all_to_all.26 = f32[32,1,128]{2,1,0:T(1,128)S(1)} all-to-all(f32[32,1,128]{2,1,0:T(1,128)S(1)} %bitcast.10), channel_id=1, replica_groups=mesh['z'=16,'core'=2,'y'=4,'x'=4] {'z','core'}, dimensions={0} | all-to-all | bytes 32768 | tf_op jit(solution)/shard_map/all_to_all | solution.py:353
  109.6 0.6 answer.1
  (10 shorter events, 0.1 us)
Async XLA Ops:
  0.0 25.8 %copy-start = (s32[1280]{0:T(1024)S(1)}, s32[1280]{0:T(1024)}, u32[]{:S(2)}) copy-start(s32[1280]{0:T(1024)} %param.13) | copy-start | bytes 15364
  2.3 5.2 %copy-start.4 = (bf16[80,2048]{1,0:T(8,128)(2,1)S(1)}, bf16[80,2048]{1,0:T(8,128)(2,1)}, u32[]{:S(2)}) copy-start(bf16[80,2048]{1,0:T(8,128)(2,1)} %own.1) | copy-start | bytes 983044
  2.3 24.7 %all-to-all-start = ((bf16[4,1408,128]{2,1,0:T(8,128)(2,1)}), bf16[4,1408,128]{2,1,0:T(8,128)(2,1)S(1)}, u32[]{:S(2)}, u32[]{:S(2)}) async-start(bf16[4,1408,128]{2,1,0:T(8,128)(2,1)} %weights.1), calls=%async_computation | async-start | bytes 2883584 | tf_op jit(solution)/shard_map/all_to_all | solution.py:317
  7.5 11.8 %collective-permute-start = (bf16[80,2048]{1,0:T(8,128)(2,1)S(1)}, bf16[80,2048]{1,0:T(8,128)(2,1)S(1)}, u32[]{:S(2)}, u32[]{:S(2)}) collective-permute-start(bf16[80,2048]{1,0:T(8,128)(2,1)S(1)} %copy-done.4), channel_id=1, source_target_pairs={{0,1},{1,2},{2,3},{3,0},{4,5},{5,6},{6,7},{7,4},{8,9},{9,10},{10,1... | collective-permute-start | bytes 983048 | tf_op jit(solution)/shard_map/ppermute | solution.py:216
  10.6 10.6 %collective-permute-start.1 = (bf16[80,2048]{1,0:T(8,128)(2,1)S(1)}, bf16[80,2048]{1,0:T(8,128)(2,1)S(1)}, u32[]{:S(2)}, u32[]{:S(2)}) collective-permute-start(bf16[80,2048]{1,0:T(8,128)(2,1)S(1)} %copy-done.4), channel_id=1, source_target_pairs={{0,3},{1,0},{2,1},{3,2},{4,7},{5,4},{6,5},{7,6},{8,11},{9,8},{10,9... | collective-permute-start | bytes 983048 | tf_op jit(solution)/shard_map/ppermute | solution.py:216
  15.1 12.0 %collective-permute-start.2 = (bf16[144,768]{1,0:T(8,128)(2,1)S(1)}, bf16[144,768]{1,0:T(8,128)(2,1)S(1)}, u32[]{:S(2)}, u32[]{:S(2)}) collective-permute-start(bf16[144,768]{1,0:T(8,128)(2,1)S(1)} %unit.1.low), channel_id=1, source_target_pairs={{0,1},{1,0},{2,3},{3,2},{4,5},{5,4},{6,7},{7,6},{8,9},{9,8},{10,11... | collective-permute-start | bytes 663560 | tf_op jit(solution)/shard_map/ppermute | solution.py:226
  19.2 19.7 %copy-start.2 = (bf16[80,2048]{1,0:T(8,128)(2,1)}, bf16[80,2048]{1,0:T(8,128)(2,1)S(1)}, u32[]{:S(2)}) copy-start(bf16[80,2048]{1,0:T(8,128)(2,1)S(1)} %collective-permute-done.left) | copy-start | bytes 983044
  19.3 19.7 %collective-permute-start.3 = (bf16[48,2048]{1,0:T(8,128)(2,1)S(1)}, bf16[48,2048]{1,0:T(8,128)(2,1)S(1)}, u32[]{:S(2)}, u32[]{:S(2)}) collective-permute-start(bf16[48,2048]{1,0:T(8,128)(2,1)S(1)} %slice.16), channel_id=1, source_target_pairs={{0,1},{1,2},{2,3},{3,0},{4,5},{5,6},{6,7},{7,4},{8,9},{9,10},{10,1... | collective-permute-start | bytes 589832 | tf_op jit(solution)/shard_map/ppermute | solution.py:216
  21.2 4.6 %copy-start.3 = (bf16[80,2048]{1,0:T(8,128)(2,1)}, bf16[80,2048]{1,0:T(8,128)(2,1)S(1)}, u32[]{:S(2)}) copy-start(bf16[80,2048]{1,0:T(8,128)(2,1)S(1)} %collective-permute-done.1.right) | copy-start | bytes 983044
  21.2 17.7 %collective-permute-start.4 = (bf16[32,2048]{1,0:T(8,128)(2,1)S(1)}, bf16[32,2048]{1,0:T(8,128)(2,1)S(1)}, u32[]{:S(2)}, u32[]{:S(2)}) collective-permute-start(bf16[32,2048]{1,0:T(8,128)(2,1)S(1)} %slice.17), channel_id=1, source_target_pairs={{0,3},{1,0},{2,1},{3,2},{4,7},{5,4},{6,5},{7,6},{8,11},{9,8},{10,9... | collective-permute-start | bytes 393224 | tf_op jit(solution)/shard_map/ppermute | solution.py:216
  27.1 13.6 %collective-permute-start.5 = (bf16[4,1408,128]{2,1,0:T(8,128)(2,1)S(1)}, bf16[4,1408,128]{2,1,0:T(8,128)(2,1)S(1)}, u32[]{:S(2)}, u32[]{:S(2)}) collective-permute-start(bf16[4,1408,128]{2,1,0:T(8,128)(2,1)S(1)} %all-to-all-done.mine), channel_id=1, source_target_pairs={{0,16},{16,0},{1,17},{17,1},{2,18},{18,2},{3,19},{19,3},{4,20},{20... | collective-permute-start | bytes 4325384 | tf_op jit(solution)/shard_map/ppermute | solution.py:312
  34.1 11.9 %collective-permute-start.6 = (bf16[288,768]{1,0:T(8,128)(2,1)S(1)}, bf16[288,768]{1,0:T(8,128)(2,1)S(1)}, u32[]{:S(2)}, u32[]{:S(2)}) collective-permute-start(bf16[288,768]{1,0:T(8,128)(2,1)S(1)} %join.2.low), channel_id=1, source_target_pairs={{0,3},{1,2},{2,1},{3,0},{4,7},{5,6},{6,5},{7,4},{8,11},{9,10},{10,... | collective-permute-start | bytes 1327112 | tf_op jit(solution)/shard_map/ppermute | solution.py:226
  42.6 11.5 %all-to-all-start.1 = ((bf16[4,80,768]{2,1,0:T(8,128)(2,1)}), bf16[4,80,768]{2,1,0:T(8,128)(2,1)S(1)}, u32[]{:S(2)}, u32[]{:S(2)}) async-start(bf16[4,80,768]{2,1,0:T(8,128)(2,1)} %head.1), calls=%async_computation.1 | async-start | bytes 983040 | tf_op jit(solution)/shard_map/all_to_all | solution.py:347
  46.1 23.9 %collective-permute-start.7 = (bf16[576,768]{1,0:T(8,128)(2,1)S(1)}, bf16[576,768]{1,0:T(8,128)(2,1)S(1)}, u32[]{:S(2)}, u32[]{:S(2)}) collective-permute-start(bf16[576,768]{1,0:T(8,128)(2,1)S(1)} %join.3.own), channel_id=1, source_target_pairs={{0,4},{1,5},{2,6},{3,7},{4,8},{5,9},{6,10},{7,11},{8,12},{9,13},{1... | collective-permute-start | bytes 2654216 | tf_op jit(solution)/shard_map/ppermute | solution.py:226
  49.4 22.6 %collective-permute-start.8 = (bf16[576,768]{1,0:T(8,128)(2,1)S(1)}, bf16[576,768]{1,0:T(8,128)(2,1)S(1)}, u32[]{:S(2)}, u32[]{:S(2)}) collective-permute-start(bf16[576,768]{1,0:T(8,128)(2,1)S(1)} %join.3.own), channel_id=1, source_target_pairs={{0,12},{1,13},{2,14},{3,15},{4,0},{5,1},{6,2},{7,3},{8,4},{9,5},{1... | collective-permute-start | bytes 2654216 | tf_op jit(solution)/shard_map/ppermute | solution.py:226
  55.4 36.6 %all-to-all-start.2 = ((bf16[32,16,256]{2,1,0:T(8,128)(2,1)}), bf16[32,16,256]{2,1,0:T(8,128)(2,1)S(1)}, u32[]{:S(2)}, u32[]{:S(2)}) async-start(bf16[32,16,256]{2,1,0:T(8,128)(2,1)} %query.1), calls=%async_computation.2 | async-start | bytes 524288 | tf_op jit(solution)/shard_map/all_to_all | solution.py:351
  70.1 10.6 %collective-permute-start.9 = (bf16[288,768]{1,0:T(8,128)(2,1)S(1)}, bf16[288,768]{1,0:T(8,128)(2,1)S(1)}, u32[]{:S(2)}, u32[]{:S(2)}) collective-permute-start(bf16[288,768]{1,0:T(8,128)(2,1)S(1)} %slice.18), channel_id=1, source_target_pairs={{0,4},{1,5},{2,6},{3,7},{4,8},{5,9},{6,10},{7,11},{8,12},{9,13},{1... | collective-permute-start | bytes 1327112 | tf_op jit(solution)/shard_map/ppermute | solution.py:226
  72.0 9.8 %collective-permute-start.10 = (bf16[288,768]{1,0:T(8,128)(2,1)S(1)}, bf16[288,768]{1,0:T(8,128)(2,1)}, u32[]{:S(2)}, u32[]{:S(2)}) collective-permute-start(bf16[288,768]{1,0:T(8,128)(2,1)S(1)} %slice.19), channel_id=1, source_target_pairs={{0,12},{1,13},{2,14},{3,15},{4,0},{5,1},{6,2},{7,3},{8,4},{9,5},{1... | collective-permute-start | bytes 1327112 | tf_op jit(solution)/shard_map/ppermute | solution.py:226
  80.6 0.8 copy-start.1
